TPU v7x, 256 devices: a whole 4x4x8 slice. The times are simulated.
256 devices in a mesh: seq: 64 (over y, x_hi, z), head: 4 (over x_lo, core).
Axes of the slice: x: 4 (x_hi: 2, x_lo: 2; x = x_hi * 2 + x_lo), y: 4, z: 8, core: 2. Of those that a mesh axis runs over, the one named last changes fastest.
Arguments:
- encoder_queries: bfloat16 [98304, 2048], P('seq', 'head'), may hold values from -30 to 30
- encoder_keys: bfloat16 [98304, 2048], P('seq', 'head'), may hold values from -4 to 4
- encoder_values: bfloat16 [98304, 2048], P('seq', 'head'), may hold values from -24 to 24
- block_lists: int32 [768, 4], P('seq'), may hold values from 0 to 767, as said below
- block_counts: int32 [768], P('seq'), may hold values from 1 to 4
- decoder_queries: bfloat16 [32768, 2048], P('seq', 'head'), may hold values from -30 to 30
- span_owner: int32 [256], replicated, may hold values from 0 to 63, as said below
- cross_slots: int32 [256, 2], replicated, may hold values from 0 to 11, as said below
- out_weight: bfloat16 [2048, 4096], P('head'), may hold values from -4.1875 to 4.1875
- decoder_input: bfloat16 [32768, 4096], P('seq', 'head'), may hold values from -6 to 6
Outputs:
- encoder_out: bfloat16 [98304, 2048], P('seq', 'head')
- decoder_out: bfloat16 [32768, 4096], P('seq', 'head')
Inputs may be any that keep to these rules, and one draw needn't show every extreme that they name: `block_lists`: slot 0 of row b is b; the slots below block_counts[b] hold distinct blocks within 2 blocks of b; the other slots hold b. span_owner[d] differs from d // 4 by at most one. `cross_slots`: the 2 entries of a row are distinct.
All inputs are finite; a program needn't handle non-finite values.
Results may differ from a plain program's by a relative error of at most 0.015.
Values may be sent and summed in bfloat16 or wider, within the bound.
No kernel may reach another device: no remote copies, remote signals or barrier semaphores. Data moves between devices by JAX's collectives and lax.ppermute only.
A program may use at most 128 MiB of HBM per device.

v0:
```python
import functools

import jax
import jax.numpy as jnp
from jax import lax
from jax.experimental import pallas as pl
from jax.experimental.pallas import tpu as pltpu
from jax.sharding import Mesh
from jax.sharding import PartitionSpec as P


HD = 64
BLK = 128
REACH = 2
SLOTS = 4
QUAD = 4
QW = HD * QUAD
HEAD = ("head_0", "head_1")
EXP_SCALE = 0.125 * 1.4426950408889634


def attend(q, k_blocks, v_blocks):
    lane = lax.broadcasted_iota(jnp.int32, (BLK, QW), 1) // HD
    zero = jnp.zeros_like(q)
    rows = jnp.concatenate([jnp.where(lane == h, q, zero) for h in range(QUAD)], axis=0)
    k = jnp.concatenate(k_blocks, axis=0)
    v = jnp.concatenate(v_blocks, axis=0)
    s = lax.dot_general(rows, k, (((1,), (1,)), ((), ())), preferred_element_type=jnp.float32)
    m = jnp.max(s, axis=1, keepdims=True)
    p = jnp.exp2((s - m) * EXP_SCALE)
    l = jnp.sum(p, axis=1, keepdims=True)
    o = lax.dot_general(
        p.astype(jnp.bfloat16), v, (((1,), (0,)), ((), ())), preferred_element_type=jnp.float32
    )
    o = o * (1.0 / l)
    out = o[:BLK]
    for h in range(1, QUAD):
        out = jnp.where(lane == h, o[h * BLK : (h + 1) * BLK], out)
    return out.astype(jnp.bfloat16)


def attend_listed(q_ref, k_ref, v_ref, ids, o_ref):
    for c in range(q_ref.shape[-1] // QW):
        cols = pl.ds(c * QW, QW)
        o_ref[:, cols] = attend(
            q_ref[:, cols], [k_ref[i, :, cols] for i in ids], [v_ref[i, :, cols] for i in ids]
        )


def branch_on_count(count, ids, q_ref, k_ref, v_ref, o_ref):
    for n in range(1, SLOTS + 1):

        @pl.when(count == n)
        def _(n=n):
            attend_listed(q_ref, k_ref, v_ref, ids[:n], o_ref)


def send_kernel(k, v, q, up, down, sem):
    halo = REACH * BLK
    tail = k.shape[0] - halo
    copies = [
        pltpu.make_async_copy(src, dst, sem)
        for src, dst in (
            (q, up.at[pl.ds(2 * halo, q.shape[0])]),
            (q, down.at[pl.ds(2 * halo, q.shape[0])]),
            (k.at[pl.ds(tail, halo)], up.at[pl.ds(0, halo)]),
            (k.at[pl.ds(0, halo)], down.at[pl.ds(0, halo)]),
            (v.at[pl.ds(tail, halo)], up.at[pl.ds(halo, halo)]),
            (v.at[pl.ds(0, halo)], down.at[pl.ds(halo, halo)]),
        )
    ]
    for copy in copies:
        copy.start()
    for copy in copies:
        copy.wait()


def send_call(k, v, q):
    rows = 2 * REACH * BLK + q.shape[0]
    shape = jax.ShapeDtypeStruct((rows, k.shape[1]), k.dtype)
    hbm = pl.BlockSpec(memory_space=pl.ANY)
    return pl.pallas_call(
        send_kernel,
        in_specs=[hbm] * 3,
        out_specs=[hbm] * 2,
        out_shape=[shape] * 2,
        scratch_shapes=[pltpu.SemaphoreType.DMA],
        name="pack_edges",
    )(k, v, q)


def cut_kernel(part, w, a, b, c, sem):
    columns = a.shape[1]
    copies = []
    for flip, dst in ((2, a), (3, b), (1, c)):
        start = pl.multiple_of((part[0] ^ flip) * columns, columns)
        half = w.shape[0] // 2
        for i in range(2):
            rows = pl.ds(i * half, half)
            copies.append(
                pltpu.make_async_copy(w.at[rows, pl.ds(start, columns)], dst.at[rows], sem)
            )
    for copy in copies:
        copy.start()
    for copy in copies:
        copy.wait()


def cut_call(part, w, columns):
    shape = jax.ShapeDtypeStruct((w.shape[0], columns), w.dtype)
    hbm = pl.BlockSpec(memory_space=pl.ANY)
    return pl.pallas_call(
        cut_kernel,
        in_specs=[pl.BlockSpec(memory_space=pltpu.SMEM), hbm],
        out_specs=[hbm] * 3,
        out_shape=[shape] * 3,
        scratch_shapes=[pltpu.SemaphoreType.DMA],
        name="cut_weight",
    )(part, w)


def inner_kernel(position, counts, lists, q_ref, k_ref, v_ref, o_ref):
    b = REACH + pl.program_id(0)
    base = position[0] * k_ref.shape[0]
    ids = [lists[j, b] - base for j in range(SLOTS)]
    branch_on_count(counts[b], ids, q_ref, k_ref, v_ref, o_ref)


def inner_call(position, counts, lists, q, k3, v3):
    blocks, _, width = k3.shape
    inner = blocks - 2 * REACH
    whole = pl.BlockSpec((blocks, BLK, width), lambda b, p, c, l: (0, 0, 0))
    rows = pl.BlockSpec((BLK, width), lambda b, p, c, l: (REACH + b, 0))
    return pl.pallas_call(
        inner_kernel,
        grid_spec=pltpu.PrefetchScalarGridSpec(
            num_scalar_prefetch=3, grid=(inner,), in_specs=[rows, whole, whole], out_specs=rows
        ),
        out_shape=jax.ShapeDtypeStruct((blocks * BLK, width), jnp.bfloat16),
        name="encoder_inner",
    )(position, counts, lists, q, k3, v3)


def stage_kernel(
    sources, take_needed, pos, counts, lists, owners, slots, q, k, v, up, down, dec, _, *refs
):
    e = refs[0]
    answers = refs[1 : 1 + len(sources)]
    kb, vb, eb, qe, qd, ob, sems = refs[1 + len(sources) :]
    blocks = k.shape[0]
    near = 2 * REACH
    mine = pos[0]
    per = answers[0].shape[0]
    total = owners.shape[0] // per
    hold = pl.ds(0, REACH)
    next_hold = pl.ds(REACH, REACH)
    first = [
        (up.at[hold], kb.at[pl.ds(0, REACH)]),
        (k, kb.at[pl.ds(REACH, blocks)]),
        (down.at[hold], kb.at[pl.ds(REACH + blocks, REACH)]),
        (up.at[next_hold], vb.at[pl.ds(0, REACH)]),
        (v.at[pl.ds(0, near)], vb.at[pl.ds(REACH, near)]),
        (v.at[pl.ds(blocks - near, near)], vb.at[pl.ds(REACH + blocks - near, near)]),
        (down.at[next_hold], vb.at[pl.ds(REACH + blocks, REACH)]),
        (q.at[pl.ds(0, REACH)], qe.at[pl.ds(0, REACH)]),
        (q.at[pl.ds(blocks - REACH, REACH)], qe.at[pl.ds(REACH, REACH)]),
    ]
    inner = pl.ds(REACH, blocks - near)
    second = [(e.at[inner], eb.at[inner])]
    if not take_needed:
        second = [(e, eb)]
    for i, shift in enumerate(sources):
        src = {-1: up.at[pl.ds(near, per)], 1: down.at[pl.ds(near, per)], 0: dec}[shift]
        second.append((src, qd.at[pl.ds(i * per, per)]))
    first = [pltpu.make_async_copy(a, b, sems.at[0]) for a, b in first]
    second = [pltpu.make_async_copy(a, b, sems.at[1]) for a, b in second]
    for copy in first + second:
        copy.start()

    def candidate(shift, t):
        source = mine + shift
        valid = (source >= 0) & (source < total)
        d = jnp.clip(source, 0, total - 1) * per + t
        return valid & (owners[d] == mine), slots[0, d], slots[1, d]

    needed = jnp.int32(0)
    for shift in (-1, 1):
        for t in range(per):
            live, s0, s1 = candidate(shift, t)
            bits = jnp.left_shift(jnp.int32(1), s0) | jnp.left_shift(jnp.int32(1), s1)
            needed = needed | jnp.where(live, bits, 0)

    def edge_of(t):
        return jnp.where(t < REACH, t, blocks - near + t)

    def due(t):
        return (jnp.right_shift(needed, edge_of(t)) & 1) == (1 if take_needed else 0)

    for copy in first:
        copy.wait()
    if not take_needed:
        for copy in second:
            copy.wait()

    @pl.loop(0, near)
    def _(t):
        @pl.when(due(t))
        def _():
            b = edge_of(t)
            base = mine * blocks - REACH
            ids = [lists[j, b] - base for j in range(SLOTS)]
            branch_on_count(counts[b], ids, qe.at[t], kb, vb, eb.at[b])
            pltpu.make_async_copy(eb.at[b], e.at[b], sems.at[2]).start()

    if take_needed:
        for copy in second:
            copy.wait()

    for i, shift in enumerate(sources):

        @pl.loop(0, per)
        def _(t, i=i, shift=shift):
            live, s0, s1 = candidate(shift, t)

            @pl.when(live)
            def _():
                for c in range(ob.shape[-1] // QW):
                    cols = pl.ds(c * QW, QW)
                    ob[i * per + t, :, cols] = attend(
                        qd[i * per + t, :, cols],
                        [kb[REACH + s, :, cols] for s in (s0, s1)],
                        [eb[s, :, cols] for s in (s0, s1)],
                    )

            @pl.when(jnp.logical_not(live))
            def _():
                ob[i * per + t] = jnp.zeros(ob.shape[1:], ob.dtype)

        pltpu.make_async_copy(ob.at[pl.ds(i * per, per)], answers[i], sems.at[3]).start()

    for i in range(len(sources)):
        pltpu.make_async_copy(ob.at[pl.ds(i * per, per)], answers[i], sems.at[3]).wait()

    @pl.loop(0, near)
    def _(t):
        @pl.when(due(t))
        def _():
            b = edge_of(t)
            pltpu.make_async_copy(eb.at[b], e.at[b], sems.at[2]).wait()


def stage_call(sources, take_needed, scalars, q, k3, v3, up, down, dec, e):
    blocks, _, width = k3.shape
    near = 2 * REACH
    per = dec.shape[0] // BLK
    smem = pl.BlockSpec(memory_space=pltpu.SMEM)
    hbm = pl.BlockSpec(memory_space=pl.ANY)
    answer = jax.ShapeDtypeStruct((per, BLK, width), jnp.bfloat16)

    def cut(x):
        return x.reshape(-1, BLK, width)

    def room(n):
        return pltpu.VMEM((n, BLK, width), jnp.bfloat16)

    served = per * len(sources)
    out = pl.pallas_call(
        functools.partial(stage_kernel, sources, take_needed),
        in_specs=[smem] * 5 + [hbm] * 7,
        out_specs=[hbm] * (1 + len(sources)),
        out_shape=[jax.ShapeDtypeStruct(k3.shape, jnp.bfloat16)] + [answer] * len(sources),
        scratch_shapes=[
            room(blocks + near),
            room(blocks + near),
            room(blocks),
            room(near),
            room(served),
            room(served),
            pltpu.SemaphoreType.DMA((4,)),
        ],
        input_output_aliases={11: 0},
        name="serve_remote" if take_needed else "serve_own",
    )(*scalars, cut(q), k3, v3, cut(up), cut(down), cut(dec), e)
    return out[0], [x.reshape(per * BLK, width) for x in out[1:]]


def project_kernel(part, c0, c1, c2, c3, w0, w1, w2, w3, r_ref, o_ref):
    total = r_ref[...].astype(jnp.float32)
    for c, w in ((c0, w0), (c1, w1), (c2, w2), (c3, w3)):
        total = total + jnp.dot(c[...], w[...], preferred_element_type=jnp.float32)
    o_ref[...] = total.astype(o_ref.dtype)


def project_call(part, contexts, own_weight, weights, residual):
    tokens, width = contexts[0].shape
    columns = residual.shape[1]
    tile = min(tokens, 256)
    c_spec = pl.BlockSpec((tile, width), lambda i, p: (i, 0))
    w_own = pl.BlockSpec((width, columns), lambda i, p: (0, p[0]))
    w_spec = pl.BlockSpec((width, columns), lambda i, p: (0, 0))
    r_spec = pl.BlockSpec((tile, columns), lambda i, p: (i, 0))
    return pl.pallas_call(
        project_kernel,
        grid_spec=pltpu.PrefetchScalarGridSpec(
            num_scalar_prefetch=1,
            grid=(tokens // tile,),
            in_specs=[c_spec] * 4 + [w_own, w_spec, w_spec, w_spec, r_spec],
            out_specs=r_spec,
        ),
        out_shape=jax.ShapeDtypeStruct(residual.shape, jnp.bfloat16),
        cost_estimate=pl.CostEstimate(
            flops=2 * tokens * width * 4 * columns, transcendentals=0, bytes_accessed=8_000_000
        ),
        name="project",
    )(part, *contexts, own_weight, *weights, residual)


def shifted(block, axis, distance):
    devices = range(lax.axis_size(axis))
    route = [(i - distance, i) for i in devices if i - distance in devices]
    return lax.ppermute(block, axis, route)


def swapped(block, flip):
    return lax.ppermute(block, HEAD, [(i, i ^ flip) for i in range(4)])


def body(
    encoder_queries,
    encoder_keys,
    encoder_values,
    block_lists,
    block_counts,
    decoder_queries,
    span_owner,
    cross_slots,
    out_weight,
    decoder_input,
):
    position = lax.axis_index("seq").astype(jnp.int32).reshape(1)
    part = lax.axis_index(HEAD).astype(jnp.int32).reshape(1)
    blocks = encoder_queries.shape[0] // BLK
    width = encoder_queries.shape[1]
    columns = decoder_input.shape[1]
    lists = block_lists.T
    slots = cross_slots.T
    up, down = send_call(encoder_keys, encoder_values, decoder_queries)
    up = shifted(up, "seq", 1)
    down = shifted(down, "seq", -1)
    across2, across3, across1 = cut_call(part, out_weight, columns)
    w2 = swapped(across2, 2)
    w3 = swapped(across3, 3)
    w1 = swapped(across1, 1)
    k3 = encoder_keys.reshape(blocks, BLK, width)
    v3 = encoder_values.reshape(blocks, BLK, width)
    partial = inner_call(position, block_counts, lists, encoder_queries, k3, v3)
    scalars = (position, block_counts, lists, span_owner, slots)
    shared = (encoder_queries, k3, v3, up, down, decoder_queries)
    e3, (for_prev, for_next) = stage_call(
        (-1, 1), True, scalars, *shared, partial.reshape(blocks, BLK, width)
    )
    from_next = shifted(for_prev, "seq", -1)
    from_prev = shifted(for_next, "seq", 1)
    e3, (own,) = stage_call((0,), False, scalars, *shared, e3)
    context = own + from_next + from_prev
    across = swapped(context, 2)
    beside = swapped(context, 1)
    corner = swapped(across, 1)
    decoder_out = project_call(
        part, [context, beside, across, corner], out_weight, [w1, w2, w3], decoder_input
    )
    return (e3.reshape(blocks * BLK, width), decoder_out)


def solution(mesh):
    split = Mesh(mesh.devices.reshape(mesh.shape["seq"], 2, 2), ("seq", "head_0", "head_1"))
    placed = (
        P("seq", HEAD),
        P("seq", HEAD),
        P("seq", HEAD),
        P("seq", None),
        P("seq"),
        P("seq", HEAD),
        P(),
        P(),
        P(HEAD, None),
        P("seq", HEAD),
    )
    return jax.shard_map(
        body,
        mesh=split,
        in_specs=placed,
        out_specs=(P("seq", HEAD), P("seq", HEAD)),
        check_vma=False,
    )
```

profile of v0, /device:TPU:24, one launch (start us, length us, event | category | flops | bytes accessed | tf_op | source)
XLA Modules:
  0.0 284.0 jit_solution(5481707268040179557)
XLA Ops:
  0.6 64.6 %pack_edges.1 = (bf16[1024,512]{1,0:T(8,128)(2,1)}, bf16[1024,512]{1,0:T(8,128)(2,1)}) custom-call(bf16[1536,512]{1,0:T(8,128)(2,1)} %k.1, bf16[1536,512]{1,0:T(8,128)(2,1)} %v.1, bf16[512,512]{1,0:T(8,128)(2,1)} %q.1), custom_call_target="tpu_custom_call" | custom-call | tf_op jit(solution)/shard_map/pack_edges/pallas_call | solution.py:82
  65.3 3.8 %collective-permute-start = (bf16[1024,512]{1,0:T(8,128)(2,1)}, bf16[1024,512]{1,0:T(8,128)(2,1)S(1)}, u32[]{:S(2)}, u32[]{:S(2)}) collective-permute-start(bf16[1024,512]{1,0:T(8,128)(2,1)} %get-tuple-element.12), channel_id=1, source_target_pairs={{0,4},{4,8},{8,12},{12,16},{16,20},{20,24},{24,28},{28,32},{32,36}... | collective-permute-start | bytes 3145736 | tf_op jit(solution)/shard_map/ppermute | solution.py:321
  69.1 8.5 %collective-permute-start.1 = (bf16[1024,512]{1,0:T(8,128)(2,1)}, bf16[1024,512]{1,0:T(8,128)(2,1)S(1)}, u32[]{:S(2)}, u32[]{:S(2)}) collective-permute-start(bf16[1024,512]{1,0:T(8,128)(2,1)} %get-tuple-element.13), channel_id=1, source_target_pairs={{4,0},{8,4},{12,8},{16,12},{20,16},{24,20},{28,24},{32,28},{36,32}... | collective-permute-start | bytes 3145736 | tf_op jit(solution)/shard_map/ppermute | solution.py:321
  77.6 11.9 %encoder_inner.1 = bf16[1536,512]{1,0:T(8,128)(2,1)} custom-call(s32[1]{0:T(128)} %bitcast.position.pos, s32[12]{0:T(128)} %counts.5, s32[4,12]{1,0:T(4,128)} %bitcast.34, bf16[1536,512]{1,0:T(8,128)(2,1)} %q_ref.1, bf16[12,128,512]{2,1,0:T(8,128)(2,1)} %bitcast.18, bf16[12,128,512]{2,1,0:T(8,128)(2,1)} %bitcast.21), custom_call_target="tpu_custom_call" | custom-call | tf_op jit(solution)/shard_map/encoder_inner/pallas_call | solution.py:134
  89.5 9.5 %collective-permute-done = bf16[1024,512]{1,0:T(8,128)(2,1)S(1)} collective-permute-done((bf16[1024,512]{1,0:T(8,128)(2,1)}, bf16[1024,512]{1,0:T(8,128)(2,1)S(1)}, u32[]{:S(2)}, u32[]{:S(2)}) %collective-permute-start) | collective-permute-done | bytes 1048608 | tf_op jit(solution)/shard_map/ppermute | solution.py:321
  99.0 1.3 collective-permute-done.1
  100.3 1.0 copy-done.1
  101.3 11.1 %serve_remote.1 = (bf16[12,128,512]{2,1,0:T(8,128)(2,1)}, bf16[4,128,512]{2,1,0:T(8,128)(2,1)}, bf16[4,128,512]{2,1,0:T(8,128)(2,1)}) custom-call(s32[1]{0:T(128)} %bitcast.position.pos, s32[12]{0:T(128)} %counts.5, s32[4,12]{1,0:T(4,128)} %bitcast.35, s32[256]{0:T(256)} %owners.3, s32[2,256]{1,0:T(2,128)} %bitcast.37, ...), custom_call_target="tpu_custom_call", output_to_operand_aliasing={{0}: (11, {})} | custom-call | tf_op jit(solution)/shard_map/serve_remote/pallas_call | solution.py:267
  112.4 5.4 %collective-permute-start.2 = (bf16[512,512]{1,0:T(8,128)(2,1)}, bf16[512,512]{1,0:T(8,128)(2,1)S(1)}, u32[]{:S(2)}, u32[]{:S(2)}) collective-permute-start(bf16[512,512]{1,0:T(8,128)(2,1)} %bitcast.40), channel_id=1, source_target_pairs={{4,0},{8,4},{12,8},{16,12},{20,16},{24,20},{28,24},{32,28},{36,32}... | collective-permute-start | bytes 1572872 | tf_op jit(solution)/shard_map/ppermute | solution.py:321
  117.8 1.9 collective-permute-start.3
  119.7 96.4 %cut_weight.1 = (bf16[512,1024]{1,0:T(8,128)(2,1)}, bf16[512,1024]{1,0:T(8,128)(2,1)}, bf16[512,1024]{1,0:T(8,128)(2,1)}) custom-call(s32[1]{0:T(128)} %bitcast.11.part, bf16[512,4096]{1,0:T(8,128)(2,1)} %w0.1), custom_call_target="tpu_custom_call" | custom-call | tf_op jit(solution)/shard_map/cut_weight/pallas_call | solution.py:112
  216.1 0.1 collective-permute-start.7
  216.2 0.7 collective-permute-start.8
  216.9 1.2 collective-permute-start.9
  218.1 7.0 %serve_own.1 = (bf16[12,128,512]{2,1,0:T(8,128)(2,1)}, bf16[4,128,512]{2,1,0:T(8,128)(2,1)}) custom-call(s32[1]{0:T(128)} %bitcast.position.pos, s32[12]{0:T(128)} %counts.5, s32[4,12]{1,0:T(4,128)} %bitcast.36, s32[256]{0:T(256)} %owners.3, s32[2,256]{1,0:T(2,128)} %bitcast.38, bf16[12,128,512]{2,1,0:T(8,128)(2,1)} %bitcast.25, ...), custom_call_target="tpu_custom_call", output_to_operand_aliasing={{0}: (11, {})} | custom-call | tf_op jit(solution)/shard_map/serve_own/pallas_call | solution.py:267
  225.1 0.0 copy-start.7
  225.2 0.8 copy-done.7
  225.9 1.3 fusion.c0
  227.2 0.7 collective-permute-start.5
  227.9 0.1 collective-permute-start.4
  228.0 47.7 %collective-permute-done.5.c2 = bf16[512,512]{1,0:T(8,128)(2,1)S(1)} collective-permute-done((bf16[512,512]{1,0:T(8,128)(2,1)S(1)}, bf16[512,512]{1,0:T(8,128)(2,1)S(1)}, u32[]{:S(2)}, u32[]{:S(2)}) %collective-permute-start.5) | collective-permute-done | bytes 524320 | tf_op jit(solution)/shard_map/ppermute | solution.py:325
  275.8 0.9 copy-done.6
  276.6 1.1 collective-permute-done.6.c3
  277.8 6.2 %project.1 = bf16[512,1024]{1,0:T(8,128)(2,1)} custom-call(s32[1]{0:T(128)} %bitcast.11.part, bf16[512,512]{1,0:T(8,128)(2,1)} %copy-done.2, bf16[512,512]{1,0:T(8,128)(2,1)} %copy-done.6, bf16[512,512]{1,0:T(8,128)(2,1)} %copy-done.5, bf16[512,512]{1,0:T(8,128)(2,1)} %collective-permute-done.6.c3, bf16[512,4096]{1,0:T(8,128)(2,1)} %w0.1, ...), custom_call_target="tpu_custom_call" | custom-call | flops 2147483648 | bytes 8000000 | tf_op jit(solution)/shard_map/project/pallas_call | solution.py:302
  (19 shorter events, 0.0 us)
Async XLA Ops:
  65.3 33.8 %collective-permute-start = (bf16[1024,512]{1,0:T(8,128)(2,1)}, bf16[1024,512]{1,0:T(8,128)(2,1)S(1)}, u32[]{:S(2)}, u32[]{:S(2)}) collective-permute-start(bf16[1024,512]{1,0:T(8,128)(2,1)} %get-tuple-element.12), channel_id=1, source_target_pairs={{0,4},{4,8},{8,12},{12,16},{16,20},{20,24},{24,28},{28,32},{32,36}... | collective-permute-start | bytes 3145736 | tf_op jit(solution)/shard_map/ppermute | solution.py:321
  69.1 31.2 %collective-permute-start.1 = (bf16[1024,512]{1,0:T(8,128)(2,1)}, bf16[1024,512]{1,0:T(8,128)(2,1)S(1)}, u32[]{:S(2)}, u32[]{:S(2)}) collective-permute-start(bf16[1024,512]{1,0:T(8,128)(2,1)} %get-tuple-element.13), channel_id=1, source_target_pairs={{4,0},{8,4},{12,8},{16,12},{20,16},{24,20},{28,24},{32,28},{36,32}... | collective-permute-start | bytes 3145736 | tf_op jit(solution)/shard_map/ppermute | solution.py:321
  99.0 1.3 copy-start
  100.3 1.0 copy-start.1
  112.4 112.7 %collective-permute-start.2 = (bf16[512,512]{1,0:T(8,128)(2,1)}, bf16[512,512]{1,0:T(8,128)(2,1)S(1)}, u32[]{:S(2)}, u32[]{:S(2)}) collective-permute-start(bf16[512,512]{1,0:T(8,128)(2,1)} %bitcast.40), channel_id=1, source_target_pairs={{4,0},{8,4},{12,8},{16,12},{20,16},{24,20},{28,24},{32,28},{36,32}... | collective-permute-start | bytes 1572872 | tf_op jit(solution)/shard_map/ppermute | solution.py:321
  117.8 107.4 %collective-permute-start.3 = (bf16[512,512]{1,0:T(8,128)(2,1)}, bf16[512,512]{1,0:T(8,128)(2,1)S(1)}, u32[]{:S(2)}, u32[]{:S(2)}) collective-permute-start(bf16[512,512]{1,0:T(8,128)(2,1)} %bitcast.39), channel_id=1, source_target_pairs={{0,4},{4,8},{8,12},{12,16},{16,20},{20,24},{24,28},{28,32},{32,36}... | collective-permute-start | bytes 1572872 | tf_op jit(solution)/shard_map/ppermute | solution.py:321
  216.1 59.6 %collective-permute-start.7 = (bf16[512,1024]{1,0:T(8,128)(2,1)}, bf16[512,1024]{1,0:T(8,128)(2,1)S(1)}, u32[]{:S(2)}, u32[]{:S(2)}) collective-permute-start(bf16[512,1024]{1,0:T(8,128)(2,1)} %get-tuple-element.19), channel_id=1, source_target_pairs={{0,1},{1,0},{2,3},{3,2},{4,5},{5,4},{6,7},{7,6},{8,9},{9,8},{10,11... | collective-permute-start | bytes 3145736 | tf_op jit(solution)/shard_map/ppermute | solution.py:325
  216.2 59.5 %collective-permute-start.8 = (bf16[512,1024]{1,0:T(8,128)(2,1)}, bf16[512,1024]{1,0:T(8,128)(2,1)S(1)}, u32[]{:S(2)}, u32[]{:S(2)}) collective-permute-start(bf16[512,1024]{1,0:T(8,128)(2,1)} %get-tuple-element.20), channel_id=1, source_target_pairs={{0,2},{1,3},{2,0},{3,1},{4,6},{5,7},{6,4},{7,5},{8,10},{9,11},{10,... | collective-permute-start | bytes 3145736 | tf_op jit(solution)/shard_map/ppermute | solution.py:325
  216.9 58.8 %collective-permute-start.9 = (bf16[512,1024]{1,0:T(8,128)(2,1)}, bf16[512,1024]{1,0:T(8,128)(2,1)}, u32[]{:S(2)}, u32[]{:S(2)}) collective-permute-start(bf16[512,1024]{1,0:T(8,128)(2,1)} %get-tuple-element.21), channel_id=1, source_target_pairs={{0,3},{1,2},{2,1},{3,0},{4,7},{5,6},{6,5},{7,4},{8,11},{9,10},{10,... | collective-permute-start | bytes 3145736 | tf_op jit(solution)/shard_map/ppermute | solution.py:325
  225.1 0.8 copy-start.7
  227.2 50.5 %copy-start.2 = (bf16[512,512]{1,0:T(8,128)(2,1)}, bf16[512,512]{1,0:T(8,128)(2,1)S(1)}, u32[]{:S(2)}) copy-start(bf16[512,512]{1,0:T(8,128)(2,1)S(1)} %fusion.c0) | copy-start | bytes 1572868
  227.2 48.5 %collective-permute-start.5 = (bf16[512,512]{1,0:T(8,128)(2,1)S(1)}, bf16[512,512]{1,0:T(8,128)(2,1)S(1)}, u32[]{:S(2)}, u32[]{:S(2)}) collective-permute-start(bf16[512,512]{1,0:T(8,128)(2,1)S(1)} %fusion.c0), channel_id=1, source_target_pairs={{0,2},{1,3},{2,0},{3,1},{4,6},{5,7},{6,4},{7,5},{8,10},{9,11},{10,... | collective-permute-start | bytes 1572872 | tf_op jit(solution)/shard_map/ppermute | solution.py:325
  227.9 47.8 %collective-permute-start.4 = (bf16[512,512]{1,0:T(8,128)(2,1)S(1)}, bf16[512,512]{1,0:T(8,128)(2,1)S(1)}, u32[]{:S(2)}, u32[]{:S(2)}) collective-permute-start(bf16[512,512]{1,0:T(8,128)(2,1)S(1)} %fusion.c0), channel_id=1, source_target_pairs={{0,1},{1,0},{2,3},{3,2},{4,5},{5,4},{6,7},{7,6},{8,9},{9,8},{10,11... | collective-permute-start | bytes 1572872 | tf_op jit(solution)/shard_map/ppermute | solution.py:325
  275.7 2.0 copy-start.5
  275.7 2.0 collective-permute-start.6
  275.7 2.0 copy-start.3
  275.7 2.0 copy-start.4
  275.8 0.9 copy-start.6
where the time goes:
time: 286 us; the launch traced here: 284 us
  Pallas kernels  197 us (69%)
  waiting for transfers between devices  59.6 us (21%)
  starting transfers between devices  22.4 us (8%)
    pallas_call x1, Pallas kernels, cut_call(): pl.pallas_call(cut_kernel, in_specs=[pl.BlockSpec(memory_space=pltpu.SMEM...  96.4 us
    pallas_call x1, Pallas kernels, send_call(): pl.pallas_call(send_kernel, in_specs=[hbm] * 3, out_specs=[hbm] * 2, out_...  64.6 us
    ppermute x6, waiting for transfers between devices, swapped(): return lax.ppermute(block, HEAD, [(i, i ^ flip) for i in range(4)])  48.8 us
    ppermute x4, starting transfers between devices, shifted(): return lax.ppermute(block, axis, route)  19.6 us
    pallas_call x2, Pallas kernels, stage_call(): pl.pallas_call(functools.partial(stage_kernel, sources, take_needed), in_...  18.1 us
    pallas_call x1, Pallas kernels, inner_call(): pl.pallas_call(inner_kernel, grid_spec=pltpu.PrefetchScalarGridSpec(num_s...  11.9 us
    ppermute x4, waiting for transfers between devices, shifted(): return lax.ppermute(block, axis, route)  10.8 us
    pallas_call x1, Pallas kernels, project_call(): pl.pallas_call(project_kernel, grid_spec=pltpu.PrefetchScalarGridSpec(num...  6.2 us
  transfers between devices with their start and end apart: 10, of which 4 were waited for; matrix products, arithmetic and copies ran while one was open for 0% of the time, Pallas kernels for 41%

commit v1 on v0

--- a/solution.py
+++ b/solution.py
@@ -55,55 +55,62 @@
             attend_listed(q_ref, k_ref, v_ref, ids[:n], o_ref)
 
 
-def send_kernel(k, v, q, up, down, sem):
+def move(plan, stages, load_sem, store_sem):
+    loads = [pltpu.make_async_copy(src, stages[i], load_sem.at[i]) for src, i, _ in plan]
+    stores = []
+    for load in loads:
+        load.start()
+    for load, (_, i, targets) in zip(loads, plan):
+        load.wait()
+        for dst in targets:
+            stores.append(pltpu.make_async_copy(stages[i], dst, store_sem))
+            stores[-1].start()
+    for store in stores:
+        store.wait()
+
+
+def send_kernel(k, v, q, up, down, s0, s1, s2, s3, s4, load_sem, store_sem):
     halo = REACH * BLK
-    tail = k.shape[0] - halo
-    copies = [
-        pltpu.make_async_copy(src, dst, sem)
-        for src, dst in (
-            (q, up.at[pl.ds(2 * halo, q.shape[0])]),
-            (q, down.at[pl.ds(2 * halo, q.shape[0])]),
-            (k.at[pl.ds(tail, halo)], up.at[pl.ds(0, halo)]),
-            (k.at[pl.ds(0, halo)], down.at[pl.ds(0, halo)]),
-            (v.at[pl.ds(tail, halo)], up.at[pl.ds(halo, halo)]),
-            (v.at[pl.ds(0, halo)], down.at[pl.ds(halo, halo)]),
-        )
-    ]
-    for copy in copies:
-        copy.start()
-    for copy in copies:
-        copy.wait()
+    tail = pl.ds(k.shape[0] - halo, halo)
+    head = pl.ds(0, halo)
+    rest = pl.ds(2 * halo, q.shape[0])
+    plan = (
+        (k.at[tail], 0, (up.at[head],)),
+        (v.at[tail], 1, (up.at[pl.ds(halo, halo)],)),
+        (k.at[head], 2, (down.at[head],)),
+        (v.at[head], 3, (down.at[pl.ds(halo, halo)],)),
+        (q, 4, (up.at[rest], down.at[rest])),
+    )
+    move(plan, (s0, s1, s2, s3, s4), load_sem, store_sem)
 
 
 def send_call(k, v, q):
-    rows = 2 * REACH * BLK + q.shape[0]
-    shape = jax.ShapeDtypeStruct((rows, k.shape[1]), k.dtype)
+    halo = REACH * BLK
+    width = k.shape[1]
+    shape = jax.ShapeDtypeStruct((2 * halo + q.shape[0], width), k.dtype)
     hbm = pl.BlockSpec(memory_space=pl.ANY)
     return pl.pallas_call(
         send_kernel,
         in_specs=[hbm] * 3,
         out_specs=[hbm] * 2,
         out_shape=[shape] * 2,
-        scratch_shapes=[pltpu.SemaphoreType.DMA],
+        scratch_shapes=[pltpu.VMEM((halo, width), k.dtype)] * 4
+        + [
+            pltpu.VMEM(q.shape, q.dtype),
+            pltpu.SemaphoreType.DMA((5,)),
+            pltpu.SemaphoreType.DMA,
+        ],
         name="pack_edges",
     )(k, v, q)
 
 
-def cut_kernel(part, w, a, b, c, sem):
+def cut_kernel(part, w, a, b, c, sa, sb, sc, load_sem, store_sem):
     columns = a.shape[1]
-    copies = []
-    for flip, dst in ((2, a), (3, b), (1, c)):
+    plan = []
+    for i, (flip, dst) in enumerate(((2, a), (3, b), (1, c))):
         start = pl.multiple_of((part[0] ^ flip) * columns, columns)
-        half = w.shape[0] // 2
-        for i in range(2):
-            rows = pl.ds(i * half, half)
-            copies.append(
-                pltpu.make_async_copy(w.at[rows, pl.ds(start, columns)], dst.at[rows], sem)
-            )
-    for copy in copies:
-        copy.start()
-    for copy in copies:
-        copy.wait()
+        plan.append((w.at[:, pl.ds(start, columns)], i, (dst,)))
+    move(plan, (sa, sb, sc), load_sem, store_sem)
 
 
 def cut_call(part, w, columns):
@@ -114,7 +121,8 @@
         in_specs=[pl.BlockSpec(memory_space=pltpu.SMEM), hbm],
         out_specs=[hbm] * 3,
         out_shape=[shape] * 3,
-        scratch_shapes=[pltpu.SemaphoreType.DMA],
+        scratch_shapes=[pltpu.VMEM(shape.shape, w.dtype)] * 3
+        + [pltpu.SemaphoreType.DMA((3,)), pltpu.SemaphoreType.DMA],
         name="cut_weight",
     )(part, w)
 

time: 286 us -> 140 us (0.49)
  the two profiles are of different devices: /device:TPU:24 before, /device:TPU:9 now
where the time goes in v1:
time: 140 us
  waiting for transfers between devices  65.8 us (47%)
  Pallas kernels  38.6 us (28%)
  starting transfers between devices  30.8 us (22%)
  local copies, waits for them, and re-layouts  2.64 us (2%)
    ppermute x6, waiting for transfers between devices, swapped(): return lax.ppermute(block, HEAD, [(i, i ^ flip) for i in range(4)])  52.4 us
    ppermute x4, starting transfers between devices, shifted(): return lax.ppermute(block, axis, route)  23.4 us
    pallas_call x2, Pallas kernels, stage_call(): pl.pallas_call(functools.partial(stage_kernel, sources, take_needed), in_...  16.4 us
    ppermute x4, waiting for transfers between devices, shifted(): return lax.ppermute(block, axis, route)  13.4 us
    pallas_call x1, Pallas kernels, inner_call(): pl.pallas_call(inner_kernel, grid_spec=pltpu.PrefetchScalarGridSpec(num_s...  10.7 us
    ppermute x6, starting transfers between devices, swapped(): return lax.ppermute(block, HEAD, [(i, i ^ flip) for i in range(4)])  7.45 us
    pallas_call x1, Pallas kernels, project_call(): pl.pallas_call(project_kernel, grid_spec=pltpu.PrefetchScalarGridSpec(num...  6.2 us
    pallas_call x1, Pallas kernels, cut_call(): pl.pallas_call(cut_kernel, in_specs=[pl.BlockSpec(memory_space=pltpu.SMEM...  2.91 us
  transfers between devices with their start and end apart: 10, of which 5 were waited for; matrix products, arithmetic and copies ran while one was open for 1% of the time, Pallas kernels for 15%

profile of v1, /device:TPU:9, one launch (start us, length us, event | category | flops | bytes accessed | tf_op | source)
XLA Modules:
  0.0 139.9 jit_solution(8557286309416723204)
XLA Ops:
  0.6 2.4 %pack_edges.1 = (bf16[1024,512]{1,0:T(8,128)(2,1)}, bf16[1024,512]{1,0:T(8,128)(2,1)}) custom-call(bf16[1536,512]{1,0:T(8,128)(2,1)} %k.1, bf16[1536,512]{1,0:T(8,128)(2,1)} %v.1, bf16[512,512]{1,0:T(8,128)(2,1)} %q.1), custom_call_target="tpu_custom_call" | custom-call | tf_op jit(solution)/shard_map/pack_edges/pallas_call | solution.py:92
  3.0 3.5 %collective-permute-start = (bf16[1024,512]{1,0:T(8,128)(2,1)}, bf16[1024,512]{1,0:T(8,128)(2,1)S(1)}, u32[]{:S(2)}, u32[]{:S(2)}) collective-permute-start(bf16[1024,512]{1,0:T(8,128)(2,1)} %get-tuple-element.12), channel_id=1, source_target_pairs={{0,4},{4,8},{8,12},{12,16},{16,20},{20,24},{24,28},{28,32},{32,36}... | collective-permute-start | bytes 3145736 | tf_op jit(solution)/shard_map/ppermute | solution.py:329
  6.6 8.2 %collective-permute-start.1 = (bf16[1024,512]{1,0:T(8,128)(2,1)}, bf16[1024,512]{1,0:T(8,128)(2,1)S(1)}, u32[]{:S(2)}, u32[]{:S(2)}) collective-permute-start(bf16[1024,512]{1,0:T(8,128)(2,1)} %get-tuple-element.13), channel_id=1, source_target_pairs={{4,0},{8,4},{12,8},{16,12},{20,16},{24,20},{28,24},{32,28},{36,32}... | collective-permute-start | bytes 3145736 | tf_op jit(solution)/shard_map/ppermute | solution.py:329
  14.8 10.7 %encoder_inner.1 = bf16[1536,512]{1,0:T(8,128)(2,1)} custom-call(s32[1]{0:T(128)} %bitcast.position.pos, s32[12]{0:T(128)} %counts.5, s32[4,12]{1,0:T(4,128)} %bitcast.34, bf16[1536,512]{1,0:T(8,128)(2,1)} %q_ref.1, bf16[12,128,512]{2,1,0:T(8,128)(2,1)} %bitcast.18, bf16[12,128,512]{2,1,0:T(8,128)(2,1)} %bitcast.21), custom_call_target="tpu_custom_call" | custom-call | tf_op jit(solution)/shard_map/encoder_inner/pallas_call | solution.py:142
  25.5 10.5 %collective-permute-done = bf16[1024,512]{1,0:T(8,128)(2,1)S(1)} collective-permute-done((bf16[1024,512]{1,0:T(8,128)(2,1)}, bf16[1024,512]{1,0:T(8,128)(2,1)S(1)}, u32[]{:S(2)}, u32[]{:S(2)}) %collective-permute-start) | collective-permute-done | bytes 1048608 | tf_op jit(solution)/shard_map/ppermute | solution.py:329
  35.9 1.0 collective-permute-done.1
  36.9 1.0 copy-done.1
  37.9 8.5 %serve_remote.1 = (bf16[12,128,512]{2,1,0:T(8,128)(2,1)}, bf16[4,128,512]{2,1,0:T(8,128)(2,1)}, bf16[4,128,512]{2,1,0:T(8,128)(2,1)}) custom-call(s32[1]{0:T(128)} %bitcast.position.pos, s32[12]{0:T(128)} %counts.5, s32[4,12]{1,0:T(4,128)} %bitcast.35, s32[256]{0:T(256)} %owners.3, s32[2,256]{1,0:T(2,128)} %bitcast.37, ...), custom_call_target="tpu_custom_call", output_to_operand_aliasing={{0}: (11, {})} | custom-call | tf_op jit(solution)/shard_map/serve_remote/pallas_call | solution.py:275
  46.4 9.7 %collective-permute-start.2 = (bf16[512,512]{1,0:T(8,128)(2,1)}, bf16[512,512]{1,0:T(8,128)(2,1)S(1)}, u32[]{:S(2)}, u32[]{:S(2)}) collective-permute-start(bf16[512,512]{1,0:T(8,128)(2,1)} %bitcast.40), channel_id=1, source_target_pairs={{4,0},{8,4},{12,8},{16,12},{20,16},{24,20},{28,24},{32,28},{36,32}... | collective-permute-start | bytes 1572872 | tf_op jit(solution)/shard_map/ppermute | solution.py:329
  56.1 1.9 %collective-permute-start.3 = (bf16[512,512]{1,0:T(8,128)(2,1)}, bf16[512,512]{1,0:T(8,128)(2,1)S(1)}, u32[]{:S(2)}, u32[]{:S(2)}) collective-permute-start(bf16[512,512]{1,0:T(8,128)(2,1)} %bitcast.39), channel_id=1, source_target_pairs={{0,4},{4,8},{8,12},{12,16},{16,20},{20,24},{24,28},{28,32},{32,36}... | collective-permute-start | bytes 1572872 | tf_op jit(solution)/shard_map/ppermute | solution.py:329
  58.0 2.9 %cut_weight.1 = (bf16[512,1024]{1,0:T(8,128)(2,1)}, bf16[512,1024]{1,0:T(8,128)(2,1)}, bf16[512,1024]{1,0:T(8,128)(2,1)}) custom-call(s32[1]{0:T(128)} %bitcast.11.part, bf16[512,4096]{1,0:T(8,128)(2,1)} %w0.1), custom_call_target="tpu_custom_call" | custom-call | tf_op jit(solution)/shard_map/cut_weight/pallas_call | solution.py:119
  60.9 1.9 %collective-permute-start.7 = (bf16[512,1024]{1,0:T(8,128)(2,1)}, bf16[512,1024]{1,0:T(8,128)(2,1)S(1)}, u32[]{:S(2)}, u32[]{:S(2)}) collective-permute-start(bf16[512,1024]{1,0:T(8,128)(2,1)} %get-tuple-element.19), channel_id=1, source_target_pairs={{0,1},{1,0},{2,3},{3,2},{4,5},{5,4},{6,7},{7,6},{8,9},{9,8},{10,11... | collective-permute-start | bytes 3145736 | tf_op jit(solution)/shard_map/ppermute | solution.py:333
  63.2 1.4 %collective-permute-start.9 = (bf16[512,1024]{1,0:T(8,128)(2,1)}, bf16[512,1024]{1,0:T(8,128)(2,1)}, u32[]{:S(2)}, u32[]{:S(2)}) collective-permute-start(bf16[512,1024]{1,0:T(8,128)(2,1)} %get-tuple-element.21), channel_id=1, source_target_pairs={{0,3},{1,2},{2,1},{3,0},{4,7},{5,6},{6,5},{7,4},{8,11},{9,10},{10,... | collective-permute-start | bytes 3145736 | tf_op jit(solution)/shard_map/ppermute | solution.py:333
  64.6 7.9 %serve_own.1 = (bf16[12,128,512]{2,1,0:T(8,128)(2,1)}, bf16[4,128,512]{2,1,0:T(8,128)(2,1)}) custom-call(s32[1]{0:T(128)} %bitcast.position.pos, s32[12]{0:T(128)} %counts.5, s32[4,12]{1,0:T(4,128)} %bitcast.36, s32[256]{0:T(256)} %owners.3, s32[2,256]{1,0:T(2,128)} %bitcast.38, bf16[12,128,512]{2,1,0:T(8,128)(2,1)} %bitcast.25, ...), custom_call_target="tpu_custom_call", output_to_operand_aliasing={{0}: (11, {})} | custom-call | tf_op jit(solution)/shard_map/serve_own/pallas_call | solution.py:275
  72.5 1.9 %collective-permute-done.3 = bf16[512,512]{1,0:T(8,128)(2,1)S(1)} collective-permute-done((bf16[512,512]{1,0:T(8,128)(2,1)}, bf16[512,512]{1,0:T(8,128)(2,1)S(1)}, u32[]{:S(2)}, u32[]{:S(2)}) %collective-permute-start.3) | collective-permute-done | bytes 524320 | tf_op jit(solution)/shard_map/ppermute | solution.py:329
  74.5 0.8 copy-done.7
  75.3 1.3 fusion.c0
  76.5 0.4 collective-permute-start.5
  77.0 3.0 %collective-permute-start.4 = (bf16[512,512]{1,0:T(8,128)(2,1)S(1)}, bf16[512,512]{1,0:T(8,128)(2,1)S(1)}, u32[]{:S(2)}, u32[]{:S(2)}) collective-permute-start(bf16[512,512]{1,0:T(8,128)(2,1)S(1)} %fusion.c0), channel_id=1, source_target_pairs={{0,1},{1,0},{2,3},{3,2},{4,5},{5,4},{6,7},{7,6},{8,9},{9,8},{10,11... | collective-permute-start | bytes 1572872 | tf_op jit(solution)/shard_map/ppermute | solution.py:333
  79.9 51.6 %collective-permute-done.5.c2 = bf16[512,512]{1,0:T(8,128)(2,1)S(1)} collective-permute-done((bf16[512,512]{1,0:T(8,128)(2,1)S(1)}, bf16[512,512]{1,0:T(8,128)(2,1)S(1)}, u32[]{:S(2)}, u32[]{:S(2)}) %collective-permute-start.5) | collective-permute-done | bytes 524320 | tf_op jit(solution)/shard_map/ppermute | solution.py:333
  131.5 0.4 collective-permute-start.6
  132.0 0.9 copy-done.6
  132.9 0.8 collective-permute-done.6.c3
  133.7 6.2 %project.1 = bf16[512,1024]{1,0:T(8,128)(2,1)} custom-call(s32[1]{0:T(128)} %bitcast.11.part, bf16[512,512]{1,0:T(8,128)(2,1)} %copy-done.2, bf16[512,512]{1,0:T(8,128)(2,1)} %copy-done.6, bf16[512,512]{1,0:T(8,128)(2,1)} %copy-done.5, bf16[512,512]{1,0:T(8,128)(2,1)} %collective-permute-done.6.c3, bf16[512,4096]{1,0:T(8,128)(2,1)} %w0.1, ...), custom_call_target="tpu_custom_call" | custom-call | flops 2147483648 | bytes 8000000 | tf_op jit(solution)/shard_map/project/pallas_call | solution.py:310
  (19 shorter events, 0.3 us)
Async XLA Ops:
  3.0 32.9 %collective-permute-start = (bf16[1024,512]{1,0:T(8,128)(2,1)}, bf16[1024,512]{1,0:T(8,128)(2,1)S(1)}, u32[]{:S(2)}, u32[]{:S(2)}) collective-permute-start(bf16[1024,512]{1,0:T(8,128)(2,1)} %get-tuple-element.12), channel_id=1, source_target_pairs={{0,4},{4,8},{8,12},{12,16},{16,20},{20,24},{24,28},{28,32},{32,36}... | collective-permute-start | bytes 3145736 | tf_op jit(solution)/shard_map/ppermute | solution.py:329
  6.6 30.4 %collective-permute-start.1 = (bf16[1024,512]{1,0:T(8,128)(2,1)}, bf16[1024,512]{1,0:T(8,128)(2,1)S(1)}, u32[]{:S(2)}, u32[]{:S(2)}) collective-permute-start(bf16[1024,512]{1,0:T(8,128)(2,1)} %get-tuple-element.13), channel_id=1, source_target_pairs={{4,0},{8,4},{12,8},{16,12},{20,16},{24,20},{28,24},{32,28},{36,32}... | collective-permute-start | bytes 3145736 | tf_op jit(solution)/shard_map/ppermute | solution.py:329
  35.9 1.0 copy-start
  36.9 1.0 copy-start.1
  46.4 26.1 %collective-permute-start.2 = (bf16[512,512]{1,0:T(8,128)(2,1)}, bf16[512,512]{1,0:T(8,128)(2,1)S(1)}, u32[]{:S(2)}, u32[]{:S(2)}) collective-permute-start(bf16[512,512]{1,0:T(8,128)(2,1)} %bitcast.40), channel_id=1, source_target_pairs={{4,0},{8,4},{12,8},{16,12},{20,16},{24,20},{28,24},{32,28},{36,32}... | collective-permute-start | bytes 1572872 | tf_op jit(solution)/shard_map/ppermute | solution.py:329
  56.1 18.4 %collective-permute-start.3 = (bf16[512,512]{1,0:T(8,128)(2,1)}, bf16[512,512]{1,0:T(8,128)(2,1)S(1)}, u32[]{:S(2)}, u32[]{:S(2)}) collective-permute-start(bf16[512,512]{1,0:T(8,128)(2,1)} %bitcast.39), channel_id=1, source_target_pairs={{0,4},{4,8},{8,12},{12,16},{16,20},{20,24},{24,28},{28,32},{32,36}... | collective-permute-start | bytes 1572872 | tf_op jit(solution)/shard_map/ppermute | solution.py:329
  60.9 71.0 %collective-permute-start.7 = (bf16[512,1024]{1,0:T(8,128)(2,1)}, bf16[512,1024]{1,0:T(8,128)(2,1)S(1)}, u32[]{:S(2)}, u32[]{:S(2)}) collective-permute-start(bf16[512,1024]{1,0:T(8,128)(2,1)} %get-tuple-element.19), channel_id=1, source_target_pairs={{0,1},{1,0},{2,3},{3,2},{4,5},{5,4},{6,7},{7,6},{8,9},{9,8},{10,11... | collective-permute-start | bytes 3145736 | tf_op jit(solution)/shard_map/ppermute | solution.py:333
  62.8 69.1 %collective-permute-start.8 = (bf16[512,1024]{1,0:T(8,128)(2,1)}, bf16[512,1024]{1,0:T(8,128)(2,1)S(1)}, u32[]{:S(2)}, u32[]{:S(2)}) collective-permute-start(bf16[512,1024]{1,0:T(8,128)(2,1)} %get-tuple-element.20), channel_id=1, source_target_pairs={{0,2},{1,3},{2,0},{3,1},{4,6},{5,7},{6,4},{7,5},{8,10},{9,11},{10,... | collective-permute-start | bytes 3145736 | tf_op jit(solution)/shard_map/ppermute | solution.py:333
  63.2 68.8 %collective-permute-start.9 = (bf16[512,1024]{1,0:T(8,128)(2,1)}, bf16[512,1024]{1,0:T(8,128)(2,1)}, u32[]{:S(2)}, u32[]{:S(2)}) collective-permute-start(bf16[512,1024]{1,0:T(8,128)(2,1)} %get-tuple-element.21), channel_id=1, source_target_pairs={{0,3},{1,2},{2,1},{3,0},{4,7},{5,6},{6,5},{7,4},{8,11},{9,10},{10,... | collective-permute-start | bytes 3145736 | tf_op jit(solution)/shard_map/ppermute | solution.py:333
  74.5 0.8 copy-start.7
  76.5 57.1 %copy-start.2 = (bf16[512,512]{1,0:T(8,128)(2,1)}, bf16[512,512]{1,0:T(8,128)(2,1)S(1)}, u32[]{:S(2)}) copy-start(bf16[512,512]{1,0:T(8,128)(2,1)S(1)} %fusion.c0) | copy-start | bytes 1572868
  76.5 55.0 %collective-permute-start.5 = (bf16[512,512]{1,0:T(8,128)(2,1)S(1)}, bf16[512,512]{1,0:T(8,128)(2,1)S(1)}, u32[]{:S(2)}, u32[]{:S(2)}) collective-permute-start(bf16[512,512]{1,0:T(8,128)(2,1)S(1)} %fusion.c0), channel_id=1, source_target_pairs={{0,2},{1,3},{2,0},{3,1},{4,6},{5,7},{6,4},{7,5},{8,10},{9,11},{10,... | collective-permute-start | bytes 1572872 | tf_op jit(solution)/shard_map/ppermute | solution.py:333
  77.0 55.1 %collective-permute-start.4 = (bf16[512,512]{1,0:T(8,128)(2,1)S(1)}, bf16[512,512]{1,0:T(8,128)(2,1)S(1)}, u32[]{:S(2)}, u32[]{:S(2)}) collective-permute-start(bf16[512,512]{1,0:T(8,128)(2,1)S(1)} %fusion.c0), channel_id=1, source_target_pairs={{0,1},{1,0},{2,3},{3,2},{4,5},{5,4},{6,7},{7,6},{8,9},{9,8},{10,11... | collective-permute-start | bytes 1572872 | tf_op jit(solution)/shard_map/ppermute | solution.py:333
  131.5 2.1 %copy-start.5 = (bf16[512,512]{1,0:T(8,128)(2,1)}, bf16[512,512]{1,0:T(8,128)(2,1)S(1)}, u32[]{:S(2)}) copy-start(bf16[512,512]{1,0:T(8,128)(2,1)S(1)} %collective-permute-done.5.c2) | copy-start | bytes 1572868
  131.5 2.1 %collective-permute-start.6 = (bf16[512,512]{1,0:T(8,128)(2,1)S(1)}, bf16[512,512]{1,0:T(8,128)(2,1)}, u32[]{:S(2)}, u32[]{:S(2)}) collective-permute-start(bf16[512,512]{1,0:T(8,128)(2,1)S(1)} %collective-permute-done.5.c2), channel_id=1, source_target_pairs={{0,1},{1,0},{2,3},{3,2},{4,5},{5,4},{6,7},{7,6},{8,9},{9,8},{10,11... | collective-permute-start | bytes 1572872 | tf_op jit(solution)/shard_map/ppermute | solution.py:333
  132.0 1.7 %copy-start.3 = (bf16[512,1024]{1,0:T(8,128)(2,1)}, bf16[512,1024]{1,0:T(8,128)(2,1)S(1)}, u32[]{:S(2)}) copy-start(bf16[512,1024]{1,0:T(8,128)(2,1)S(1)} %collective-permute-done.7.w1) | copy-start | bytes 3145732
  132.0 1.7 %copy-start.4 = (bf16[512,1024]{1,0:T(8,128)(2,1)}, bf16[512,1024]{1,0:T(8,128)(2,1)S(1)}, u32[]{:S(2)}) copy-start(bf16[512,1024]{1,0:T(8,128)(2,1)S(1)} %collective-permute-done.8.w2) | copy-start | bytes 3145732
  132.0 0.9 copy-start.6

commit v2 on v1

--- a/solution.py
+++ b/solution.py
@@ -14,6 +14,7 @@
 REACH = 2
 SLOTS = 4
 QUAD = 4
+Z_CHIPS = 8
 QW = HD * QUAD
 HEAD = ("head_0", "head_1")
 EXP_SCALE = 0.125 * 1.4426950408889634
@@ -292,35 +293,35 @@
     return out[0], [x.reshape(per * BLK, width) for x in out[1:]]
 
 
-def project_kernel(part, c0, c1, c2, c3, w0, w1, w2, w3, r_ref, o_ref):
+def project_kernel(part, c0, c1, w0, w1, r_ref, o_ref):
     total = r_ref[...].astype(jnp.float32)
-    for c, w in ((c0, w0), (c1, w1), (c2, w2), (c3, w3)):
+    for c, w in ((c0, w0), (c1, w1)):
         total = total + jnp.dot(c[...], w[...], preferred_element_type=jnp.float32)
     o_ref[...] = total.astype(o_ref.dtype)
 
 
-def project_call(part, contexts, own_weight, weights, residual):
+def project_call(part, contexts, weights, added, dtype):
     tokens, width = contexts[0].shape
-    columns = residual.shape[1]
+    columns = added.shape[1]
     tile = min(tokens, 256)
     c_spec = pl.BlockSpec((tile, width), lambda i, p: (i, 0))
-    w_own = pl.BlockSpec((width, columns), lambda i, p: (0, p[0]))
-    w_spec = pl.BlockSpec((width, columns), lambda i, p: (0, 0))
+    w_specs = [
+        pl.BlockSpec((width, columns), lambda i, p: (0, p[0]))
+        if w.shape[1] > columns
+        else pl.BlockSpec((width, columns), lambda i, p: (0, 0))
+        for w in weights
+    ]
     r_spec = pl.BlockSpec((tile, columns), lambda i, p: (i, 0))
     return pl.pallas_call(
         project_kernel,
         grid_spec=pltpu.PrefetchScalarGridSpec(
             num_scalar_prefetch=1,
             grid=(tokens // tile,),
-            in_specs=[c_spec] * 4 + [w_own, w_spec, w_spec, w_spec, r_spec],
+            in_specs=[c_spec] * 2 + w_specs + [r_spec],
             out_specs=r_spec,
         ),
-        out_shape=jax.ShapeDtypeStruct(residual.shape, jnp.bfloat16),
-        cost_estimate=pl.CostEstimate(
-            flops=2 * tokens * width * 4 * columns, transcendentals=0, bytes_accessed=8_000_000
-        ),
-        name="project",
-    )(part, *contexts, own_weight, *weights, residual)
+        out_shape=jax.ShapeDtypeStruct(added.shape, dtype),
+    )(part, *contexts, *weights, added)
 
 
 def shifted(block, axis, distance):
@@ -331,6 +332,15 @@
 
 def swapped(block, flip):
     return lax.ppermute(block, HEAD, [(i, i ^ flip) for i in range(4)])
+
+
+def other_side(block, flip):
+    axes = ("seq", *HEAD)
+    route = []
+    for s in range(lax.axis_size("seq")):
+        for h in range(4):
+            route.append((s * 4 + h, (s ^ Z_CHIPS) * 4 + (h ^ flip)))
+    return lax.ppermute(block, axes, route)
 
 
 def body(
@@ -357,7 +367,7 @@
     down = shifted(down, "seq", -1)
     across2, across3, across1 = cut_call(part, out_weight, columns)
     w2 = swapped(across2, 2)
-    w3 = swapped(across3, 3)
+    w3 = other_side(across3, 3)
     w1 = swapped(across1, 1)
     k3 = encoder_keys.reshape(blocks, BLK, width)
     v3 = encoder_values.reshape(blocks, BLK, width)
@@ -374,9 +384,8 @@
     across = swapped(context, 2)
     beside = swapped(context, 1)
     corner = swapped(across, 1)
-    decoder_out = project_call(
-        part, [context, beside, across, corner], out_weight, [w1, w2, w3], decoder_input
-    )
+    total = project_call(part, [context, beside], [out_weight, w1], decoder_input, jnp.float32)
+    decoder_out = project_call(part, [across, corner], [w2, w3], total, jnp.bfloat16)
     return (e3.reshape(blocks * BLK, width), decoder_out)
 
 

time: 140 us -> 120 us (0.86)
  waiting for transfers between devices: 65.8 us -> 42 us
  Pallas kernels: 38.6 us -> 41.1 us
    ppermute x6 -> x5, waiting for transfers between devices: 52.4 us -> 29.1 us  [swapped(): return lax.ppermute(block, HEAD, [(i, i ^ flip) for i in range(4)])]
    pallas_call x1 -> x2, Pallas kernels: 6.2 us -> 8.78 us  [project_call(): pl.pallas_call(project_kernel, grid_spec=pltpu.PrefetchScalarGridSpec(num...]
    ppermute x0 -> x1, starting transfers between devices: none -> 1.99 us  [other_side(): return lax.ppermute(block, axes, route)]
    ppermute x6 -> x5, starting transfers between devices: 7.45 us -> 6.03 us  [swapped(): return lax.ppermute(block, HEAD, [(i, i ^ flip) for i in range(4)])]
    unnamed x16 -> x14, local copies, waits for them, and re-layouts: 2.64 us -> 3.06 us
  transfers between devices with their start and end apart: 10 -> 10, of which waited for: 5 -> 4; matrix products, arithmetic and copies ran while one was open for 1% -> 1% of each run, Pallas kernels for 15% -> 22%
where the time goes in v2:
time: 120 us
  waiting for transfers between devices  42 us (35%)
  Pallas kernels  41.1 us (34%)
  starting transfers between devices  31.4 us (26%)
  local copies, waits for them, and re-layouts  3.06 us (3%)
  other arithmetic  1.28 us (1%)
    ppermute x5, waiting for transfers between devices, swapped(): return lax.ppermute(block, HEAD, [(i, i ^ flip) for i in range(4)])  29.1 us
    ppermute x4, starting transfers between devices, shifted(): return lax.ppermute(block, axis, route)  23.4 us
    pallas_call x2, Pallas kernels, stage_call(): pl.pallas_call(functools.partial(stage_kernel, sources, take_needed), in_...  16.4 us
    ppermute x4, waiting for transfers between devices, shifted(): return lax.ppermute(block, axis, route)  12.8 us
    pallas_call x1, Pallas kernels, inner_call(): pl.pallas_call(inner_kernel, grid_spec=pltpu.PrefetchScalarGridSpec(num_s...  10.7 us
    pallas_call x2, Pallas kernels, project_call(): pl.pallas_call(project_kernel, grid_spec=pltpu.PrefetchScalarGridSpec(num...  8.78 us
    ppermute x5, starting transfers between devices, swapped(): return lax.ppermute(block, HEAD, [(i, i ^ flip) for i in range(4)])  6.03 us
    unnamed x14, local copies, waits for them, and re-layouts  3.06 us
  transfers between devices with their start and end apart: 10, of which 4 were waited for; matrix products, arithmetic and copies ran while one was open for 1% of the time, Pallas kernels for 22%

profile of v2, /device:TPU:9, one launch (start us, length us, event | category | flops | bytes accessed | tf_op | source)
XLA Modules:
  0.0 119.6 jit_solution(17967440444810129204)
XLA Ops:
  0.6 2.4 %pack_edges.1 = (bf16[1024,512]{1,0:T(8,128)(2,1)}, bf16[1024,512]{1,0:T(8,128)(2,1)}) custom-call(bf16[1536,512]{1,0:T(8,128)(2,1)} %k.1, bf16[1536,512]{1,0:T(8,128)(2,1)} %v.1, bf16[512,512]{1,0:T(8,128)(2,1)} %q.1), custom_call_target="tpu_custom_call" | custom-call | tf_op jit(solution)/shard_map/pack_edges/pallas_call | solution.py:93
  3.0 3.5 %collective-permute-start = (bf16[1024,512]{1,0:T(8,128)(2,1)}, bf16[1024,512]{1,0:T(8,128)(2,1)S(1)}, u32[]{:S(2)}, u32[]{:S(2)}) collective-permute-start(bf16[1024,512]{1,0:T(8,128)(2,1)} %get-tuple-element.12), channel_id=1, source_target_pairs={{0,4},{4,8},{8,12},{12,16},{16,20},{20,24},{24,28},{28,32},{32,36}... | collective-permute-start | bytes 3145736 | tf_op jit(solution)/shard_map/ppermute | solution.py:330
  6.6 8.2 %collective-permute-start.1 = (bf16[1024,512]{1,0:T(8,128)(2,1)}, bf16[1024,512]{1,0:T(8,128)(2,1)S(1)}, u32[]{:S(2)}, u32[]{:S(2)}) collective-permute-start(bf16[1024,512]{1,0:T(8,128)(2,1)} %get-tuple-element.13), channel_id=1, source_target_pairs={{4,0},{8,4},{12,8},{16,12},{20,16},{24,20},{28,24},{32,28},{36,32}... | collective-permute-start | bytes 3145736 | tf_op jit(solution)/shard_map/ppermute | solution.py:330
  14.8 10.7 %encoder_inner.1 = bf16[1536,512]{1,0:T(8,128)(2,1)} custom-call(s32[1]{0:T(128)} %bitcast.position.pos, s32[12]{0:T(128)} %counts.5, s32[4,12]{1,0:T(4,128)} %bitcast.34, bf16[1536,512]{1,0:T(8,128)(2,1)} %q_ref.1, bf16[12,128,512]{2,1,0:T(8,128)(2,1)} %bitcast.18, bf16[12,128,512]{2,1,0:T(8,128)(2,1)} %bitcast.21), custom_call_target="tpu_custom_call" | custom-call | tf_op jit(solution)/shard_map/encoder_inner/pallas_call | solution.py:143
  25.5 10.5 %collective-permute-done = bf16[1024,512]{1,0:T(8,128)(2,1)S(1)} collective-permute-done((bf16[1024,512]{1,0:T(8,128)(2,1)}, bf16[1024,512]{1,0:T(8,128)(2,1)S(1)}, u32[]{:S(2)}, u32[]{:S(2)}) %collective-permute-start) | collective-permute-done | bytes 1048608 | tf_op jit(solution)/shard_map/ppermute | solution.py:330
  35.9 1.0 collective-permute-done.1
  36.9 1.0 copy-done.1
  37.9 8.5 %serve_remote.1 = (bf16[12,128,512]{2,1,0:T(8,128)(2,1)}, bf16[4,128,512]{2,1,0:T(8,128)(2,1)}, bf16[4,128,512]{2,1,0:T(8,128)(2,1)}) custom-call(s32[1]{0:T(128)} %bitcast.position.pos, s32[12]{0:T(128)} %counts.5, s32[4,12]{1,0:T(4,128)} %bitcast.35, s32[256]{0:T(256)} %owners.3, s32[2,256]{1,0:T(2,128)} %bitcast.37, ...), custom_call_target="tpu_custom_call", output_to_operand_aliasing={{0}: (11, {})} | custom-call | tf_op jit(solution)/shard_map/serve_remote/pallas_call | solution.py:276
  46.4 9.7 %collective-permute-start.2 = (bf16[512,512]{1,0:T(8,128)(2,1)}, bf16[512,512]{1,0:T(8,128)(2,1)S(1)}, u32[]{:S(2)}, u32[]{:S(2)}) collective-permute-start(bf16[512,512]{1,0:T(8,128)(2,1)} %bitcast.40), channel_id=1, source_target_pairs={{4,0},{8,4},{12,8},{16,12},{20,16},{24,20},{28,24},{32,28},{36,32}... | collective-permute-start | bytes 1572872 | tf_op jit(solution)/shard_map/ppermute | solution.py:330
  56.1 1.9 %collective-permute-start.3 = (bf16[512,512]{1,0:T(8,128)(2,1)}, bf16[512,512]{1,0:T(8,128)(2,1)S(1)}, u32[]{:S(2)}, u32[]{:S(2)}) collective-permute-start(bf16[512,512]{1,0:T(8,128)(2,1)} %bitcast.39), channel_id=1, source_target_pairs={{0,4},{4,8},{8,12},{12,16},{16,20},{20,24},{24,28},{28,32},{32,36}... | collective-permute-start | bytes 1572872 | tf_op jit(solution)/shard_map/ppermute | solution.py:330
  58.0 2.9 %cut_weight.1 = (bf16[512,1024]{1,0:T(8,128)(2,1)}, bf16[512,1024]{1,0:T(8,128)(2,1)}, bf16[512,1024]{1,0:T(8,128)(2,1)}) custom-call(s32[1]{0:T(128)} %bitcast.11.part, bf16[512,4096]{1,0:T(8,128)(2,1)} %w0.1), custom_call_target="tpu_custom_call" | custom-call | tf_op jit(solution)/shard_map/cut_weight/pallas_call | solution.py:120
  61.0 1.9 %collective-permute-start.9 = (bf16[512,1024]{1,0:T(8,128)(2,1)}, bf16[512,1024]{1,0:T(8,128)(2,1)}, u32[]{:S(2)}, u32[]{:S(2)}) collective-permute-start(bf16[512,1024]{1,0:T(8,128)(2,1)} %get-tuple-element.21), channel_id=1, source_target_pairs={{0,1},{1,0},{2,3},{3,2},{4,5},{5,4},{6,7},{7,6},{8,9},{9,8},{10,11... | collective-permute-start | bytes 3145736 | tf_op jit(solution)/shard_map/ppermute | solution.py:334
  63.2 2.0 %collective-permute-start.7 = (bf16[512,1024]{1,0:T(8,128)(2,1)}, bf16[512,1024]{1,0:T(8,128)(2,1)S(1)}, u32[]{:S(2)}, u32[]{:S(2)}) collective-permute-start(bf16[512,1024]{1,0:T(8,128)(2,1)} %get-tuple-element.20), channel_id=1, source_target_pairs={{0,35},{1,34},{2,33},{3,32},{4,39},{5,38},{6,37},{7,36},{8,43},{9,... | collective-permute-start | bytes 3145736 | tf_op jit(solution)/shard_map/ppermute | solution.py:343
  65.2 7.9 %serve_own.1 = (bf16[12,128,512]{2,1,0:T(8,128)(2,1)}, bf16[4,128,512]{2,1,0:T(8,128)(2,1)}) custom-call(s32[1]{0:T(128)} %bitcast.position.pos, s32[12]{0:T(128)} %counts.5, s32[4,12]{1,0:T(4,128)} %bitcast.36, s32[256]{0:T(256)} %owners.3, s32[2,256]{1,0:T(2,128)} %bitcast.38, bf16[12,128,512]{2,1,0:T(8,128)(2,1)} %bitcast.25, ...), custom_call_target="tpu_custom_call", output_to_operand_aliasing={{0}: (11, {})} | custom-call | tf_op jit(solution)/shard_map/serve_own/pallas_call | solution.py:276
  73.1 1.4 %collective-permute-done.3 = bf16[512,512]{1,0:T(8,128)(2,1)S(1)} collective-permute-done((bf16[512,512]{1,0:T(8,128)(2,1)}, bf16[512,512]{1,0:T(8,128)(2,1)S(1)}, u32[]{:S(2)}, u32[]{:S(2)}) %collective-permute-start.3) | collective-permute-done | bytes 524320 | tf_op jit(solution)/shard_map/ppermute | solution.py:330
  74.5 0.8 copy-done.6
  75.3 1.3 %fusion.c0 = bf16[512,512]{1,0:T(8,128)(2,1)S(1)} fusion(bf16[512,512]{1,0:T(8,128)(2,1)} %copy-done.6, bf16[512,512]{1,0:T(8,128)(2,1)S(1)} %collective-permute-done.2, bf16[4,128,512]{2,1,0:T(8,128)(2,1)} %get-tuple-element.16), kind=kLoop, calls=%fused_computation.1 | loop fusion | flops 524288 | bytes 2097152 | tf_op jit(solution)/shard_map/add | solution.py:383
  76.6 0.4 collective-permute-start.4
  77.0 3.0 %collective-permute-start.8 = (bf16[512,512]{1,0:T(8,128)(2,1)S(1)}, bf16[512,512]{1,0:T(8,128)(2,1)}, u32[]{:S(2)}, u32[]{:S(2)}) collective-permute-start(bf16[512,512]{1,0:T(8,128)(2,1)S(1)} %fusion.c0), channel_id=1, source_target_pairs={{0,1},{1,0},{2,3},{3,2},{4,5},{5,4},{6,7},{7,6},{8,9},{9,8},{10,11... | collective-permute-start | bytes 1572872 | tf_op jit(solution)/shard_map/ppermute | solution.py:334
  79.9 29.1 %collective-permute-done.4.c0 = bf16[512,512]{1,0:T(8,128)(2,1)S(1)} collective-permute-done((bf16[512,512]{1,0:T(8,128)(2,1)S(1)}, bf16[512,512]{1,0:T(8,128)(2,1)S(1)}, u32[]{:S(2)}, u32[]{:S(2)}) %collective-permute-start.4) | collective-permute-done | bytes 524320 | tf_op jit(solution)/shard_map/ppermute | solution.py:334
  109.1 0.4 collective-permute-start.5
  109.5 4.4 %shard_map.113.r_ref = f32[512,1024]{1,0:T(8,128)} custom-call(s32[1]{0:T(128)} %bitcast.11.part, bf16[512,512]{1,0:T(8,128)(2,1)} %copy-done.2, bf16[512,512]{1,0:T(8,128)(2,1)} %collective-permute-done.8.c1, bf16[512,4096]{1,0:T(8,128)(2,1)} %w0.1, bf16[512,1024]{1,0:T(8,128)(2,1)} %collective-permute-done.9.w1, bf16[512,1024]{1,0:T(8,128)(2,1)} %r_ref.1), custom_call_target="tpu_custom_call" | custom-call | tf_op jit(solution)/shard_map/pallas_call | solution.py:315
  114.0 1.0 copy-done.3
  115.3 4.4 %shard_map.114 = bf16[512,1024]{1,0:T(8,128)(2,1)} custom-call(s32[1]{0:T(128)} %bitcast.11.part, bf16[512,512]{1,0:T(8,128)(2,1)} %copy-done.5, bf16[512,512]{1,0:T(8,128)(2,1)} %collective-permute-done.5.c1, bf16[512,1024]{1,0:T(8,128)(2,1)} %copy-done.3, bf16[512,1024]{1,0:T(8,128)(2,1)} %copy-done.4, f32[512,1024]{1,0:T(8,128)} %shard_map.113.r_ref), custom_call_target="tpu_custom_call" | custom-call | tf_op jit(solution)/shard_map/pallas_call | solution.py:315
  (18 shorter events, 0.7 us)
Async XLA Ops:
  3.0 32.9 %collective-permute-start = (bf16[1024,512]{1,0:T(8,128)(2,1)}, bf16[1024,512]{1,0:T(8,128)(2,1)S(1)}, u32[]{:S(2)}, u32[]{:S(2)}) collective-permute-start(bf16[1024,512]{1,0:T(8,128)(2,1)} %get-tuple-element.12), channel_id=1, source_target_pairs={{0,4},{4,8},{8,12},{12,16},{16,20},{20,24},{24,28},{28,32},{32,36}... | collective-permute-start | bytes 3145736 | tf_op jit(solution)/shard_map/ppermute | solution.py:330
  6.6 30.4 %collective-permute-start.1 = (bf16[1024,512]{1,0:T(8,128)(2,1)}, bf16[1024,512]{1,0:T(8,128)(2,1)S(1)}, u32[]{:S(2)}, u32[]{:S(2)}) collective-permute-start(bf16[1024,512]{1,0:T(8,128)(2,1)} %get-tuple-element.13), channel_id=1, source_target_pairs={{4,0},{8,4},{12,8},{16,12},{20,16},{24,20},{28,24},{32,28},{36,32}... | collective-permute-start | bytes 3145736 | tf_op jit(solution)/shard_map/ppermute | solution.py:330
  35.9 1.0 copy-start
  36.9 1.0 copy-start.1
  46.4 26.7 %collective-permute-start.2 = (bf16[512,512]{1,0:T(8,128)(2,1)}, bf16[512,512]{1,0:T(8,128)(2,1)S(1)}, u32[]{:S(2)}, u32[]{:S(2)}) collective-permute-start(bf16[512,512]{1,0:T(8,128)(2,1)} %bitcast.40), channel_id=1, source_target_pairs={{4,0},{8,4},{12,8},{16,12},{20,16},{24,20},{28,24},{32,28},{36,32}... | collective-permute-start | bytes 1572872 | tf_op jit(solution)/shard_map/ppermute | solution.py:330
  56.1 18.4 %collective-permute-start.3 = (bf16[512,512]{1,0:T(8,128)(2,1)}, bf16[512,512]{1,0:T(8,128)(2,1)S(1)}, u32[]{:S(2)}, u32[]{:S(2)}) collective-permute-start(bf16[512,512]{1,0:T(8,128)(2,1)} %bitcast.39), channel_id=1, source_target_pairs={{0,4},{4,8},{8,12},{12,16},{16,20},{20,24},{24,28},{28,32},{32,36}... | collective-permute-start | bytes 1572872 | tf_op jit(solution)/shard_map/ppermute | solution.py:330
  61.0 48.6 %collective-permute-start.9 = (bf16[512,1024]{1,0:T(8,128)(2,1)}, bf16[512,1024]{1,0:T(8,128)(2,1)}, u32[]{:S(2)}, u32[]{:S(2)}) collective-permute-start(bf16[512,1024]{1,0:T(8,128)(2,1)} %get-tuple-element.21), channel_id=1, source_target_pairs={{0,1},{1,0},{2,3},{3,2},{4,5},{5,4},{6,7},{7,6},{8,9},{9,8},{10,11... | collective-permute-start | bytes 3145736 | tf_op jit(solution)/shard_map/ppermute | solution.py:334
  62.8 51.1 %collective-permute-start.6 = (bf16[512,1024]{1,0:T(8,128)(2,1)}, bf16[512,1024]{1,0:T(8,128)(2,1)S(1)}, u32[]{:S(2)}, u32[]{:S(2)}) collective-permute-start(bf16[512,1024]{1,0:T(8,128)(2,1)} %get-tuple-element.19), channel_id=1, source_target_pairs={{0,2},{1,3},{2,0},{3,1},{4,6},{5,7},{6,4},{7,5},{8,10},{9,11},{10,... | collective-permute-start | bytes 3145736 | tf_op jit(solution)/shard_map/ppermute | solution.py:334
  63.2 50.8 %collective-permute-start.7 = (bf16[512,1024]{1,0:T(8,128)(2,1)}, bf16[512,1024]{1,0:T(8,128)(2,1)S(1)}, u32[]{:S(2)}, u32[]{:S(2)}) collective-permute-start(bf16[512,1024]{1,0:T(8,128)(2,1)} %get-tuple-element.20), channel_id=1, source_target_pairs={{0,35},{1,34},{2,33},{3,32},{4,39},{5,38},{6,37},{7,36},{8,43},{9,... | collective-permute-start | bytes 3145736 | tf_op jit(solution)/shard_map/ppermute | solution.py:343
  74.5 0.8 copy-start.6
  76.5 33.0 %copy-start.2 = (bf16[512,512]{1,0:T(8,128)(2,1)}, bf16[512,512]{1,0:T(8,128)(2,1)S(1)}, u32[]{:S(2)}) copy-start(bf16[512,512]{1,0:T(8,128)(2,1)S(1)} %fusion.c0) | copy-start | bytes 1572868
  76.6 32.5 %collective-permute-start.4 = (bf16[512,512]{1,0:T(8,128)(2,1)S(1)}, bf16[512,512]{1,0:T(8,128)(2,1)S(1)}, u32[]{:S(2)}, u32[]{:S(2)}) collective-permute-start(bf16[512,512]{1,0:T(8,128)(2,1)S(1)} %fusion.c0), channel_id=1, source_target_pairs={{0,2},{1,3},{2,0},{3,1},{4,6},{5,7},{6,4},{7,5},{8,10},{9,11},{10,... | collective-permute-start | bytes 1572872 | tf_op jit(solution)/shard_map/ppermute | solution.py:334
  77.0 32.5 %collective-permute-start.8 = (bf16[512,512]{1,0:T(8,128)(2,1)S(1)}, bf16[512,512]{1,0:T(8,128)(2,1)}, u32[]{:S(2)}, u32[]{:S(2)}) collective-permute-start(bf16[512,512]{1,0:T(8,128)(2,1)S(1)} %fusion.c0), channel_id=1, source_target_pairs={{0,1},{1,0},{2,3},{3,2},{4,5},{5,4},{6,7},{7,6},{8,9},{9,8},{10,11... | collective-permute-start | bytes 1572872 | tf_op jit(solution)/shard_map/ppermute | solution.py:334
  109.1 4.9 %copy-start.5 = (bf16[512,512]{1,0:T(8,128)(2,1)}, bf16[512,512]{1,0:T(8,128)(2,1)S(1)}, u32[]{:S(2)}) copy-start(bf16[512,512]{1,0:T(8,128)(2,1)S(1)} %collective-permute-done.4.c0) | copy-start | bytes 1572868
  109.1 4.9 %collective-permute-start.5 = (bf16[512,512]{1,0:T(8,128)(2,1)S(1)}, bf16[512,512]{1,0:T(8,128)(2,1)}, u32[]{:S(2)}, u32[]{:S(2)}) collective-permute-start(bf16[512,512]{1,0:T(8,128)(2,1)S(1)} %collective-permute-done.4.c0), channel_id=1, source_target_pairs={{0,1},{1,0},{2,3},{3,2},{4,5},{5,4},{6,7},{7,6},{8,9},{9,8},{10,11... | collective-permute-start | bytes 1572872 | tf_op jit(solution)/shard_map/ppermute | solution.py:334
  113.9 1.0 copy-start.3
  114.0 1.3 %copy-start.4 = (bf16[512,1024]{1,0:T(8,128)(2,1)}, bf16[512,1024]{1,0:T(8,128)(2,1)S(1)}, u32[]{:S(2)}) copy-start(bf16[512,1024]{1,0:T(8,128)(2,1)S(1)} %collective-permute-done.7.w1) | copy-start | bytes 3145732

commit v3 on v2

--- a/solution.py
+++ b/solution.py
@@ -56,43 +56,55 @@
             attend_listed(q_ref, k_ref, v_ref, ids[:n], o_ref)
 
 
-def move(plan, stages, load_sem, store_sem):
-    loads = [pltpu.make_async_copy(src, stages[i], load_sem.at[i]) for src, i, _ in plan]
-    stores = []
-    for load in loads:
-        load.start()
-    for load, (_, i, targets) in zip(loads, plan):
-        load.wait()
-        for dst in targets:
-            stores.append(pltpu.make_async_copy(stages[i], dst, store_sem))
-            stores[-1].start()
-    for store in stores:
-        store.wait()
-
-
-def send_kernel(k, v, q, up, down, s0, s1, s2, s3, s4, load_sem, store_sem):
+def send_kernel(pos, k, v, q, near, far, s0, s1, s2, s3, s4, load_sem, store_sem):
     halo = REACH * BLK
     tail = pl.ds(k.shape[0] - halo, halo)
     head = pl.ds(0, halo)
     rest = pl.ds(2 * halo, q.shape[0])
-    plan = (
-        (k.at[tail], 0, (up.at[head],)),
-        (v.at[tail], 1, (up.at[pl.ds(halo, halo)],)),
-        (k.at[head], 2, (down.at[head],)),
-        (v.at[head], 3, (down.at[pl.ds(halo, halo)],)),
-        (q, 4, (up.at[rest], down.at[rest])),
-    )
-    move(plan, (s0, s1, s2, s3, s4), load_sem, store_sem)
-
-
-def send_call(k, v, q):
+    values = pl.ds(halo, halo)
+    stages = (s0, s1, s2, s3, s4)
+    sources = (k.at[tail], v.at[tail], k.at[head], v.at[head], q)
+    loads = [pltpu.make_async_copy(x, stages[i], load_sem.at[i]) for i, x in enumerate(sources)]
+    for load in loads:
+        load.start()
+    for load in loads:
+        load.wait()
+
+    def stores(up, down):
+        pairs = (
+            (s0, up.at[head]),
+            (s1, up.at[values]),
+            (s2, down.at[head]),
+            (s3, down.at[values]),
+            (s4, up.at[rest]),
+            (s4, down.at[rest]),
+        )
+        return [pltpu.make_async_copy(a, b, store_sem) for a, b in pairs]
+
+    even = pos[0] % 2 == 0
+
+    @pl.when(even)
+    def _():
+        for store in stores(near, far):
+            store.start()
+
+    @pl.when(jnp.logical_not(even))
+    def _():
+        for store in stores(far, near):
+            store.start()
+
+    for store in stores(near, far):
+        store.wait()
+
+
+def send_call(position, k, v, q):
     halo = REACH * BLK
     width = k.shape[1]
     shape = jax.ShapeDtypeStruct((2 * halo + q.shape[0], width), k.dtype)
     hbm = pl.BlockSpec(memory_space=pl.ANY)
     return pl.pallas_call(
         send_kernel,
-        in_specs=[hbm] * 3,
+        in_specs=[pl.BlockSpec(memory_space=pltpu.SMEM)] + [hbm] * 3,
         out_specs=[hbm] * 2,
         out_shape=[shape] * 2,
         scratch_shapes=[pltpu.VMEM((halo, width), k.dtype)] * 4
@@ -102,15 +114,27 @@
             pltpu.SemaphoreType.DMA,
         ],
         name="pack_edges",
-    )(k, v, q)
+    )(position, k, v, q)
+
+
+def move(plan, stages, load_sem, store_sem):
+    loads = [pltpu.make_async_copy(src, stages[i], load_sem.at[i]) for i, (src, _) in enumerate(plan)]
+    stores = [pltpu.make_async_copy(stages[i], dst, store_sem) for i, (_, dst) in enumerate(plan)]
+    for load in loads:
+        load.start()
+    for load, store in zip(loads, stores):
+        load.wait()
+        store.start()
+    for store in stores:
+        store.wait()
 
 
 def cut_kernel(part, w, a, b, c, sa, sb, sc, load_sem, store_sem):
     columns = a.shape[1]
     plan = []
-    for i, (flip, dst) in enumerate(((2, a), (3, b), (1, c))):
+    for flip, dst in ((2, a), (3, b), (1, c)):
         start = pl.multiple_of((part[0] ^ flip) * columns, columns)
-        plan.append((w.at[:, pl.ds(start, columns)], i, (dst,)))
+        plan.append((w.at[:, pl.ds(start, columns)], dst))
     move(plan, (sa, sb, sc), load_sem, store_sem)
 
 
@@ -151,7 +175,7 @@
 
 
 def stage_kernel(
-    sources, take_needed, pos, counts, lists, owners, slots, q, k, v, up, down, dec, _, *refs
+    sources, take_needed, pos, counts, lists, owners, slots, q, k, v, beside, beyond, dec, _, *refs
 ):
     e = refs[0]
     answers = refs[1 : 1 + len(sources)]
@@ -161,30 +185,56 @@
     mine = pos[0]
     per = answers[0].shape[0]
     total = owners.shape[0] // per
-    hold = pl.ds(0, REACH)
-    next_hold = pl.ds(REACH, REACH)
+    even = mine % 2 == 0
+    inner = pl.ds(REACH, blocks - near)
+    edge_sem, rest_sem, edge_out_sem, answer_sem = (sems.at[i] for i in range(4))
+
+    def from_neighbours(up, down):
+        first = [
+            (up.at[pl.ds(0, REACH)], kb.at[pl.ds(0, REACH)]),
+            (down.at[pl.ds(0, REACH)], kb.at[pl.ds(REACH + blocks, REACH)]),
+            (up.at[pl.ds(REACH, REACH)], vb.at[pl.ds(0, REACH)]),
+            (down.at[pl.ds(REACH, REACH)], vb.at[pl.ds(REACH + blocks, REACH)]),
+        ]
+        second = []
+        for i, shift in enumerate(sources):
+            if shift:
+                src = (up if shift < 0 else down).at[pl.ds(near, per)]
+                second.append((src, qd.at[pl.ds(i * per, per)]))
+        return [pltpu.make_async_copy(a, b, edge_sem) for a, b in first], [
+            pltpu.make_async_copy(a, b, rest_sem) for a, b in second
+        ]
+
     first = [
-        (up.at[hold], kb.at[pl.ds(0, REACH)]),
         (k, kb.at[pl.ds(REACH, blocks)]),
-        (down.at[hold], kb.at[pl.ds(REACH + blocks, REACH)]),
-        (up.at[next_hold], vb.at[pl.ds(0, REACH)]),
         (v.at[pl.ds(0, near)], vb.at[pl.ds(REACH, near)]),
         (v.at[pl.ds(blocks - near, near)], vb.at[pl.ds(REACH + blocks - near, near)]),
-        (down.at[next_hold], vb.at[pl.ds(REACH + blocks, REACH)]),
         (q.at[pl.ds(0, REACH)], qe.at[pl.ds(0, REACH)]),
         (q.at[pl.ds(blocks - REACH, REACH)], qe.at[pl.ds(REACH, REACH)]),
     ]
-    inner = pl.ds(REACH, blocks - near)
-    second = [(e.at[inner], eb.at[inner])]
-    if not take_needed:
-        second = [(e, eb)]
-    for i, shift in enumerate(sources):
-        src = {-1: up.at[pl.ds(near, per)], 1: down.at[pl.ds(near, per)], 0: dec}[shift]
-        second.append((src, qd.at[pl.ds(i * per, per)]))
-    first = [pltpu.make_async_copy(a, b, sems.at[0]) for a, b in first]
-    second = [pltpu.make_async_copy(a, b, sems.at[1]) for a, b in second]
+    second = [(e.at[inner], eb.at[inner]) if take_needed else (e, eb)]
+    if 0 in sources:
+        second.append((dec, qd.at[pl.ds(sources.index(0) * per, per)]))
+    first = [pltpu.make_async_copy(a, b, edge_sem) for a, b in first]
+    second = [pltpu.make_async_copy(a, b, rest_sem) for a, b in second]
+
+    @pl.when(even)
+    def _():
+        for group in from_neighbours(beyond, beside):
+            for copy in group:
+                copy.start()
+
+    @pl.when(jnp.logical_not(even))
+    def _():
+        for group in from_neighbours(beside, beyond):
+            for copy in group:
+                copy.start()
+
     for copy in first + second:
         copy.start()
+    more_first, more_second = from_neighbours(beyond, beside)
+    first += more_first
+    second += more_second
 
     def candidate(shift, t):
         source = mine + shift
@@ -219,7 +269,7 @@
             base = mine * blocks - REACH
             ids = [lists[j, b] - base for j in range(SLOTS)]
             branch_on_count(counts[b], ids, qe.at[t], kb, vb, eb.at[b])
-            pltpu.make_async_copy(eb.at[b], e.at[b], sems.at[2]).start()
+            pltpu.make_async_copy(eb.at[b], e.at[b], edge_out_sem).start()
 
     if take_needed:
         for copy in second:
@@ -245,20 +295,32 @@
             def _():
                 ob[i * per + t] = jnp.zeros(ob.shape[1:], ob.dtype)
 
-        pltpu.make_async_copy(ob.at[pl.ds(i * per, per)], answers[i], sems.at[3]).start()
+        rows = ob.at[pl.ds(i * per, per)]
+        if shift == 0:
+            pltpu.make_async_copy(rows, answers[0], answer_sem).start()
+        else:
+            to_beside = even if shift > 0 else jnp.logical_not(even)
+
+            @pl.when(to_beside)
+            def _(rows=rows):
+                pltpu.make_async_copy(rows, answers[0], answer_sem).start()
+
+            @pl.when(jnp.logical_not(to_beside))
+            def _(rows=rows):
+                pltpu.make_async_copy(rows, answers[1], answer_sem).start()
 
     for i in range(len(sources)):
-        pltpu.make_async_copy(ob.at[pl.ds(i * per, per)], answers[i], sems.at[3]).wait()
+        pltpu.make_async_copy(ob.at[pl.ds(i * per, per)], answers[i], answer_sem).wait()
 
     @pl.loop(0, near)
     def _(t):
         @pl.when(due(t))
         def _():
             b = edge_of(t)
-            pltpu.make_async_copy(eb.at[b], e.at[b], sems.at[2]).wait()
-
-
-def stage_call(sources, take_needed, scalars, q, k3, v3, up, down, dec, e):
+            pltpu.make_async_copy(eb.at[b], e.at[b], edge_out_sem).wait()
+
+
+def stage_call(sources, take_needed, scalars, q, k3, v3, beside, beyond, dec, e):
     blocks, _, width = k3.shape
     near = 2 * REACH
     per = dec.shape[0] // BLK
@@ -289,7 +351,7 @@
         ],
         input_output_aliases={11: 0},
         name="serve_remote" if take_needed else "serve_own",
-    )(*scalars, cut(q), k3, v3, cut(up), cut(down), cut(dec), e)
+    )(*scalars, cut(q), k3, v3, cut(beside), cut(beyond), cut(dec), e)
     return out[0], [x.reshape(per * BLK, width) for x in out[1:]]
 
 
@@ -324,10 +386,11 @@
     )(part, *contexts, *weights, added)
 
 
-def shifted(block, axis, distance):
-    devices = range(lax.axis_size(axis))
-    route = [(i - distance, i) for i in devices if i - distance in devices]
-    return lax.ppermute(block, axis, route)
+def exchanged(block, first):
+    route = []
+    for i in range(first, lax.axis_size("seq") - 1, 2):
+        route += [(i, i + 1), (i + 1, i)]
+    return lax.ppermute(block, "seq", route)
 
 
 def swapped(block, flip):
@@ -362,9 +425,9 @@
     columns = decoder_input.shape[1]
     lists = block_lists.T
     slots = cross_slots.T
-    up, down = send_call(encoder_keys, encoder_values, decoder_queries)
-    up = shifted(up, "seq", 1)
-    down = shifted(down, "seq", -1)
+    beside, beyond = send_call(position, encoder_keys, encoder_values, decoder_queries)
+    beside = exchanged(beside, 0)
+    beyond = exchanged(beyond, 1)
     across2, across3, across1 = cut_call(part, out_weight, columns)
     w2 = swapped(across2, 2)
     w3 = other_side(across3, 3)
@@ -373,14 +436,14 @@
     v3 = encoder_values.reshape(blocks, BLK, width)
     partial = inner_call(position, block_counts, lists, encoder_queries, k3, v3)
     scalars = (position, block_counts, lists, span_owner, slots)
-    shared = (encoder_queries, k3, v3, up, down, decoder_queries)
-    e3, (for_prev, for_next) = stage_call(
+    shared = (encoder_queries, k3, v3, beside, beyond, decoder_queries)
+    e3, (for_beside, for_beyond) = stage_call(
         (-1, 1), True, scalars, *shared, partial.reshape(blocks, BLK, width)
     )
-    from_next = shifted(for_prev, "seq", -1)
-    from_prev = shifted(for_next, "seq", 1)
+    from_beside = exchanged(for_beside, 0)
+    from_beyond = exchanged(for_beyond, 1)
     e3, (own,) = stage_call((0,), False, scalars, *shared, e3)
-    context = own + from_next + from_prev
+    context = own + from_beside + from_beyond
     across = swapped(context, 2)
     beside = swapped(context, 1)
     corner = swapped(across, 1)

time: 120 us -> 113 us (0.942)
  the two profiles are of different devices: /device:TPU:9 before, /device:TPU:21 now
where the time goes in v3:
time: 113 us; the launch traced here: 112 us
  waiting for transfers between devices  42.5 us (38%)
  Pallas kernels  41.7 us (37%)
  starting transfers between devices  23 us (20%)
  local copies, waits for them, and re-layouts  3.05 us (3%)
  other arithmetic  1.28 us (1%)
    ppermute x5, waiting for transfers between devices, swapped(): return lax.ppermute(block, HEAD, [(i, i ^ flip) for i in range(4)])  30.7 us
    ppermute x4, starting transfers between devices, exchanged(): return lax.ppermute(block, 'seq', route)  16.3 us
    pallas_call x2, Pallas kernels, stage_call(): pl.pallas_call(functools.partial(stage_kernel, sources, take_needed), in_...  16.2 us
    ppermute x4, waiting for transfers between devices, exchanged(): return lax.ppermute(block, 'seq', route)  11.8 us
    pallas_call x1, Pallas kernels, inner_call(): pl.pallas_call(inner_kernel, grid_spec=pltpu.PrefetchScalarGridSpec(num_s...  11.1 us
    pallas_call x2, Pallas kernels, project_call(): pl.pallas_call(project_kernel, grid_spec=pltpu.PrefetchScalarGridSpec(num...  8.78 us
    ppermute x5, starting transfers between devices, swapped(): return lax.ppermute(block, HEAD, [(i, i ^ flip) for i in range(4)])  6.69 us
    unnamed x14, local copies, waits for them, and re-layouts  3.05 us
  transfers between devices with their start and end apart: 10, of which 3 were waited for; matrix products, arithmetic and copies ran while one was open for 1% of the time, Pallas kernels for 22%

profile of v3, /device:TPU:21, one launch (start us, length us, event | category | flops | bytes accessed | tf_op | source)
XLA Modules:
  0.0 112.3 jit_solution(101200503398564516)
XLA Ops:
  0.6 2.7 %pack_edges.1 = (bf16[1024,512]{1,0:T(8,128)(2,1)}, bf16[1024,512]{1,0:T(8,128)(2,1)}) custom-call(s32[1]{0:T(128)} %bitcast.pos.position, bf16[1536,512]{1,0:T(8,128)(2,1)} %k.1, bf16[1536,512]{1,0:T(8,128)(2,1)} %v.1, bf16[512,512]{1,0:T(8,128)(2,1)} %q.1), custom_call_target="tpu_custom_call" | custom-call | tf_op jit(solution)/shard_map/pack_edges/pallas_call | solution.py:105
  3.4 1.7 %collective-permute-start = (bf16[1024,512]{1,0:T(8,128)(2,1)}, bf16[1024,512]{1,0:T(8,128)(2,1)S(1)}, u32[]{:S(2)}, u32[]{:S(2)}) collective-permute-start(bf16[1024,512]{1,0:T(8,128)(2,1)} %get-tuple-element.12), channel_id=1, source_target_pairs={{0,4},{4,0},{8,12},{12,8},{16,20},{20,16},{24,28},{28,24},{32,36},... | collective-permute-start | bytes 3145736 | tf_op jit(solution)/shard_map/ppermute | solution.py:393
  5.1 6.5 %collective-permute-start.1 = (bf16[1024,512]{1,0:T(8,128)(2,1)}, bf16[1024,512]{1,0:T(8,128)(2,1)S(1)}, u32[]{:S(2)}, u32[]{:S(2)}) collective-permute-start(bf16[1024,512]{1,0:T(8,128)(2,1)} %get-tuple-element.13), channel_id=1, source_target_pairs={{4,8},{8,4},{12,16},{16,12},{20,24},{24,20},{28,32},{32,28},{36,40... | collective-permute-start | bytes 3145736 | tf_op jit(solution)/shard_map/ppermute | solution.py:393
  11.6 11.1 %encoder_inner.1 = bf16[1536,512]{1,0:T(8,128)(2,1)} custom-call(s32[1]{0:T(128)} %bitcast.pos.position, s32[12]{0:T(128)} %counts.5, s32[4,12]{1,0:T(4,128)} %bitcast.34, bf16[1536,512]{1,0:T(8,128)(2,1)} %q_ref.1, bf16[12,128,512]{2,1,0:T(8,128)(2,1)} %bitcast.18, bf16[12,128,512]{2,1,0:T(8,128)(2,1)} %bitcast.21), custom_call_target="tpu_custom_call" | custom-call | tf_op jit(solution)/shard_map/encoder_inner/pallas_call | solution.py:167
  22.7 5.3 %collective-permute-done = bf16[1024,512]{1,0:T(8,128)(2,1)S(1)} collective-permute-done((bf16[1024,512]{1,0:T(8,128)(2,1)}, bf16[1024,512]{1,0:T(8,128)(2,1)S(1)}, u32[]{:S(2)}, u32[]{:S(2)}) %collective-permute-start) | collective-permute-done | bytes 1048608 | tf_op jit(solution)/shard_map/ppermute | solution.py:393
  28.1 6.5 %collective-permute-done.1 = bf16[1024,512]{1,0:T(8,128)(2,1)S(1)} collective-permute-done((bf16[1024,512]{1,0:T(8,128)(2,1)}, bf16[1024,512]{1,0:T(8,128)(2,1)S(1)}, u32[]{:S(2)}, u32[]{:S(2)}) %collective-permute-start.1) | collective-permute-done | bytes 1048608 | tf_op jit(solution)/shard_map/ppermute | solution.py:393
  34.6 1.0 copy-done.1
  35.5 10.0 %serve_remote.1 = (bf16[12,128,512]{2,1,0:T(8,128)(2,1)}, bf16[4,128,512]{2,1,0:T(8,128)(2,1)}, bf16[4,128,512]{2,1,0:T(8,128)(2,1)}) custom-call(s32[1]{0:T(128)} %bitcast.pos.position, s32[12]{0:T(128)} %counts.5, s32[4,12]{1,0:T(4,128)} %bitcast.35, s32[256]{0:T(256)} %owners.3, s32[2,256]{1,0:T(2,128)} %bitcast.37, ...), custom_call_target="tpu_custom_call", output_to_operand_aliasing={{0}: (11, {})} | custom-call | tf_op jit(solution)/shard_map/serve_remote/pallas_call | solution.py:338
  45.5 0.1 collective-permute-start.2
  45.6 8.0 %collective-permute-start.3 = (bf16[512,512]{1,0:T(8,128)(2,1)}, bf16[512,512]{1,0:T(8,128)(2,1)S(1)}, u32[]{:S(2)}, u32[]{:S(2)}) collective-permute-start(bf16[512,512]{1,0:T(8,128)(2,1)} %bitcast.39), channel_id=1, source_target_pairs={{4,8},{8,4},{12,16},{16,12},{20,24},{24,20},{28,32},{32,28},{36,40... | collective-permute-start | bytes 1572872 | tf_op jit(solution)/shard_map/ppermute | solution.py:393
  53.6 2.9 %cut_weight.1 = (bf16[512,1024]{1,0:T(8,128)(2,1)}, bf16[512,1024]{1,0:T(8,128)(2,1)}, bf16[512,1024]{1,0:T(8,128)(2,1)}) custom-call(s32[1]{0:T(128)} %bitcast.11.part, bf16[512,4096]{1,0:T(8,128)(2,1)} %w0.1), custom_call_target="tpu_custom_call" | custom-call | tf_op jit(solution)/shard_map/cut_weight/pallas_call | solution.py:144
  56.5 2.2 %collective-permute-start.9 = (bf16[512,1024]{1,0:T(8,128)(2,1)}, bf16[512,1024]{1,0:T(8,128)(2,1)}, u32[]{:S(2)}, u32[]{:S(2)}) collective-permute-start(bf16[512,1024]{1,0:T(8,128)(2,1)} %get-tuple-element.21), channel_id=1, source_target_pairs={{0,1},{1,0},{2,3},{3,2},{4,5},{5,4},{6,7},{7,6},{8,9},{9,8},{10,11... | collective-permute-start | bytes 3145736 | tf_op jit(solution)/shard_map/ppermute | solution.py:397
  58.7 1.8 %collective-permute-start.6 = (bf16[512,1024]{1,0:T(8,128)(2,1)}, bf16[512,1024]{1,0:T(8,128)(2,1)S(1)}, u32[]{:S(2)}, u32[]{:S(2)}) collective-permute-start(bf16[512,1024]{1,0:T(8,128)(2,1)} %get-tuple-element.19), channel_id=1, source_target_pairs={{0,2},{1,3},{2,0},{3,1},{4,6},{5,7},{6,4},{7,5},{8,10},{9,11},{10,... | collective-permute-start | bytes 3145736 | tf_op jit(solution)/shard_map/ppermute | solution.py:397
  60.5 6.2 %serve_own.1 = (bf16[12,128,512]{2,1,0:T(8,128)(2,1)}, bf16[4,128,512]{2,1,0:T(8,128)(2,1)}) custom-call(s32[1]{0:T(128)} %bitcast.pos.position, s32[12]{0:T(128)} %counts.5, s32[4,12]{1,0:T(4,128)} %bitcast.36, s32[256]{0:T(256)} %owners.3, s32[2,256]{1,0:T(2,128)} %bitcast.38, bf16[12,128,512]{2,1,0:T(8,128)(2,1)} %bitcast.25, ...), custom_call_target="tpu_custom_call", output_to_operand_aliasing={{0}: (11, {})} | custom-call | tf_op jit(solution)/shard_map/serve_own/pallas_call | solution.py:338
  66.8 0.8 copy-done.6
  67.6 1.3 %fusion.c0 = bf16[512,512]{1,0:T(8,128)(2,1)S(1)} fusion(bf16[512,512]{1,0:T(8,128)(2,1)} %copy-done.6, bf16[512,512]{1,0:T(8,128)(2,1)S(1)} %collective-permute-done.2, bf16[4,128,512]{2,1,0:T(8,128)(2,1)} %get-tuple-element.16), kind=kLoop, calls=%fused_computation.1 | loop fusion | flops 524288 | bytes 2097152 | tf_op jit(solution)/shard_map/add | solution.py:446
  68.8 0.1 collective-permute-start.4
  68.9 2.2 %collective-permute-start.8 = (bf16[512,512]{1,0:T(8,128)(2,1)S(1)}, bf16[512,512]{1,0:T(8,128)(2,1)}, u32[]{:S(2)}, u32[]{:S(2)}) collective-permute-start(bf16[512,512]{1,0:T(8,128)(2,1)S(1)} %fusion.c0), channel_id=1, source_target_pairs={{0,1},{1,0},{2,3},{3,2},{4,5},{5,4},{6,7},{7,6},{8,9},{9,8},{10,11... | collective-permute-start | bytes 1572872 | tf_op jit(solution)/shard_map/ppermute | solution.py:397
  71.1 30.7 %collective-permute-done.4.c0 = bf16[512,512]{1,0:T(8,128)(2,1)S(1)} collective-permute-done((bf16[512,512]{1,0:T(8,128)(2,1)S(1)}, bf16[512,512]{1,0:T(8,128)(2,1)S(1)}, u32[]{:S(2)}, u32[]{:S(2)}) %collective-permute-start.4) | collective-permute-done | bytes 524320 | tf_op jit(solution)/shard_map/ppermute | solution.py:397
  101.8 0.4 collective-permute-start.5
  102.2 4.4 %shard_map.113.r_ref = f32[512,1024]{1,0:T(8,128)} custom-call(s32[1]{0:T(128)} %bitcast.11.part, bf16[512,512]{1,0:T(8,128)(2,1)} %copy-done.2, bf16[512,512]{1,0:T(8,128)(2,1)} %collective-permute-done.8.c1, bf16[512,4096]{1,0:T(8,128)(2,1)} %w0.1, bf16[512,1024]{1,0:T(8,128)(2,1)} %collective-permute-done.9.w1, bf16[512,1024]{1,0:T(8,128)(2,1)} %r_ref.1), custom_call_target="tpu_custom_call" | custom-call | tf_op jit(solution)/shard_map/pallas_call | solution.py:377
  106.7 1.0 copy-done.3
  107.7 0.3 copy-done.4
  108.0 4.4 %shard_map.114 = bf16[512,1024]{1,0:T(8,128)(2,1)} custom-call(s32[1]{0:T(128)} %bitcast.11.part, bf16[512,512]{1,0:T(8,128)(2,1)} %copy-done.5, bf16[512,512]{1,0:T(8,128)(2,1)} %collective-permute-done.5.c1, bf16[512,1024]{1,0:T(8,128)(2,1)} %copy-done.3, bf16[512,1024]{1,0:T(8,128)(2,1)} %copy-done.4, f32[512,1024]{1,0:T(8,128)} %shard_map.113.r_ref), custom_call_target="tpu_custom_call" | custom-call | tf_op jit(solution)/shard_map/pallas_call | solution.py:377
  (18 shorter events, 0.0 us)
Async XLA Ops:
  3.4 24.7 %collective-permute-start = (bf16[1024,512]{1,0:T(8,128)(2,1)}, bf16[1024,512]{1,0:T(8,128)(2,1)S(1)}, u32[]{:S(2)}, u32[]{:S(2)}) collective-permute-start(bf16[1024,512]{1,0:T(8,128)(2,1)} %get-tuple-element.12), channel_id=1, source_target_pairs={{0,4},{4,0},{8,12},{12,8},{16,20},{20,16},{24,28},{28,24},{32,36},... | collective-permute-start | bytes 3145736 | tf_op jit(solution)/shard_map/ppermute | solution.py:393
  5.1 29.5 %collective-permute-start.1 = (bf16[1024,512]{1,0:T(8,128)(2,1)}, bf16[1024,512]{1,0:T(8,128)(2,1)S(1)}, u32[]{:S(2)}, u32[]{:S(2)}) collective-permute-start(bf16[1024,512]{1,0:T(8,128)(2,1)} %get-tuple-element.13), channel_id=1, source_target_pairs={{4,8},{8,4},{12,16},{16,12},{20,24},{24,20},{28,32},{32,28},{36,40... | collective-permute-start | bytes 3145736 | tf_op jit(solution)/shard_map/ppermute | solution.py:393
  28.1 6.5 %copy-start = (bf16[1024,512]{1,0:T(8,128)(2,1)}, bf16[1024,512]{1,0:T(8,128)(2,1)S(1)}, u32[]{:S(2)}) copy-start(bf16[1024,512]{1,0:T(8,128)(2,1)S(1)} %collective-permute-done) | copy-start | bytes 3145732
  34.6 1.0 copy-start.1
  45.5 21.2 %collective-permute-start.2 = (bf16[512,512]{1,0:T(8,128)(2,1)}, bf16[512,512]{1,0:T(8,128)(2,1)S(1)}, u32[]{:S(2)}, u32[]{:S(2)}) collective-permute-start(bf16[512,512]{1,0:T(8,128)(2,1)} %bitcast.40), channel_id=1, source_target_pairs={{0,4},{4,0},{8,12},{12,8},{16,20},{20,16},{24,28},{28,24},{32,36},... | collective-permute-start | bytes 1572872 | tf_op jit(solution)/shard_map/ppermute | solution.py:393
  45.6 21.1 %collective-permute-start.3 = (bf16[512,512]{1,0:T(8,128)(2,1)}, bf16[512,512]{1,0:T(8,128)(2,1)S(1)}, u32[]{:S(2)}, u32[]{:S(2)}) collective-permute-start(bf16[512,512]{1,0:T(8,128)(2,1)} %bitcast.39), channel_id=1, source_target_pairs={{4,8},{8,4},{12,16},{16,12},{20,24},{24,20},{28,32},{32,28},{36,40... | collective-permute-start | bytes 1572872 | tf_op jit(solution)/shard_map/ppermute | solution.py:393
  56.5 45.7 %collective-permute-start.9 = (bf16[512,1024]{1,0:T(8,128)(2,1)}, bf16[512,1024]{1,0:T(8,128)(2,1)}, u32[]{:S(2)}, u32[]{:S(2)}) collective-permute-start(bf16[512,1024]{1,0:T(8,128)(2,1)} %get-tuple-element.21), channel_id=1, source_target_pairs={{0,1},{1,0},{2,3},{3,2},{4,5},{5,4},{6,7},{7,6},{8,9},{9,8},{10,11... | collective-permute-start | bytes 3145736 | tf_op jit(solution)/shard_map/ppermute | solution.py:397
  58.7 48.0 %collective-permute-start.6 = (bf16[512,1024]{1,0:T(8,128)(2,1)}, bf16[512,1024]{1,0:T(8,128)(2,1)S(1)}, u32[]{:S(2)}, u32[]{:S(2)}) collective-permute-start(bf16[512,1024]{1,0:T(8,128)(2,1)} %get-tuple-element.19), channel_id=1, source_target_pairs={{0,2},{1,3},{2,0},{3,1},{4,6},{5,7},{6,4},{7,5},{8,10},{9,11},{10,... | collective-permute-start | bytes 3145736 | tf_op jit(solution)/shard_map/ppermute | solution.py:397
  60.5 46.2 %collective-permute-start.7 = (bf16[512,1024]{1,0:T(8,128)(2,1)}, bf16[512,1024]{1,0:T(8,128)(2,1)S(1)}, u32[]{:S(2)}, u32[]{:S(2)}) collective-permute-start(bf16[512,1024]{1,0:T(8,128)(2,1)} %get-tuple-element.20), channel_id=1, source_target_pairs={{0,35},{1,34},{2,33},{3,32},{4,39},{5,38},{6,37},{7,36},{8,43},{9,... | collective-permute-start | bytes 3145736 | tf_op jit(solution)/shard_map/ppermute | solution.py:406
  66.8 0.8 copy-start.6
  68.8 33.4 %copy-start.2 = (bf16[512,512]{1,0:T(8,128)(2,1)}, bf16[512,512]{1,0:T(8,128)(2,1)S(1)}, u32[]{:S(2)}) copy-start(bf16[512,512]{1,0:T(8,128)(2,1)S(1)} %fusion.c0) | copy-start | bytes 1572868
  68.8 32.9 %collective-permute-start.4 = (bf16[512,512]{1,0:T(8,128)(2,1)S(1)}, bf16[512,512]{1,0:T(8,128)(2,1)S(1)}, u32[]{:S(2)}, u32[]{:S(2)}) collective-permute-start(bf16[512,512]{1,0:T(8,128)(2,1)S(1)} %fusion.c0), channel_id=1, source_target_pairs={{0,2},{1,3},{2,0},{3,1},{4,6},{5,7},{6,4},{7,5},{8,10},{9,11},{10,... | collective-permute-start | bytes 1572872 | tf_op jit(solution)/shard_map/ppermute | solution.py:397
  68.9 33.3 %collective-permute-start.8 = (bf16[512,512]{1,0:T(8,128)(2,1)S(1)}, bf16[512,512]{1,0:T(8,128)(2,1)}, u32[]{:S(2)}, u32[]{:S(2)}) collective-permute-start(bf16[512,512]{1,0:T(8,128)(2,1)S(1)} %fusion.c0), channel_id=1, source_target_pairs={{0,1},{1,0},{2,3},{3,2},{4,5},{5,4},{6,7},{7,6},{8,9},{9,8},{10,11... | collective-permute-start | bytes 1572872 | tf_op jit(solution)/shard_map/ppermute | solution.py:397
  101.8 4.9 %copy-start.5 = (bf16[512,512]{1,0:T(8,128)(2,1)}, bf16[512,512]{1,0:T(8,128)(2,1)S(1)}, u32[]{:S(2)}) copy-start(bf16[512,512]{1,0:T(8,128)(2,1)S(1)} %collective-permute-done.4.c0) | copy-start | bytes 1572868
  101.8 4.9 %collective-permute-start.5 = (bf16[512,512]{1,0:T(8,128)(2,1)S(1)}, bf16[512,512]{1,0:T(8,128)(2,1)}, u32[]{:S(2)}, u32[]{:S(2)}) collective-permute-start(bf16[512,512]{1,0:T(8,128)(2,1)S(1)} %collective-permute-done.4.c0), channel_id=1, source_target_pairs={{0,1},{1,0},{2,3},{3,2},{4,5},{5,4},{6,7},{7,6},{8,9},{9,8},{10,11... | collective-permute-start | bytes 1572872 | tf_op jit(solution)/shard_map/ppermute | solution.py:397
  106.7 1.0 copy-start.3
  106.7 1.3 %copy-start.4 = (bf16[512,1024]{1,0:T(8,128)(2,1)}, bf16[512,1024]{1,0:T(8,128)(2,1)S(1)}, u32[]{:S(2)}) copy-start(bf16[512,1024]{1,0:T(8,128)(2,1)S(1)} %collective-permute-done.7.w1) | copy-start | bytes 3145732

commit v4 on v3

v4 whole, which is shorter than its diff:
```python
import jax
import jax.numpy as jnp
from jax import lax
from jax.experimental import pallas as pl
from jax.experimental.pallas import tpu as pltpu
from jax.sharding import Mesh
from jax.sharding import PartitionSpec as P


HD = 64
BLK = 128
REACH = 2
SLOTS = 4
CROSS = 2
QUAD = 4
Z_CHIPS = 8
QW = HD * QUAD
HEAD = ("head_0", "head_1")
EXP_SCALE = 0.125 * 1.4426950408889634


def attend(q_ref, k_refs, v_refs, o_ref):
    quads = [pl.ds(c * QW, QW) for c in range(q_ref.shape[-1] // QW)]
    lane = lax.broadcasted_iota(jnp.int32, (BLK, QW), 1) // HD
    scores = []
    for cols in quads:
        q = q_ref[:, cols]
        zero = jnp.zeros_like(q)
        rows = jnp.concatenate([jnp.where(lane == h, q, zero) for h in range(QUAD)], axis=0)
        k = jnp.concatenate([r[:, cols] for r in k_refs], axis=0)
        scores.append(
            lax.dot_general(rows, k, (((1,), (1,)), ((), ())), preferred_element_type=jnp.float32)
        )
    for cols, s in zip(quads, scores):
        m = jnp.max(s, axis=1, keepdims=True)
        p = jnp.exp2((s - m) * EXP_SCALE)
        l = jnp.sum(p, axis=1, keepdims=True)
        v = jnp.concatenate([r[:, cols] for r in v_refs], axis=0)
        o = lax.dot_general(
            p.astype(jnp.bfloat16), v, (((1,), (0,)), ((), ())), preferred_element_type=jnp.float32
        )
        o = o * (1.0 / l)
        out = o[:BLK]
        for h in range(1, QUAD):
            out = jnp.where(lane == h, o[h * BLK : (h + 1) * BLK], out)
        o_ref[:, cols] = out.astype(jnp.bfloat16)


def send_kernel(pos, k, v, beside, beyond, s0, s1, s2, s3, load_sem, store_sem):
    halo = REACH * BLK
    tail = pl.ds(k.shape[0] - halo, halo)
    head = pl.ds(0, halo)
    values = pl.ds(halo, halo)
    sources = ((k.at[tail], s0), (v.at[tail], s1), (k.at[head], s2), (v.at[head], s3))
    loads = [pltpu.make_async_copy(x, y, load_sem) for x, y in sources]
    for load in loads:
        load.start()
    for load in loads:
        load.wait()

    def stores(up, down):
        pairs = ((s0, up.at[head]), (s1, up.at[values]), (s2, down.at[head]), (s3, down.at[values]))
        return [pltpu.make_async_copy(a, b, store_sem) for a, b in pairs]

    even = pos[0] % 2 == 0

    @pl.when(even)
    def _():
        for store in stores(beside, beyond):
            store.start()

    @pl.when(jnp.logical_not(even))
    def _():
        for store in stores(beyond, beside):
            store.start()

    for store in stores(beside, beyond):
        store.wait()


def send_call(position, k, v):
    halo = REACH * BLK
    width = k.shape[1]
    shape = jax.ShapeDtypeStruct((2 * halo, width), k.dtype)
    hbm = pl.BlockSpec(memory_space=pl.ANY)
    return pl.pallas_call(
        send_kernel,
        in_specs=[pl.BlockSpec(memory_space=pltpu.SMEM)] + [hbm] * 2,
        out_specs=[hbm] * 2,
        out_shape=[shape] * 2,
        scratch_shapes=[pltpu.VMEM((halo, width), k.dtype)] * 4
        + [pltpu.SemaphoreType.DMA, pltpu.SemaphoreType.DMA],
        name="pack_edges",
    )(position, k, v)


def encoder_kernel(
    pos, counts, lists, q, k, v, beside, beyond, e, kb, vb, qb, eb, edge_sem, k_sem, v_sem, q_sem, e_sem
):
    blocks = k.shape[0]
    even = pos[0] % 2 == 0
    base = pos[0] * blocks - REACH

    def edges(up, down):
        pairs = (
            (up.at[pl.ds(0, REACH)], kb.at[pl.ds(0, REACH)]),
            (up.at[pl.ds(REACH, REACH)], vb.at[pl.ds(0, REACH)]),
            (down.at[pl.ds(0, REACH)], kb.at[pl.ds(REACH + blocks, REACH)]),
            (down.at[pl.ds(REACH, REACH)], vb.at[pl.ds(REACH + blocks, REACH)]),
        )
        return [pltpu.make_async_copy(a, b, edge_sem) for a, b in pairs]

    def keys(i):
        return pltpu.make_async_copy(k.at[i], kb.at[REACH + i], k_sem.at[i])

    def values(i):
        return pltpu.make_async_copy(v.at[i], vb.at[REACH + i], v_sem.at[i])

    def queries(i):
        return pltpu.make_async_copy(q.at[i], qb.at[i], q_sem.at[i])

    def result(i):
        return pltpu.make_async_copy(eb.at[i], e.at[i], e_sem)

    @pl.when(even)
    def _():
        for copy in edges(beyond, beside):
            copy.start()

    @pl.when(jnp.logical_not(even))
    def _():
        for copy in edges(beside, beyond):
            copy.start()

    for i in range(blocks):
        keys(i).start()
        values(i).start()
        queries(i).start()
    for copy in edges(beyond, beside):
        copy.wait()
    for i in range(REACH):
        keys(i).wait()
        values(i).wait()

    @pl.loop(0, blocks)
    def _(b):
        @pl.when(b + REACH < blocks)
        def _():
            keys(b + REACH).wait()
            values(b + REACH).wait()

        queries(b).wait()
        count = counts[b]
        ids = [lists[j, b] - base for j in range(SLOTS)]
        for n in range(1, SLOTS + 1):

            @pl.when(count == n)
            def _(n=n):
                attend(
                    qb.at[b], [kb.at[i] for i in ids[:n]], [vb.at[i] for i in ids[:n]], eb.at[b]
                )

        result(b).start()

    for i in range(blocks):
        result(i).wait()


def encoder_call(position, counts, lists, q, k3, v3, beside, beyond):
    blocks, _, width = k3.shape
    smem = pl.BlockSpec(memory_space=pltpu.SMEM)
    hbm = pl.BlockSpec(memory_space=pl.ANY)
    vmem = pl.BlockSpec(memory_space=pltpu.VMEM)

    def room(n):
        return pltpu.VMEM((n, BLK, width), jnp.bfloat16)

    return pl.pallas_call(
        encoder_kernel,
        in_specs=[smem] * 3 + [hbm] * 3 + [vmem] * 2,
        out_specs=hbm,
        out_shape=jax.ShapeDtypeStruct(k3.shape, jnp.bfloat16),
        scratch_shapes=[
            room(blocks + 2 * REACH),
            room(blocks + 2 * REACH),
            room(blocks),
            room(blocks),
            pltpu.SemaphoreType.DMA,
            pltpu.SemaphoreType.DMA((blocks,)),
            pltpu.SemaphoreType.DMA((blocks,)),
            pltpu.SemaphoreType.DMA((blocks,)),
            pltpu.SemaphoreType.DMA,
        ],
        name="encoder",
    )(position, counts, lists, cut(q), k3, v3, in_vmem(cut(beside)), in_vmem(cut(beyond)))


def serve_kernel(pos, owners, slots, k, e, *refs):
    sources = (len(refs) - 6) // 2
    queries = refs[:sources]
    answers = refs[sources : 2 * sources]
    kb, eb, qb, ob, load_sems, answer_sem = refs[2 * sources :]
    mine = pos[0]
    per = queries[0].shape[0]
    total = owners.shape[0] // per
    ahead = jnp.where(mine % 2 == 0, 1, -1)
    shifts = (0,) if sources == 1 else (ahead, -ahead)

    def candidate(i, t):
        source = mine + shifts[i]
        d = jnp.clip(source, 0, total - 1) * per + t
        live = (source >= 0) & (source < total) & (owners[d] == mine)
        return live, slots[0, d], slots[1, d]

    def loads(i, t, s0, s1):
        n = i * per + t
        sem = load_sems.at[n]
        return [
            pltpu.make_async_copy(a, b, sem)
            for a, b in (
                (queries[i].at[t], qb.at[n]),
                (k.at[s0], kb.at[n, 0]),
                (k.at[s1], kb.at[n, 1]),
                (e.at[s0], eb.at[n, 0]),
                (e.at[s1], eb.at[n, 1]),
            )
        ]

    for i in range(sources):
        for t in range(per):
            live, s0, s1 = candidate(i, t)

            @pl.when(live)
            def _(i=i, t=t, s0=s0, s1=s1):
                for copy in loads(i, t, s0, s1):
                    copy.start()

    for i in range(sources):

        @pl.loop(0, per)
        def _(t, i=i):
            live, s0, s1 = candidate(i, t)
            n = i * per + t

            @pl.when(live)
            def _():
                for copy in loads(i, t, s0, s1):
                    copy.wait()
                attend(
                    qb.at[n],
                    [kb.at[n, j] for j in range(CROSS)],
                    [eb.at[n, j] for j in range(CROSS)],
                    ob.at[n],
                )

            @pl.when(jnp.logical_not(live))
            def _():
                ob[n] = jnp.zeros(ob.shape[1:], ob.dtype)

        pltpu.make_async_copy(ob.at[pl.ds(i * per, per)], answers[i], answer_sem).start()

    for i in range(sources):
        pltpu.make_async_copy(ob.at[pl.ds(i * per, per)], answers[i], answer_sem).wait()


def serve_call(position, owners, slots, k3, e3, queries):
    width = k3.shape[-1]
    sources = len(queries)
    queries = [cut(x) for x in queries]
    per = queries[0].shape[0]
    smem = pl.BlockSpec(memory_space=pltpu.SMEM)
    hbm = pl.BlockSpec(memory_space=pl.ANY)
    vmem = pl.BlockSpec(memory_space=pltpu.VMEM)
    served = per * sources
    if sources > 1:
        queries = [in_vmem(x) for x in queries]
    out = pl.pallas_call(
        serve_kernel,
        in_specs=[smem] * 3 + [hbm] * 2 + [vmem if sources > 1 else hbm] * sources,
        out_specs=[hbm] * sources,
        out_shape=[jax.ShapeDtypeStruct((per, BLK, width), jnp.bfloat16)] * sources,
        scratch_shapes=[
            pltpu.VMEM((served, CROSS, BLK, width), jnp.bfloat16),
            pltpu.VMEM((served, CROSS, BLK, width), jnp.bfloat16),
            pltpu.VMEM((served, BLK, width), jnp.bfloat16),
            pltpu.VMEM((served, BLK, width), jnp.bfloat16),
            pltpu.SemaphoreType.DMA((served,)),
            pltpu.SemaphoreType.DMA,
        ],
    )(position, owners, slots, k3, e3, *queries)
    return [x.reshape(per * BLK, width) for x in out]


def cut(x):
    return x.reshape(-1, BLK, x.shape[-1])


def in_vmem(x):
    return pltpu.with_memory_space_constraint(x, pltpu.VMEM)


def move(plan, stages, load_sem, store_sem):
    loads = [pltpu.make_async_copy(src, stages[i], load_sem.at[i]) for i, (src, _) in enumerate(plan)]
    stores = [pltpu.make_async_copy(stages[i], dst, store_sem) for i, (_, dst) in enumerate(plan)]
    for load in loads:
        load.start()
    for load, store in zip(loads, stores):
        load.wait()
        store.start()
    for store in stores:
        store.wait()


def cut_kernel(part, w, a, b, c, sa, sb, sc, load_sem, store_sem):
    columns = a.shape[1]
    plan = []
    for flip, dst in ((2, a), (3, b), (1, c)):
        start = pl.multiple_of((part[0] ^ flip) * columns, columns)
        plan.append((w.at[:, pl.ds(start, columns)], dst))
    move(plan, (sa, sb, sc), load_sem, store_sem)


def cut_call(part, w, columns):
    shape = jax.ShapeDtypeStruct((w.shape[0], columns), w.dtype)
    hbm = pl.BlockSpec(memory_space=pl.ANY)
    return pl.pallas_call(
        cut_kernel,
        in_specs=[pl.BlockSpec(memory_space=pltpu.SMEM), hbm],
        out_specs=[hbm] * 3,
        out_shape=[shape] * 3,
        scratch_shapes=[pltpu.VMEM(shape.shape, w.dtype)] * 3
        + [pltpu.SemaphoreType.DMA((3,)), pltpu.SemaphoreType.DMA],
        name="cut_weight",
    )(part, w)


def project_kernel(part, c0, c1, w0, w1, r_ref, o_ref):
    total = r_ref[...].astype(jnp.float32)
    for c, w in ((c0, w0), (c1, w1)):
        total = total + jnp.dot(c[...], w[...], preferred_element_type=jnp.float32)
    o_ref[...] = total.astype(o_ref.dtype)


def project_call(part, contexts, weights, added, dtype):
    tokens, width = contexts[0].shape
    columns = added.shape[1]
    tile = min(tokens, 256)
    c_spec = pl.BlockSpec((tile, width), lambda i, p: (i, 0))
    w_specs = [
        pl.BlockSpec((width, columns), lambda i, p: (0, p[0]))
        if w.shape[1] > columns
        else pl.BlockSpec((width, columns), lambda i, p: (0, 0))
        for w in weights
    ]
    r_spec = pl.BlockSpec((tile, columns), lambda i, p: (i, 0))
    return pl.pallas_call(
        project_kernel,
        grid_spec=pltpu.PrefetchScalarGridSpec(
            num_scalar_prefetch=1,
            grid=(tokens // tile,),
            in_specs=[c_spec] * 2 + w_specs + [r_spec],
            out_specs=r_spec,
        ),
        out_shape=jax.ShapeDtypeStruct(added.shape, dtype),
    )(part, *[in_vmem(c) for c in contexts], *weights, added)


def exchanged(block, first):
    route = []
    for i in range(first, lax.axis_size("seq") - 1, 2):
        route += [(i, i + 1), (i + 1, i)]
    return lax.ppermute(block, "seq", route)


def swapped(block, flip):
    return lax.ppermute(block, HEAD, [(i, i ^ flip) for i in range(4)])


def other_side(block, flip):
    axes = ("seq", *HEAD)
    route = []
    for s in range(lax.axis_size("seq")):
        for h in range(4):
            route.append((s * 4 + h, (s ^ Z_CHIPS) * 4 + (h ^ flip)))
    return lax.ppermute(block, axes, route)


def body(
    encoder_queries,
    encoder_keys,
    encoder_values,
    block_lists,
    block_counts,
    decoder_queries,
    span_owner,
    cross_slots,
    out_weight,
    decoder_input,
):
    position = lax.axis_index("seq").astype(jnp.int32).reshape(1)
    part = lax.axis_index(HEAD).astype(jnp.int32).reshape(1)
    blocks = encoder_queries.shape[0] // BLK
    width = encoder_queries.shape[1]
    columns = decoder_input.shape[1]
    lists = block_lists.T
    slots = cross_slots.T
    k3 = cut(encoder_keys)
    v3 = cut(encoder_values)
    beside, beyond = send_call(position, encoder_keys, encoder_values)
    beside = exchanged(beside, 0)
    beyond = exchanged(beyond, 1)
    q_beside = exchanged(decoder_queries, 0)
    q_beyond = exchanged(decoder_queries, 1)
    across2, across3, across1 = cut_call(part, out_weight, columns)
    w2 = swapped(across2, 2)
    w3 = other_side(across3, 3)
    w1 = swapped(across1, 1)
    e3 = encoder_call(position, block_counts, lists, encoder_queries, k3, v3, beside, beyond)
    tables = (position, span_owner, slots, k3, e3)
    (own,) = serve_call(*tables, [decoder_queries])
    for_beside, for_beyond = serve_call(*tables, [q_beside, q_beyond])
    from_beside = exchanged(for_beside, 0)
    from_beyond = exchanged(for_beyond, 1)
    context = own + from_beside + from_beyond
    across = swapped(context, 2)
    beside = swapped(context, 1)
    corner = swapped(across, 1)
    total = project_call(part, [context, beside], [out_weight, w1], decoder_input, jnp.float32)
    decoder_out = project_call(part, [across, corner], [w2, w3], total, jnp.bfloat16)
    return (e3.reshape(blocks * BLK, width), decoder_out)


def solution(mesh):
    split = Mesh(mesh.devices.reshape(mesh.shape["seq"], 2, 2), ("seq", "head_0", "head_1"))
    placed = (
        P("seq", HEAD),
        P("seq", HEAD),
        P("seq", HEAD),
        P("seq", None),
        P("seq"),
        P("seq", HEAD),
        P(),
        P(),
        P(HEAD, None),
        P("seq", HEAD),
    )
    return jax.shard_map(
        body,
        mesh=split,
        in_specs=placed,
        out_specs=(P("seq", HEAD), P("seq", HEAD)),
        check_vma=False,
    )
```

time: 113 us -> 106 us (0.938)
  Pallas kernels: 41.7 us -> 32.1 us
  starting transfers between devices: 23 us -> 30.7 us
  local copies, waits for them, and re-layouts: 3.05 us -> 0.01 us
  waiting for transfers between devices: 42.5 us -> 40.6 us
    pallas_call x3, Pallas kernels: 27.3 us -> 18.6 us  [the longest x1 11.6 us: encoder_call(): pl.pallas_call(encoder_kernel, in_specs=[smem] * 3 + [hbm] * 3 + [vmem] *...]
    ppermute x4 -> x6, waiting for transfers between devices: 11.8 us -> 8.27 us  [exchanged(): return lax.ppermute(block, 'seq', route)]
    ppermute x4 -> x6, starting transfers between devices: 16.3 us -> 19.6 us  [exchanged(): return lax.ppermute(block, 'seq', route)]
    ppermute x5, starting transfers between devices: 6.69 us -> 9.88 us  [swapped(): return lax.ppermute(block, HEAD, [(i, i ^ flip) for i in range(4)])]
    unnamed x14 -> x2, local copies, waits for them, and re-layouts: 3.05 us -> 0.01 us
    ppermute x5, waiting for transfers between devices: 30.7 us -> 32.3 us  [swapped(): return lax.ppermute(block, HEAD, [(i, i ^ flip) for i in range(4)])]
    ppermute x1, starting transfers between devices: 0.01 us -> 1.22 us  [other_side(): return lax.ppermute(block, axes, route)]
  transfers between devices with their start and end apart: 10 -> 12, of which waited for: 3 -> 3; matrix products, arithmetic and copies ran while one was open for 1% -> 1% of each run, Pallas kernels for 22% -> 19%
where the time goes in v4:
time: 106 us; the launch traced here: 105 us
  waiting for transfers between devices  40.6 us (38%)
  Pallas kernels  32.1 us (30%)
  starting transfers between devices  30.7 us (29%)
  other arithmetic  1.12 us (1%)
    ppermute x5, waiting for transfers between devices, swapped(): return lax.ppermute(block, HEAD, [(i, i ^ flip) for i in range(4)])  32.3 us
    ppermute x6, starting transfers between devices, exchanged(): return lax.ppermute(block, 'seq', route)  19.6 us
    pallas_call x1, Pallas kernels, encoder_call(): pl.pallas_call(encoder_kernel, in_specs=[smem] * 3 + [hbm] * 3 + [vmem] *...  11.6 us
    ppermute x5, starting transfers between devices, swapped(): return lax.ppermute(block, HEAD, [(i, i ^ flip) for i in range(4)])  9.88 us
    pallas_call x2, Pallas kernels, project_call(): pl.pallas_call(project_kernel, grid_spec=pltpu.PrefetchScalarGridSpec(num...  8.28 us
    ppermute x6, waiting for transfers between devices, exchanged(): return lax.ppermute(block, 'seq', route)  8.27 us
    pallas_call x2, Pallas kernels, serve_call(): pl.pallas_call(serve_kernel, in_specs=[smem] * 3 + [hbm] * 2 + [vmem if s...  7.08 us
    pallas_call x1, Pallas kernels, cut_call(): pl.pallas_call(cut_kernel, in_specs=[pl.BlockSpec(memory_space=pltpu.SMEM...  2.93 us
  transfers between devices with their start and end apart: 12, of which 3 were waited for; matrix products, arithmetic and copies ran while one was open for 1% of the time, Pallas kernels for 19%

profile of v4, /device:TPU:21, one launch (start us, length us, event | category | flops | bytes accessed | tf_op | source)
XLA Modules:
  0.0 105.3 jit_solution(8785119987830837764)
XLA Ops:
  0.6 0.0 copy-start
  0.6 2.2 %pack_edges.1 = (bf16[512,512]{1,0:T(8,128)(2,1)}, bf16[512,512]{1,0:T(8,128)(2,1)}) custom-call(s32[1]{0:T(128)} %bitcast.pos, bf16[1536,512]{1,0:T(8,128)(2,1)} %k.1, bf16[1536,512]{1,0:T(8,128)(2,1)} %v.1), custom_call_target="tpu_custom_call" | custom-call | tf_op jit(solution)/shard_map/pack_edges/pallas_call | solution.py:86
  2.9 1.7 %collective-permute-start = (bf16[512,512]{1,0:T(8,128)(2,1)}, bf16[512,512]{1,0:T(8,128)(2,1)S(1)}, u32[]{:S(2)}, u32[]{:S(2)}) collective-permute-start(bf16[512,512]{1,0:T(8,128)(2,1)} %get-tuple-element.9), channel_id=1, source_target_pairs={{0,4},{4,0},{8,12},{12,8},{16,20},{20,16},{24,28},{28,24},{32,36},... | collective-permute-start | bytes 1572872 | tf_op jit(solution)/shard_map/ppermute | solution.py:372
  4.6 6.5 %collective-permute-start.1 = (bf16[512,512]{1,0:T(8,128)(2,1)}, bf16[512,512]{1,0:T(8,128)(2,1)S(1)}, u32[]{:S(2)}, u32[]{:S(2)}) collective-permute-start(bf16[512,512]{1,0:T(8,128)(2,1)} %get-tuple-element.10), channel_id=1, source_target_pairs={{4,8},{8,4},{12,16},{16,12},{20,24},{24,20},{28,32},{32,28},{36,40... | collective-permute-start | bytes 1572872 | tf_op jit(solution)/shard_map/ppermute | solution.py:372
  11.1 0.1 collective-permute-start.2
  11.2 3.3 %collective-permute-start.3 = (bf16[512,512]{1,0:T(8,128)(2,1)S(1)}, bf16[512,512]{1,0:T(8,128)(2,1)S(1)}, u32[]{:S(2)}, u32[]{:S(2)}) collective-permute-start(bf16[512,512]{1,0:T(8,128)(2,1)S(1)} %copy-done), channel_id=1, source_target_pairs={{4,8},{8,4},{12,16},{16,12},{20,24},{24,20},{28,32},{32,28},{36,40... | collective-permute-start | bytes 1572872 | tf_op jit(solution)/shard_map/ppermute | solution.py:372
  14.6 1.8 %collective-permute-done = bf16[512,512]{1,0:T(8,128)(2,1)S(1)} collective-permute-done((bf16[512,512]{1,0:T(8,128)(2,1)}, bf16[512,512]{1,0:T(8,128)(2,1)S(1)}, u32[]{:S(2)}, u32[]{:S(2)}) %collective-permute-start) | collective-permute-done | bytes 524320 | tf_op jit(solution)/shard_map/ppermute | solution.py:372
  16.3 6.5 %collective-permute-done.1 = bf16[512,512]{1,0:T(8,128)(2,1)S(1)} collective-permute-done((bf16[512,512]{1,0:T(8,128)(2,1)}, bf16[512,512]{1,0:T(8,128)(2,1)S(1)}, u32[]{:S(2)}, u32[]{:S(2)}) %collective-permute-start.1) | collective-permute-done | bytes 524320 | tf_op jit(solution)/shard_map/ppermute | solution.py:372
  22.8 11.6 %encoder.1.e = bf16[12,128,512]{2,1,0:T(8,128)(2,1)} custom-call(s32[1]{0:T(128)} %bitcast.pos, s32[12]{0:T(128)} %counts.1, s32[4,12]{1,0:T(4,128)} %bitcast.32, bf16[12,128,512]{2,1,0:T(8,128)(2,1)} %bitcast.28, bf16[12,128,512]{2,1,0:T(8,128)(2,1)} %bitcast.23, bf16[12,128,512]{2,1,0:T(8,128)(2,1)} %bitcast.27, bf16[4,128,512]{2,1,0:T(8,128)(2,1)S(1)} %bitcast.20, ...), custom_call_target="tpu_custom_call" | custom-call | tf_op jit(solution)/shard_map/encoder/pallas_call | solution.py:178
  34.4 5.4 %shard_map.114 = (bf16[4,128,512]{2,1,0:T(8,128)(2,1)}, bf16[4,128,512]{2,1,0:T(8,128)(2,1)}) custom-call(s32[1]{0:T(128)} %bitcast.pos, s32[256]{0:T(256)} %owners.3, s32[2,256]{1,0:T(2,128)} %bitcast.30, bf16[12,128,512]{2,1,0:T(8,128)(2,1)} %bitcast.24, bf16[12,128,512]{2,1,0:T(8,128)(2,1)} %encoder.1.e, bf16[4,128,512]{2,1,0:T(8,128)(2,1)S(1)} %bitcast.19, ...), custom_call_target="tpu_custom_call" | custom-call | tf_op jit(solution)/shard_map/pallas_call | solution.py:277
  39.8 0.1 collective-permute-start.4
  39.9 7.8 %collective-permute-start.5 = (bf16[512,512]{1,0:T(8,128)(2,1)}, bf16[512,512]{1,0:T(8,128)(2,1)S(1)}, u32[]{:S(2)}, u32[]{:S(2)}) collective-permute-start(bf16[512,512]{1,0:T(8,128)(2,1)} %bitcast.33), channel_id=1, source_target_pairs={{4,8},{8,4},{12,16},{16,12},{20,24},{24,20},{28,32},{32,28},{36,40... | collective-permute-start | bytes 1572872 | tf_op jit(solution)/shard_map/ppermute | solution.py:372
  47.8 2.9 %cut_weight.1 = (bf16[512,1024]{1,0:T(8,128)(2,1)}, bf16[512,1024]{1,0:T(8,128)(2,1)}, bf16[512,1024]{1,0:T(8,128)(2,1)}) custom-call(s32[1]{0:T(128)} %bitcast.8.part, bf16[512,4096]{1,0:T(8,128)(2,1)} %w0.1), custom_call_target="tpu_custom_call" | custom-call | tf_op jit(solution)/shard_map/cut_weight/pallas_call | solution.py:326
  50.7 3.6 %collective-permute-start.11 = (bf16[512,1024]{1,0:T(8,128)(2,1)}, bf16[512,1024]{1,0:T(8,128)(2,1)}, u32[]{:S(2)}, u32[]{:S(2)}) collective-permute-start(bf16[512,1024]{1,0:T(8,128)(2,1)} %get-tuple-element.15), channel_id=1, source_target_pairs={{0,1},{1,0},{2,3},{3,2},{4,5},{5,4},{6,7},{7,6},{8,9},{9,8},{10,11... | collective-permute-start | bytes 3145736 | tf_op jit(solution)/shard_map/ppermute | solution.py:376
  54.3 1.8 %collective-permute-start.8 = (bf16[512,1024]{1,0:T(8,128)(2,1)}, bf16[512,1024]{1,0:T(8,128)(2,1)}, u32[]{:S(2)}, u32[]{:S(2)}) collective-permute-start(bf16[512,1024]{1,0:T(8,128)(2,1)} %get-tuple-element.13), channel_id=1, source_target_pairs={{0,2},{1,3},{2,0},{3,1},{4,6},{5,7},{6,4},{7,5},{8,10},{9,11},{10,... | collective-permute-start | bytes 3145736 | tf_op jit(solution)/shard_map/ppermute | solution.py:376
  56.1 1.2 %collective-permute-start.9 = (bf16[512,1024]{1,0:T(8,128)(2,1)}, bf16[512,1024]{1,0:T(8,128)(2,1)}, u32[]{:S(2)}, u32[]{:S(2)}) collective-permute-start(bf16[512,1024]{1,0:T(8,128)(2,1)} %get-tuple-element.14), channel_id=1, source_target_pairs={{0,35},{1,34},{2,33},{3,32},{4,39},{5,38},{6,37},{7,36},{8,43},{9,... | collective-permute-start | bytes 3145736 | tf_op jit(solution)/shard_map/ppermute | solution.py:385
  57.3 1.7 %shard_map.113 = bf16[4,128,512]{2,1,0:T(8,128)(2,1)} custom-call(s32[1]{0:T(128)} %bitcast.pos, s32[256]{0:T(256)} %owners.3, s32[2,256]{1,0:T(2,128)} %bitcast.31, bf16[12,128,512]{2,1,0:T(8,128)(2,1)} %bitcast.25, bf16[12,128,512]{2,1,0:T(8,128)(2,1)} %encoder.1.e, bf16[4,128,512]{2,1,0:T(8,128)(2,1)} %bitcast.29), custom_call_target="tpu_custom_call" | custom-call | tf_op jit(solution)/shard_map/pallas_call | solution.py:277
  59.0 1.1 %fusion.c0 = bf16[512,512]{1,0:T(8,128)(2,1)S(1)} fusion(bf16[512,512]{1,0:T(8,128)(2,1)S(1)} %collective-permute-done.5, bf16[512,512]{1,0:T(8,128)(2,1)S(1)} %collective-permute-done.4, bf16[4,128,512]{2,1,0:T(8,128)(2,1)} %shard_map.113), kind=kLoop, calls=%fused_computation.1 | loop fusion | flops 524288 | bytes 2097152 | tf_op jit(solution)/shard_map/add | solution.py:424
  60.2 1.0 collective-permute-start.6
  61.2 3.1 %collective-permute-start.10 = (bf16[512,512]{1,0:T(8,128)(2,1)S(1)}, bf16[512,512]{1,0:T(8,128)(2,1)S(1)}, u32[]{:S(2)}, u32[]{:S(2)}) collective-permute-start(bf16[512,512]{1,0:T(8,128)(2,1)S(1)} %fusion.c0), channel_id=1, source_target_pairs={{0,1},{1,0},{2,3},{3,2},{4,5},{5,4},{6,7},{7,6},{8,9},{9,8},{10,11... | collective-permute-start | bytes 1572872 | tf_op jit(solution)/shard_map/ppermute | solution.py:376
  64.2 32.3 %collective-permute-done.6.c0 = bf16[512,512]{1,0:T(8,128)(2,1)S(1)} collective-permute-done((bf16[512,512]{1,0:T(8,128)(2,1)S(1)}, bf16[512,512]{1,0:T(8,128)(2,1)S(1)}, u32[]{:S(2)}, u32[]{:S(2)}) %collective-permute-start.6) | collective-permute-done | bytes 524320 | tf_op jit(solution)/shard_map/ppermute | solution.py:376
  96.6 0.4 collective-permute-start.7
  97.0 4.2 %shard_map.115.r_ref = f32[512,1024]{1,0:T(8,128)} custom-call(s32[1]{0:T(128)} %bitcast.8.part, bf16[512,512]{1,0:T(8,128)(2,1)S(1)} %fusion.c0, bf16[512,512]{1,0:T(8,128)(2,1)S(1)} %collective-permute-done.10.c1, bf16[512,4096]{1,0:T(8,128)(2,1)} %w0.1, bf16[512,1024]{1,0:T(8,128)(2,1)} %collective-permute-done.11.w1, bf16[512,1024]{1,0:T(8,128)(2,1)} %r_ref.1), custom_call_target="tpu_custom_call" | custom-call | tf_op jit(solution)/shard_map/pallas_call | solution.py:356
  101.2 4.1 %shard_map.116 = bf16[512,1024]{1,0:T(8,128)(2,1)} custom-call(s32[1]{0:T(128)} %bitcast.8.part, bf16[512,512]{1,0:T(8,128)(2,1)S(1)} %collective-permute-done.6.c0, bf16[512,512]{1,0:T(8,128)(2,1)S(1)} %collective-permute-done.7.c1, bf16[512,1024]{1,0:T(8,128)(2,1)} %collective-permute-done.8.w0, bf16[512,1024]{1,0:T(8,128)(2,1)} %collective-permute-done.9.w1, ...), custom_call_target="tpu_custom_call" | custom-call | tf_op jit(solution)/shard_map/pallas_call | solution.py:356
  (10 shorter events, 0.0 us)
Async XLA Ops:
  0.6 10.5 %copy-start = (bf16[512,512]{1,0:T(8,128)(2,1)S(1)}, bf16[512,512]{1,0:T(8,128)(2,1)}, u32[]{:S(2)}) copy-start(bf16[512,512]{1,0:T(8,128)(2,1)} %param.15) | copy-start | bytes 1572868
  2.9 13.5 %collective-permute-start = (bf16[512,512]{1,0:T(8,128)(2,1)}, bf16[512,512]{1,0:T(8,128)(2,1)S(1)}, u32[]{:S(2)}, u32[]{:S(2)}) collective-permute-start(bf16[512,512]{1,0:T(8,128)(2,1)} %get-tuple-element.9), channel_id=1, source_target_pairs={{0,4},{4,0},{8,12},{12,8},{16,20},{20,16},{24,28},{28,24},{32,36},... | collective-permute-start | bytes 1572872 | tf_op jit(solution)/shard_map/ppermute | solution.py:372
  4.6 18.2 %collective-permute-start.1 = (bf16[512,512]{1,0:T(8,128)(2,1)}, bf16[512,512]{1,0:T(8,128)(2,1)S(1)}, u32[]{:S(2)}, u32[]{:S(2)}) collective-permute-start(bf16[512,512]{1,0:T(8,128)(2,1)} %get-tuple-element.10), channel_id=1, source_target_pairs={{4,8},{8,4},{12,16},{16,12},{20,24},{24,20},{28,32},{32,28},{36,40... | collective-permute-start | bytes 1572872 | tf_op jit(solution)/shard_map/ppermute | solution.py:372
  11.1 23.3 %collective-permute-start.2 = (bf16[512,512]{1,0:T(8,128)(2,1)S(1)}, bf16[512,512]{1,0:T(8,128)(2,1)S(1)}, u32[]{:S(2)}, u32[]{:S(2)}) collective-permute-start(bf16[512,512]{1,0:T(8,128)(2,1)S(1)} %copy-done), channel_id=1, source_target_pairs={{0,4},{4,0},{8,12},{12,8},{16,20},{20,16},{24,28},{28,24},{32,36},... | collective-permute-start | bytes 1572872 | tf_op jit(solution)/shard_map/ppermute | solution.py:372
  11.2 23.2 %collective-permute-start.3 = (bf16[512,512]{1,0:T(8,128)(2,1)S(1)}, bf16[512,512]{1,0:T(8,128)(2,1)S(1)}, u32[]{:S(2)}, u32[]{:S(2)}) collective-permute-start(bf16[512,512]{1,0:T(8,128)(2,1)S(1)} %copy-done), channel_id=1, source_target_pairs={{4,8},{8,4},{12,16},{16,12},{20,24},{24,20},{28,32},{32,28},{36,40... | collective-permute-start | bytes 1572872 | tf_op jit(solution)/shard_map/ppermute | solution.py:372
  39.8 19.2 %collective-permute-start.4 = (bf16[512,512]{1,0:T(8,128)(2,1)}, bf16[512,512]{1,0:T(8,128)(2,1)S(1)}, u32[]{:S(2)}, u32[]{:S(2)}) collective-permute-start(bf16[512,512]{1,0:T(8,128)(2,1)} %bitcast.34), channel_id=1, source_target_pairs={{0,4},{4,0},{8,12},{12,8},{16,20},{20,16},{24,28},{28,24},{32,36},... | collective-permute-start | bytes 1572872 | tf_op jit(solution)/shard_map/ppermute | solution.py:372
  39.9 19.1 %collective-permute-start.5 = (bf16[512,512]{1,0:T(8,128)(2,1)}, bf16[512,512]{1,0:T(8,128)(2,1)S(1)}, u32[]{:S(2)}, u32[]{:S(2)}) collective-permute-start(bf16[512,512]{1,0:T(8,128)(2,1)} %bitcast.33), channel_id=1, source_target_pairs={{4,8},{8,4},{12,16},{16,12},{20,24},{24,20},{28,32},{32,28},{36,40... | collective-permute-start | bytes 1572872 | tf_op jit(solution)/shard_map/ppermute | solution.py:372
  50.7 46.3 %collective-permute-start.11 = (bf16[512,1024]{1,0:T(8,128)(2,1)}, bf16[512,1024]{1,0:T(8,128)(2,1)}, u32[]{:S(2)}, u32[]{:S(2)}) collective-permute-start(bf16[512,1024]{1,0:T(8,128)(2,1)} %get-tuple-element.15), channel_id=1, source_target_pairs={{0,1},{1,0},{2,3},{3,2},{4,5},{5,4},{6,7},{7,6},{8,9},{9,8},{10,11... | collective-permute-start | bytes 3145736 | tf_op jit(solution)/shard_map/ppermute | solution.py:376
  54.3 46.9 %collective-permute-start.8 = (bf16[512,1024]{1,0:T(8,128)(2,1)}, bf16[512,1024]{1,0:T(8,128)(2,1)}, u32[]{:S(2)}, u32[]{:S(2)}) collective-permute-start(bf16[512,1024]{1,0:T(8,128)(2,1)} %get-tuple-element.13), channel_id=1, source_target_pairs={{0,2},{1,3},{2,0},{3,1},{4,6},{5,7},{6,4},{7,5},{8,10},{9,11},{10,... | collective-permute-start | bytes 3145736 | tf_op jit(solution)/shard_map/ppermute | solution.py:376
  56.1 45.0 %collective-permute-start.9 = (bf16[512,1024]{1,0:T(8,128)(2,1)}, bf16[512,1024]{1,0:T(8,128)(2,1)}, u32[]{:S(2)}, u32[]{:S(2)}) collective-permute-start(bf16[512,1024]{1,0:T(8,128)(2,1)} %get-tuple-element.14), channel_id=1, source_target_pairs={{0,35},{1,34},{2,33},{3,32},{4,39},{5,38},{6,37},{7,36},{8,43},{9,... | collective-permute-start | bytes 3145736 | tf_op jit(solution)/shard_map/ppermute | solution.py:385
  60.2 36.4 %collective-permute-start.6 = (bf16[512,512]{1,0:T(8,128)(2,1)S(1)}, bf16[512,512]{1,0:T(8,128)(2,1)S(1)}, u32[]{:S(2)}, u32[]{:S(2)}) collective-permute-start(bf16[512,512]{1,0:T(8,128)(2,1)S(1)} %fusion.c0), channel_id=1, source_target_pairs={{0,2},{1,3},{2,0},{3,1},{4,6},{5,7},{6,4},{7,5},{8,10},{9,11},{10,... | collective-permute-start | bytes 1572872 | tf_op jit(solution)/shard_map/ppermute | solution.py:376
  61.2 35.8 %collective-permute-start.10 = (bf16[512,512]{1,0:T(8,128)(2,1)S(1)}, bf16[512,512]{1,0:T(8,128)(2,1)S(1)}, u32[]{:S(2)}, u32[]{:S(2)}) collective-permute-start(bf16[512,512]{1,0:T(8,128)(2,1)S(1)} %fusion.c0), channel_id=1, source_target_pairs={{0,1},{1,0},{2,3},{3,2},{4,5},{5,4},{6,7},{7,6},{8,9},{9,8},{10,11... | collective-permute-start | bytes 1572872 | tf_op jit(solution)/shard_map/ppermute | solution.py:376
  96.6 4.6 %collective-permute-start.7 = (bf16[512,512]{1,0:T(8,128)(2,1)S(1)}, bf16[512,512]{1,0:T(8,128)(2,1)S(1)}, u32[]{:S(2)}, u32[]{:S(2)}) collective-permute-start(bf16[512,512]{1,0:T(8,128)(2,1)S(1)} %collective-permute-done.6.c0), channel_id=1, source_target_pairs={{0,1},{1,0},{2,3},{3,2},{4,5},{5,4},{6,7},{7,6},{8,9},{9,8},{10,11... | collective-permute-start | bytes 1572872 | tf_op jit(solution)/shard_map/ppermute | solution.py:376

commit v5 on v4

--- a/solution.py
+++ b/solution.py
@@ -13,6 +13,7 @@
 SLOTS = 4
 CROSS = 2
 QUAD = 4
+PARTS = 2
 Z_CHIPS = 8
 QW = HD * QUAD
 HEAD = ("head_0", "head_1")
@@ -94,10 +95,58 @@
     )(position, k, v)
 
 
-def encoder_kernel(
-    pos, counts, lists, q, k, v, beside, beyond, e, kb, vb, qb, eb, edge_sem, k_sem, v_sem, q_sem, e_sem
+def encode_block(b, base, counts, lists, q_ref, kb, vb, o_ref):
+    count = counts[b]
+    ids = [lists[j, b] - base for j in range(SLOTS)]
+    for n in range(1, SLOTS + 1):
+
+        @pl.when(count == n)
+        def _(n=n):
+            attend(q_ref, [kb.at[i] for i in ids[:n]], [vb.at[i] for i in ids[:n]], o_ref)
+
+
+def inner_kernel(pos, counts, lists, q, k, v, e, kb, vb, qb, eb, k_sem, v_sem, q_sem, e_sem):
+    blocks = k.shape[0]
+    base = pos[0] * blocks
+
+    def keys(i):
+        return pltpu.make_async_copy(k.at[i], kb.at[i], k_sem.at[i])
+
+    def values(i):
+        return pltpu.make_async_copy(v.at[i], vb.at[i], v_sem.at[i])
+
+    def queries(i):
+        return pltpu.make_async_copy(q.at[i], qb.at[i], q_sem.at[i])
+
+    def result(i):
+        return pltpu.make_async_copy(eb.at[i], e.at[i], e_sem)
+
+    for i in range(blocks):
+        keys(i).start()
+        values(i).start()
+        if REACH <= i < blocks - REACH:
+            queries(i).start()
+    for i in range(2 * REACH):
+        keys(i).wait()
+        values(i).wait()
+
+    @pl.loop(REACH, blocks - REACH)
+    def _(b):
+        keys(b + REACH).wait()
+        values(b + REACH).wait()
+        queries(b).wait()
+        encode_block(b, base, counts, lists, qb.at[b], kb, vb, eb.at[b])
+        result(b).start()
+
+    for i in range(REACH, blocks - REACH):
+        result(i).wait()
+
+
+def edge_kernel(
+    pos, counts, lists, q, k, v, beside, beyond, _, e, kb, vb, qb, eb, far_sem, in_sem, e_sem
 ):
     blocks = k.shape[0]
+    near = 2 * REACH
     even = pos[0] % 2 == 0
     base = pos[0] * blocks - REACH
 
@@ -108,19 +157,20 @@
             (down.at[pl.ds(0, REACH)], kb.at[pl.ds(REACH + blocks, REACH)]),
             (down.at[pl.ds(REACH, REACH)], vb.at[pl.ds(REACH + blocks, REACH)]),
         )
-        return [pltpu.make_async_copy(a, b, edge_sem) for a, b in pairs]
-
-    def keys(i):
-        return pltpu.make_async_copy(k.at[i], kb.at[REACH + i], k_sem.at[i])
-
-    def values(i):
-        return pltpu.make_async_copy(v.at[i], vb.at[REACH + i], v_sem.at[i])
-
-    def queries(i):
-        return pltpu.make_async_copy(q.at[i], qb.at[i], q_sem.at[i])
-
-    def result(i):
-        return pltpu.make_async_copy(eb.at[i], e.at[i], e_sem)
+        return [pltpu.make_async_copy(a, b, far_sem) for a, b in pairs]
+
+    local = []
+    for start in (0, blocks - near):
+        here = pl.ds(start, near)
+        there = pl.ds(REACH + start, near)
+        local.append(pltpu.make_async_copy(k.at[here], kb.at[there], in_sem))
+        local.append(pltpu.make_async_copy(v.at[here], vb.at[there], in_sem))
+    for i, start in enumerate((0, blocks - REACH)):
+        local.append(
+            pltpu.make_async_copy(q.at[pl.ds(start, REACH)], qb.at[pl.ds(i * REACH, REACH)], in_sem)
+        )
+    for copy in local:
+        copy.start()
 
     @pl.when(even)
     def _():
@@ -132,74 +182,56 @@
         for copy in edges(beside, beyond):
             copy.start()
 
-    for i in range(blocks):
-        keys(i).start()
-        values(i).start()
-        queries(i).start()
-    for copy in edges(beyond, beside):
+    for copy in local + edges(beyond, beside):
         copy.wait()
-    for i in range(REACH):
-        keys(i).wait()
-        values(i).wait()
-
-    @pl.loop(0, blocks)
-    def _(b):
-        @pl.when(b + REACH < blocks)
-        def _():
-            keys(b + REACH).wait()
-            values(b + REACH).wait()
-
-        queries(b).wait()
-        count = counts[b]
-        ids = [lists[j, b] - base for j in range(SLOTS)]
-        for n in range(1, SLOTS + 1):
-
-            @pl.when(count == n)
-            def _(n=n):
-                attend(
-                    qb.at[b], [kb.at[i] for i in ids[:n]], [vb.at[i] for i in ids[:n]], eb.at[b]
-                )
-
-        result(b).start()
-
-    for i in range(blocks):
-        result(i).wait()
-
-
-def encoder_call(position, counts, lists, q, k3, v3, beside, beyond):
+
+    @pl.loop(0, near)
+    def _(t):
+        b = jnp.where(t < REACH, t, blocks - near + t)
+        encode_block(b, base, counts, lists, qb.at[t], kb, vb, eb.at[t])
+        pltpu.make_async_copy(eb.at[t], e.at[b], e_sem).start()
+
+    for t in range(near):
+        pltpu.make_async_copy(eb.at[t], e.at[t], e_sem).wait()
+
+
+def encoder_call(position, counts, lists, q, k3, v3, edges=None):
     blocks, _, width = k3.shape
     smem = pl.BlockSpec(memory_space=pltpu.SMEM)
     hbm = pl.BlockSpec(memory_space=pl.ANY)
-    vmem = pl.BlockSpec(memory_space=pltpu.VMEM)
+    dma = pltpu.SemaphoreType.DMA
 
     def room(n):
         return pltpu.VMEM((n, BLK, width), jnp.bfloat16)
 
+    shape = jax.ShapeDtypeStruct(k3.shape, jnp.bfloat16)
+    args = (position, counts, lists, cut(q), k3, v3)
+    if edges is None:
+        return pl.pallas_call(
+            inner_kernel,
+            in_specs=[smem] * 3 + [hbm] * 3,
+            out_specs=hbm,
+            out_shape=shape,
+            scratch_shapes=[room(blocks)] * 4 + [dma((blocks,))] * 3 + [dma],
+            name="encoder_inner",
+        )(*args)
+    beside, beyond, partial = edges
     return pl.pallas_call(
-        encoder_kernel,
-        in_specs=[smem] * 3 + [hbm] * 3 + [vmem] * 2,
+        edge_kernel,
+        in_specs=[smem] * 3 + [hbm] * 3 + [pl.BlockSpec(memory_space=pltpu.VMEM)] * 2 + [hbm],
         out_specs=hbm,
-        out_shape=jax.ShapeDtypeStruct(k3.shape, jnp.bfloat16),
-        scratch_shapes=[
-            room(blocks + 2 * REACH),
-            room(blocks + 2 * REACH),
-            room(blocks),
-            room(blocks),
-            pltpu.SemaphoreType.DMA,
-            pltpu.SemaphoreType.DMA((blocks,)),
-            pltpu.SemaphoreType.DMA((blocks,)),
-            pltpu.SemaphoreType.DMA((blocks,)),
-            pltpu.SemaphoreType.DMA,
-        ],
-        name="encoder",
-    )(position, counts, lists, cut(q), k3, v3, in_vmem(cut(beside)), in_vmem(cut(beyond)))
+        out_shape=shape,
+        scratch_shapes=[room(blocks + 2 * REACH)] * 2 + [room(2 * REACH)] * 2 + [dma] * 3,
+        input_output_aliases={8: 0},
+        name="encoder_edge",
+    )(*args, in_vmem(cut(beside)), in_vmem(cut(beyond)), partial)
 
 
 def serve_kernel(pos, owners, slots, k, e, *refs):
-    sources = (len(refs) - 6) // 2
+    sources = (len(refs) - 6) // (1 + PARTS)
     queries = refs[:sources]
-    answers = refs[sources : 2 * sources]
-    kb, eb, qb, ob, load_sems, answer_sem = refs[2 * sources :]
+    answers = refs[sources : (1 + PARTS) * sources]
+    kb, eb, qb, ob, load_sems, answer_sem = refs[(1 + PARTS) * sources :]
     mine = pos[0]
     per = queries[0].shape[0]
     total = owners.shape[0] // per
@@ -235,32 +267,40 @@
                 for copy in loads(i, t, s0, s1):
                     copy.start()
 
-    for i in range(sources):
-
-        @pl.loop(0, per)
-        def _(t, i=i):
-            live, s0, s1 = candidate(i, t)
-            n = i * per + t
-
-            @pl.when(live)
-            def _():
-                for copy in loads(i, t, s0, s1):
-                    copy.wait()
-                attend(
-                    qb.at[n],
-                    [kb.at[n, j] for j in range(CROSS)],
-                    [eb.at[n, j] for j in range(CROSS)],
-                    ob.at[n],
-                )
-
-            @pl.when(jnp.logical_not(live))
-            def _():
-                ob[n] = jnp.zeros(ob.shape[1:], ob.dtype)
-
-        pltpu.make_async_copy(ob.at[pl.ds(i * per, per)], answers[i], answer_sem).start()
-
-    for i in range(sources):
-        pltpu.make_async_copy(ob.at[pl.ds(i * per, per)], answers[i], answer_sem).wait()
+    share = per // PARTS
+
+    def answer(part, i):
+        rows = ob.at[pl.ds(i * per + part * share, share)]
+        return pltpu.make_async_copy(rows, answers[part * sources + i], answer_sem)
+
+    for part in range(PARTS):
+        for i in range(sources):
+
+            @pl.loop(part * share, (part + 1) * share)
+            def _(t, i=i):
+                live, s0, s1 = candidate(i, t)
+                n = i * per + t
+
+                @pl.when(live)
+                def _():
+                    for copy in loads(i, t, s0, s1):
+                        copy.wait()
+                    attend(
+                        qb.at[n],
+                        [kb.at[n, j] for j in range(CROSS)],
+                        [eb.at[n, j] for j in range(CROSS)],
+                        ob.at[n],
+                    )
+
+                @pl.when(jnp.logical_not(live))
+                def _():
+                    ob[n] = jnp.zeros(ob.shape[1:], ob.dtype)
+
+            answer(part, i).start()
+
+    for part in range(PARTS):
+        for i in range(sources):
+            answer(part, i).wait()
 
 
 def serve_call(position, owners, slots, k3, e3, queries):
@@ -277,8 +317,9 @@
     out = pl.pallas_call(
         serve_kernel,
         in_specs=[smem] * 3 + [hbm] * 2 + [vmem if sources > 1 else hbm] * sources,
-        out_specs=[hbm] * sources,
-        out_shape=[jax.ShapeDtypeStruct((per, BLK, width), jnp.bfloat16)] * sources,
+        out_specs=[hbm] * (sources * PARTS),
+        out_shape=[jax.ShapeDtypeStruct((per // PARTS, BLK, width), jnp.bfloat16)]
+        * (sources * PARTS),
         scratch_shapes=[
             pltpu.VMEM((served, CROSS, BLK, width), jnp.bfloat16),
             pltpu.VMEM((served, CROSS, BLK, width), jnp.bfloat16),
@@ -288,7 +329,7 @@
             pltpu.SemaphoreType.DMA,
         ],
     )(position, owners, slots, k3, e3, *queries)
-    return [x.reshape(per * BLK, width) for x in out]
+    return [x.reshape(-1, width) for x in out]
 
 
 def cut(x):
@@ -334,35 +375,40 @@
     )(part, w)
 
 
-def project_kernel(part, c0, c1, w0, w1, r_ref, o_ref):
+def project_kernel(part, c0, c1, w0, w1, r_ref, *refs):
     total = r_ref[...].astype(jnp.float32)
     for c, w in ((c0, w0), (c1, w1)):
         total = total + jnp.dot(c[...], w[...], preferred_element_type=jnp.float32)
-    o_ref[...] = total.astype(o_ref.dtype)
-
-
-def project_call(part, contexts, weights, added, dtype):
+    refs[-1][...] = total.astype(refs[-1].dtype)
+
+
+def project_call(part, contexts, weights, added, dtype, index, out_tokens, earlier=None):
     tokens, width = contexts[0].shape
     columns = added.shape[1]
-    tile = min(tokens, 256)
-    c_spec = pl.BlockSpec((tile, width), lambda i, p: (i, 0))
+    here = index if added.shape[0] > tokens else 0
+    there = index if out_tokens > tokens else 0
+    c_spec = pl.BlockSpec((tokens, width), lambda i, p: (0, 0))
     w_specs = [
         pl.BlockSpec((width, columns), lambda i, p: (0, p[0]))
         if w.shape[1] > columns
         else pl.BlockSpec((width, columns), lambda i, p: (0, 0))
         for w in weights
     ]
-    r_spec = pl.BlockSpec((tile, columns), lambda i, p: (i, 0))
+    more = [] if earlier is None else [earlier]
     return pl.pallas_call(
         project_kernel,
         grid_spec=pltpu.PrefetchScalarGridSpec(
             num_scalar_prefetch=1,
-            grid=(tokens // tile,),
-            in_specs=[c_spec] * 2 + w_specs + [r_spec],
-            out_specs=r_spec,
+            grid=(1,),
+            in_specs=[c_spec] * 2
+            + w_specs
+            + [pl.BlockSpec((tokens, columns), lambda i, p: (here, 0))]
+            + [pl.BlockSpec(memory_space=pl.ANY)] * len(more),
+            out_specs=pl.BlockSpec((tokens, columns), lambda i, p: (there, 0)),
         ),
-        out_shape=jax.ShapeDtypeStruct(added.shape, dtype),
-    )(part, *[in_vmem(c) for c in contexts], *weights, added)
+        out_shape=jax.ShapeDtypeStruct((out_tokens, columns), dtype),
+        input_output_aliases={6: 0} if more else {},
+    )(part, *[in_vmem(c) for c in contexts], *weights, added, *more)
 
 
 def exchanged(block, first):
@@ -415,18 +461,30 @@
     w2 = swapped(across2, 2)
     w3 = other_side(across3, 3)
     w1 = swapped(across1, 1)
-    e3 = encoder_call(position, block_counts, lists, encoder_queries, k3, v3, beside, beyond)
+    encoder_args = (position, block_counts, lists, encoder_queries, k3, v3)
+    partial = encoder_call(*encoder_args)
+    e3 = encoder_call(*encoder_args, edges=(beside, beyond, partial))
     tables = (position, span_owner, slots, k3, e3)
-    (own,) = serve_call(*tables, [decoder_queries])
-    for_beside, for_beyond = serve_call(*tables, [q_beside, q_beyond])
-    from_beside = exchanged(for_beside, 0)
-    from_beyond = exchanged(for_beyond, 1)
-    context = own + from_beside + from_beyond
-    across = swapped(context, 2)
-    beside = swapped(context, 1)
-    corner = swapped(across, 1)
-    total = project_call(part, [context, beside], [out_weight, w1], decoder_input, jnp.float32)
-    decoder_out = project_call(part, [across, corner], [w2, w3], total, jnp.bfloat16)
+    answers = serve_call(*tables, [q_beside, q_beyond])
+    returned = []
+    for i in range(PARTS):
+        from_beside = exchanged(answers[2 * i], 0)
+        from_beyond = exchanged(answers[2 * i + 1], 1)
+        returned.append((from_beside, from_beyond))
+    own = serve_call(*tables, [decoder_queries])
+    tokens = decoder_input.shape[0]
+    decoder_out = None
+    for i in range(PARTS):
+        context = own[i] + returned[i][0] + returned[i][1]
+        across = swapped(context, 2)
+        aside = swapped(context, 1)
+        corner = swapped(across, 1)
+        total = project_call(
+            part, [context, aside], [out_weight, w1], decoder_input, jnp.float32, i, tokens // PARTS
+        )
+        decoder_out = project_call(
+            part, [across, corner], [w2, w3], total, jnp.bfloat16, i, tokens, decoder_out
+        )
     return (e3.reshape(blocks * BLK, width), decoder_out)
 
 

time: 106 us -> 111 us (1.047)
  the two profiles are of different devices: /device:TPU:21 before, /device:TPU:23 now
where the time goes in v5:
time: 111 us; the launch traced here: 110 us
  starting transfers between devices  41.8 us (38%)
  Pallas kernels  40.2 us (36%)
  waiting for transfers between devices  24.5 us (22%)
  other arithmetic  1.98 us (2%)
    ppermute x8, starting transfers between devices, exchanged(): return lax.ppermute(block, 'seq', route)  26.6 us
    ppermute x8, waiting for transfers between devices, swapped(): return lax.ppermute(block, HEAD, [(i, i ^ flip) for i in range(4)])  22.9 us
    pallas_call x4, Pallas kernels, project_call(): pl.pallas_call(project_kernel, grid_spec=pltpu.PrefetchScalarGridSpec(num...  13.5 us
    ppermute x8, starting transfers between devices, swapped(): return lax.ppermute(block, HEAD, [(i, i ^ flip) for i in range(4)])  11.8 us
    pallas_call x1, Pallas kernels, encoder_call(): pl.pallas_call(inner_kernel, in_specs=[smem] * 3 + [hbm] * 3, out_specs=h...  8.62 us
    pallas_call x2, Pallas kernels, serve_call(): pl.pallas_call(serve_kernel, in_specs=[smem] * 3 + [hbm] * 2 + [vmem if s...  6.99 us
    pallas_call x1, Pallas kernels, encoder_call(): pl.pallas_call(edge_kernel, in_specs=[smem] * 3 + [hbm] * 3 + [pl.BlockSp...  5.98 us
    ppermute x1, starting transfers between devices, other_side(): return lax.ppermute(block, axes, route)  3.42 us
  transfers between devices with their start and end apart: 17, of which 4 were waited for; matrix products, arithmetic and copies ran while one was open for 2% of the time, Pallas kernels for 31%

profile of v5, /device:TPU:23, one launch (start us, length us, event | category | flops | bytes accessed | tf_op | source)
XLA Modules:
  0.0 110.3 jit_solution(9304444273755711327)
XLA Ops:
  0.6 2.2 %pack_edges.1 = (bf16[512,512]{1,0:T(8,128)(2,1)}, bf16[512,512]{1,0:T(8,128)(2,1)}) custom-call(s32[1]{0:T(128)} %bitcast.pos, bf16[1536,512]{1,0:T(8,128)(2,1)} %k.1, bf16[1536,512]{1,0:T(8,128)(2,1)} %v.1), custom_call_target="tpu_custom_call" | custom-call | tf_op jit(solution)/shard_map/pack_edges/pallas_call | solution.py:87
  2.9 1.7 %collective-permute-start = (bf16[512,512]{1,0:T(8,128)(2,1)}, bf16[512,512]{1,0:T(8,128)(2,1)S(1)}, u32[]{:S(2)}, u32[]{:S(2)}) collective-permute-start(bf16[512,512]{1,0:T(8,128)(2,1)} %get-tuple-element.13), channel_id=1, source_target_pairs={{0,4},{4,0},{8,12},{12,8},{16,20},{20,16},{24,28},{28,24},{32,36},... | collective-permute-start | bytes 1572872 | tf_op jit(solution)/shard_map/ppermute | solution.py:418
  4.6 7.4 %collective-permute-start.1 = (bf16[512,512]{1,0:T(8,128)(2,1)}, bf16[512,512]{1,0:T(8,128)(2,1)S(1)}, u32[]{:S(2)}, u32[]{:S(2)}) collective-permute-start(bf16[512,512]{1,0:T(8,128)(2,1)} %get-tuple-element.14), channel_id=1, source_target_pairs={{4,8},{8,4},{12,16},{16,12},{20,24},{24,20},{28,32},{32,28},{36,40... | collective-permute-start | bytes 1572872 | tf_op jit(solution)/shard_map/ppermute | solution.py:418
  12.1 3.3 %collective-permute-start.3 = (bf16[512,512]{1,0:T(8,128)(2,1)S(1)}, bf16[512,512]{1,0:T(8,128)(2,1)S(1)}, u32[]{:S(2)}, u32[]{:S(2)}) collective-permute-start(bf16[512,512]{1,0:T(8,128)(2,1)S(1)} %copy-done.1), channel_id=1, source_target_pairs={{4,8},{8,4},{12,16},{16,12},{20,24},{24,20},{28,32},{32,28},{36,40... | collective-permute-start | bytes 1572872 | tf_op jit(solution)/shard_map/ppermute | solution.py:418
  15.5 2.9 %cut_weight.1 = (bf16[512,1024]{1,0:T(8,128)(2,1)}, bf16[512,1024]{1,0:T(8,128)(2,1)}, bf16[512,1024]{1,0:T(8,128)(2,1)}) custom-call(s32[1]{0:T(128)} %bitcast.8.part, bf16[512,4096]{1,0:T(8,128)(2,1)} %w0.3), custom_call_target="tpu_custom_call" | custom-call | tf_op jit(solution)/shard_map/cut_weight/pallas_call | solution.py:367
  18.4 1.9 %collective-permute-start.11 = (bf16[512,1024]{1,0:T(8,128)(2,1)}, bf16[512,1024]{1,0:T(8,128)(2,1)}, u32[]{:S(2)}, u32[]{:S(2)}) collective-permute-start(bf16[512,1024]{1,0:T(8,128)(2,1)} %get-tuple-element.20), channel_id=1, source_target_pairs={{0,1},{1,0},{2,3},{3,2},{4,5},{5,4},{6,7},{7,6},{8,9},{9,8},{10,11... | collective-permute-start | bytes 3145736 | tf_op jit(solution)/shard_map/ppermute | solution.py:422
  20.3 8.6 %encoder_inner.1._ = bf16[12,128,512]{2,1,0:T(8,128)(2,1)} custom-call(s32[1]{0:T(128)} %bitcast.pos, s32[12]{0:T(128)} %counts.3, s32[4,12]{1,0:T(4,128)} %bitcast.41, bf16[12,128,512]{2,1,0:T(8,128)(2,1)} %bitcast.36, bf16[12,128,512]{2,1,0:T(8,128)(2,1)} %bitcast.29, bf16[12,128,512]{2,1,0:T(8,128)(2,1)} %bitcast.34), custom_call_target="tpu_custom_call" | custom-call | tf_op jit(solution)/shard_map/encoder_inner/pallas_call | solution.py:210
  29.0 6.0 %encoder_edge.1.e = bf16[12,128,512]{2,1,0:T(8,128)(2,1)} custom-call(s32[1]{0:T(128)} %bitcast.pos, s32[12]{0:T(128)} %counts.3, s32[4,12]{1,0:T(4,128)} %bitcast.42, bf16[12,128,512]{2,1,0:T(8,128)(2,1)} %bitcast.37, bf16[12,128,512]{2,1,0:T(8,128)(2,1)} %bitcast.30, bf16[12,128,512]{2,1,0:T(8,128)(2,1)} %bitcast.35, ...), custom_call_target="tpu_custom_call", output_to_operand_aliasing={{}: (8, {})} | custom-call | tf_op jit(solution)/shard_map/encoder_edge/pallas_call | solution.py:219
  35.0 5.3 %shard_map.114 = (bf16[2,128,512]{2,1,0:T(8,128)(2,1)}, bf16[2,128,512]{2,1,0:T(8,128)(2,1)}, bf16[2,128,512]{2,1,0:T(8,128)(2,1)}, bf16[2,128,512]{2,1,0:T(8,128)(2,1)}) custom-call(s32[1]{0:T(128)} %bitcast.pos, s32[256]{0:T(256)} %owners.3, s32[2,256]{1,0:T(2,128)} %bitcast.39, bf16[12,128,512]{2,1,0:T(8,128)(2,1)} %bitcast.31, ...), custom_call_target="tpu_custom_call" | custom-call | tf_op jit(solution)/shard_map/pallas_call | solution.py:317
  40.4 7.1 %collective-permute-start.13 = (bf16[256,512]{1,0:T(8,128)(2,1)}, bf16[256,512]{1,0:T(8,128)(2,1)S(1)}, u32[]{:S(2)}, u32[]{:S(2)}) collective-permute-start(bf16[256,512]{1,0:T(8,128)(2,1)} %bitcast.45), channel_id=1, source_target_pairs={{4,8},{8,4},{12,16},{16,12},{20,24},{24,20},{28,32},{32,28},{36,40... | collective-permute-start | bytes 786440 | tf_op jit(solution)/shard_map/ppermute | solution.py:418
  47.6 3.4 %collective-permute-start.9 = (bf16[512,1024]{1,0:T(8,128)(2,1)}, bf16[512,1024]{1,0:T(8,128)(2,1)}, u32[]{:S(2)}, u32[]{:S(2)}) collective-permute-start(bf16[512,1024]{1,0:T(8,128)(2,1)} %get-tuple-element.19), channel_id=1, source_target_pairs={{0,35},{1,34},{2,33},{3,32},{4,39},{5,38},{6,37},{7,36},{8,43},{9,... | collective-permute-start | bytes 3145736 | tf_op jit(solution)/shard_map/ppermute | solution.py:431
  51.0 1.5 %collective-permute-done.13 = bf16[256,512]{1,0:T(8,128)(2,1)S(1)} collective-permute-done((bf16[256,512]{1,0:T(8,128)(2,1)}, bf16[256,512]{1,0:T(8,128)(2,1)S(1)}, u32[]{:S(2)}, u32[]{:S(2)}) %collective-permute-start.13) | collective-permute-done | bytes 262176 | tf_op jit(solution)/shard_map/ppermute | solution.py:418
  52.6 6.9 %collective-permute-start.5 = (bf16[256,512]{1,0:T(8,128)(2,1)}, bf16[256,512]{1,0:T(8,128)(2,1)S(1)}, u32[]{:S(2)}, u32[]{:S(2)}) collective-permute-start(bf16[256,512]{1,0:T(8,128)(2,1)} %bitcast.43), channel_id=1, source_target_pairs={{4,8},{8,4},{12,16},{16,12},{20,24},{24,20},{28,32},{32,28},{36,40... | collective-permute-start | bytes 786440 | tf_op jit(solution)/shard_map/ppermute | solution.py:418
  59.5 1.6 %shard_map.113 = (bf16[2,128,512]{2,1,0:T(8,128)(2,1)}, bf16[2,128,512]{2,1,0:T(8,128)(2,1)}) custom-call(s32[1]{0:T(128)} %bitcast.pos, s32[256]{0:T(256)} %owners.3, s32[2,256]{1,0:T(2,128)} %bitcast.40, bf16[12,128,512]{2,1,0:T(8,128)(2,1)} %bitcast.32, bf16[12,128,512]{2,1,0:T(8,128)(2,1)} %encoder_edge.1.e, bf16[4,128,512]{2,1,0:T(8,128)(2,1)} %bitcast.38), custom_call_target="tpu_custom_call" | custom-call | tf_op jit(solution)/shard_map/pallas_call | solution.py:317
  62.1 3.1 %collective-permute-start.16 = (bf16[256,512]{1,0:T(8,128)(2,1)S(1)}, bf16[256,512]{1,0:T(8,128)(2,1)S(1)}, u32[]{:S(2)}, u32[]{:S(2)}) collective-permute-start(bf16[256,512]{1,0:T(8,128)(2,1)S(1)} %fusion.c0), channel_id=1, source_target_pairs={{0,1},{1,0},{2,3},{3,2},{4,5},{5,4},{6,7},{7,6},{8,9},{9,8},{10,11... | collective-permute-start | bytes 786440 | tf_op jit(solution)/shard_map/ppermute | solution.py:422
  66.4 1.4 %collective-permute-start.6 = (bf16[256,512]{1,0:T(8,128)(2,1)S(1)}, bf16[256,512]{1,0:T(8,128)(2,1)S(1)}, u32[]{:S(2)}, u32[]{:S(2)}) collective-permute-start(bf16[256,512]{1,0:T(8,128)(2,1)S(1)} %fusion.1.c0), channel_id=1, source_target_pairs={{0,2},{1,3},{2,0},{3,1},{4,6},{5,7},{6,4},{7,5},{8,10},{9,11},{10,... | collective-permute-start | bytes 786440 | tf_op jit(solution)/shard_map/ppermute | solution.py:422
  67.8 2.7 %collective-permute-start.10 = (bf16[256,512]{1,0:T(8,128)(2,1)S(1)}, bf16[256,512]{1,0:T(8,128)(2,1)S(1)}, u32[]{:S(2)}, u32[]{:S(2)}) collective-permute-start(bf16[256,512]{1,0:T(8,128)(2,1)S(1)} %fusion.1.c0), channel_id=1, source_target_pairs={{0,1},{1,0},{2,3},{3,2},{4,5},{5,4},{6,7},{7,6},{8,9},{9,8},{10,11... | collective-permute-start | bytes 786440 | tf_op jit(solution)/shard_map/ppermute | solution.py:422
  70.5 18.7 %collective-permute-done.14.c0 = bf16[256,512]{1,0:T(8,128)(2,1)S(1)} collective-permute-done((bf16[256,512]{1,0:T(8,128)(2,1)S(1)}, bf16[256,512]{1,0:T(8,128)(2,1)S(1)}, u32[]{:S(2)}, u32[]{:S(2)}) %collective-permute-start.14) | collective-permute-done | bytes 262176 | tf_op jit(solution)/shard_map/ppermute | solution.py:422
  89.2 1.6 %collective-permute-start.15 = (bf16[256,512]{1,0:T(8,128)(2,1)S(1)}, bf16[256,512]{1,0:T(8,128)(2,1)S(1)}, u32[]{:S(2)}, u32[]{:S(2)}) collective-permute-start(bf16[256,512]{1,0:T(8,128)(2,1)S(1)} %collective-permute-done.14.c0), channel_id=1, source_target_pairs={{0,1},{1,0},{2,3},{3,2},{4,5},{5,4},{6,7},{7,6},{8,9},{9,8},{10,11... | collective-permute-start | bytes 786440 | tf_op jit(solution)/shard_map/ppermute | solution.py:422
  90.8 4.0 %collective-permute-done.6.c0 = bf16[256,512]{1,0:T(8,128)(2,1)S(1)} collective-permute-done((bf16[256,512]{1,0:T(8,128)(2,1)S(1)}, bf16[256,512]{1,0:T(8,128)(2,1)S(1)}, u32[]{:S(2)}, u32[]{:S(2)}) %collective-permute-start.6) | collective-permute-done | bytes 262176 | tf_op jit(solution)/shard_map/ppermute | solution.py:422
  95.8 3.4 %shard_map.116.r_ref = f32[256,1024]{1,0:T(8,128)} custom-call(s32[1]{0:T(128)} %bitcast.8.part, bf16[256,512]{1,0:T(8,128)(2,1)S(1)} %fusion.c0, bf16[256,512]{1,0:T(8,128)(2,1)S(1)} %collective-permute-done.16.c1, bf16[512,4096]{1,0:T(8,128)(2,1)} %w0.3, bf16[512,1024]{1,0:T(8,128)(2,1)} %collective-permute-done.11.w1, bf16[512,1024]{1,0:T(8,128)(2,1)} %r_ref.3), custom_call_target="tpu_custom_call" | custom-call | tf_op jit(solution)/shard_map/pallas_call | solution.py:398
  99.2 3.4 %shard_map.115.r_ref = f32[256,1024]{1,0:T(8,128)} custom-call(s32[1]{0:T(128)} %bitcast.8.part, bf16[256,512]{1,0:T(8,128)(2,1)S(1)} %fusion.1.c0, bf16[256,512]{1,0:T(8,128)(2,1)S(1)} %collective-permute-done.10.c1, bf16[512,4096]{1,0:T(8,128)(2,1)} %w0.3, bf16[512,1024]{1,0:T(8,128)(2,1)} %collective-permute-done.11.w1, bf16[512,1024]{1,0:T(8,128)(2,1)} %r_ref.3), custom_call_target="tpu_custom_call" | custom-call | tf_op jit(solution)/shard_map/pallas_call | solution.py:398
  103.6 3.4 %shard_map.117.refs_0_ = bf16[512,1024]{1,0:T(8,128)(2,1)} custom-call(s32[1]{0:T(128)} %bitcast.8.part, bf16[256,512]{1,0:T(8,128)(2,1)S(1)} %collective-permute-done.14.c0, bf16[256,512]{1,0:T(8,128)(2,1)S(1)} %collective-permute-done.15.c1, bf16[512,1024]{1,0:T(8,128)(2,1)} %copy-done, bf16[512,1024]{1,0:T(8,128)(2,1)} %collective-permute-done.9.w1, ...), custom_call_target="tpu_custom_call" | custom-call | tf_op jit(solution)/shard_map/pallas_call | solution.py:398
  106.9 3.4 %shard_map.118 = bf16[512,1024]{1,0:T(8,128)(2,1)} custom-call(s32[1]{0:T(128)} %bitcast.8.part, bf16[256,512]{1,0:T(8,128)(2,1)S(1)} %collective-permute-done.6.c0, bf16[256,512]{1,0:T(8,128)(2,1)S(1)} %collective-permute-done.7.c1, bf16[512,1024]{1,0:T(8,128)(2,1)} %copy-done, ...), custom_call_target="tpu_custom_call", output_to_operand_aliasing={{}: (6, {})} | custom-call | tf_op jit(solution)/shard_map/pallas_call | solution.py:398
  (26 shorter events, 4.4 us)
Async XLA Ops:
  0.6 11.4 %copy-start.1 = (bf16[512,512]{1,0:T(8,128)(2,1)S(1)}, bf16[512,512]{1,0:T(8,128)(2,1)}, u32[]{:S(2)}) copy-start(bf16[512,512]{1,0:T(8,128)(2,1)} %param.15) | copy-start | bytes 1572868
  2.9 26.1 %collective-permute-start = (bf16[512,512]{1,0:T(8,128)(2,1)}, bf16[512,512]{1,0:T(8,128)(2,1)S(1)}, u32[]{:S(2)}, u32[]{:S(2)}) collective-permute-start(bf16[512,512]{1,0:T(8,128)(2,1)} %get-tuple-element.13), channel_id=1, source_target_pairs={{0,4},{4,0},{8,12},{12,8},{16,20},{20,16},{24,28},{28,24},{32,36},... | collective-permute-start | bytes 1572872 | tf_op jit(solution)/shard_map/ppermute | solution.py:418
  4.6 24.3 %collective-permute-start.1 = (bf16[512,512]{1,0:T(8,128)(2,1)}, bf16[512,512]{1,0:T(8,128)(2,1)S(1)}, u32[]{:S(2)}, u32[]{:S(2)}) collective-permute-start(bf16[512,512]{1,0:T(8,128)(2,1)} %get-tuple-element.14), channel_id=1, source_target_pairs={{4,8},{8,4},{12,16},{16,12},{20,24},{24,20},{28,32},{32,28},{36,40... | collective-permute-start | bytes 1572872 | tf_op jit(solution)/shard_map/ppermute | solution.py:418
  12.0 22.9 %collective-permute-start.2 = (bf16[512,512]{1,0:T(8,128)(2,1)S(1)}, bf16[512,512]{1,0:T(8,128)(2,1)S(1)}, u32[]{:S(2)}, u32[]{:S(2)}) collective-permute-start(bf16[512,512]{1,0:T(8,128)(2,1)S(1)} %copy-done.1), channel_id=1, source_target_pairs={{0,4},{4,0},{8,12},{12,8},{16,20},{20,16},{24,28},{28,24},{32,36},... | collective-permute-start | bytes 1572872 | tf_op jit(solution)/shard_map/ppermute | solution.py:418
  12.1 22.8 %collective-permute-start.3 = (bf16[512,512]{1,0:T(8,128)(2,1)S(1)}, bf16[512,512]{1,0:T(8,128)(2,1)S(1)}, u32[]{:S(2)}, u32[]{:S(2)}) collective-permute-start(bf16[512,512]{1,0:T(8,128)(2,1)S(1)} %copy-done.1), channel_id=1, source_target_pairs={{4,8},{8,4},{12,16},{16,12},{20,24},{24,20},{28,32},{32,28},{36,40... | collective-permute-start | bytes 1572872 | tf_op jit(solution)/shard_map/ppermute | solution.py:418
  18.4 49.4 %collective-permute-start.11 = (bf16[512,1024]{1,0:T(8,128)(2,1)}, bf16[512,1024]{1,0:T(8,128)(2,1)}, u32[]{:S(2)}, u32[]{:S(2)}) collective-permute-start(bf16[512,1024]{1,0:T(8,128)(2,1)} %get-tuple-element.20), channel_id=1, source_target_pairs={{0,1},{1,0},{2,3},{3,2},{4,5},{5,4},{6,7},{7,6},{8,9},{9,8},{10,11... | collective-permute-start | bytes 3145736 | tf_op jit(solution)/shard_map/ppermute | solution.py:422
  40.3 10.7 %collective-permute-start.12 = (bf16[256,512]{1,0:T(8,128)(2,1)}, bf16[256,512]{1,0:T(8,128)(2,1)S(1)}, u32[]{:S(2)}, u32[]{:S(2)}) collective-permute-start(bf16[256,512]{1,0:T(8,128)(2,1)} %bitcast.46), channel_id=1, source_target_pairs={{0,4},{4,0},{8,12},{12,8},{16,20},{20,16},{24,28},{28,24},{32,36},... | collective-permute-start | bytes 786440 | tf_op jit(solution)/shard_map/ppermute | solution.py:418
  40.4 12.1 %collective-permute-start.13 = (bf16[256,512]{1,0:T(8,128)(2,1)}, bf16[256,512]{1,0:T(8,128)(2,1)S(1)}, u32[]{:S(2)}, u32[]{:S(2)}) collective-permute-start(bf16[256,512]{1,0:T(8,128)(2,1)} %bitcast.45), channel_id=1, source_target_pairs={{4,8},{8,4},{12,16},{16,12},{20,24},{24,20},{28,32},{32,28},{36,40... | collective-permute-start | bytes 786440 | tf_op jit(solution)/shard_map/ppermute | solution.py:418
  47.5 55.1 %collective-permute-start.8 = (bf16[512,1024]{1,0:T(8,128)(2,1)}, bf16[512,1024]{1,0:T(8,128)(2,1)S(1)}, u32[]{:S(2)}, u32[]{:S(2)}) collective-permute-start(bf16[512,1024]{1,0:T(8,128)(2,1)} %get-tuple-element.18), channel_id=1, source_target_pairs={{0,2},{1,3},{2,0},{3,1},{4,6},{5,7},{6,4},{7,5},{8,10},{9,11},{10,... | collective-permute-start | bytes 3145736 | tf_op jit(solution)/shard_map/ppermute | solution.py:422
  47.6 55.0 %collective-permute-start.9 = (bf16[512,1024]{1,0:T(8,128)(2,1)}, bf16[512,1024]{1,0:T(8,128)(2,1)}, u32[]{:S(2)}, u32[]{:S(2)}) collective-permute-start(bf16[512,1024]{1,0:T(8,128)(2,1)} %get-tuple-element.19), channel_id=1, source_target_pairs={{0,35},{1,34},{2,33},{3,32},{4,39},{5,38},{6,37},{7,36},{8,43},{9,... | collective-permute-start | bytes 3145736 | tf_op jit(solution)/shard_map/ppermute | solution.py:431
  51.0 11.1 %collective-permute-start.4 = (bf16[256,512]{1,0:T(8,128)(2,1)}, bf16[256,512]{1,0:T(8,128)(2,1)S(1)}, u32[]{:S(2)}, u32[]{:S(2)}) collective-permute-start(bf16[256,512]{1,0:T(8,128)(2,1)} %bitcast.44), channel_id=1, source_target_pairs={{0,4},{4,0},{8,12},{12,8},{16,20},{20,16},{24,28},{28,24},{32,36},... | collective-permute-start | bytes 786440 | tf_op jit(solution)/shard_map/ppermute | solution.py:418
  52.6 12.7 %collective-permute-start.5 = (bf16[256,512]{1,0:T(8,128)(2,1)}, bf16[256,512]{1,0:T(8,128)(2,1)S(1)}, u32[]{:S(2)}, u32[]{:S(2)}) collective-permute-start(bf16[256,512]{1,0:T(8,128)(2,1)} %bitcast.43), channel_id=1, source_target_pairs={{4,8},{8,4},{12,16},{16,12},{20,24},{24,20},{28,32},{32,28},{36,40... | collective-permute-start | bytes 786440 | tf_op jit(solution)/shard_map/ppermute | solution.py:418
  62.1 4.3 %collective-permute-start.16 = (bf16[256,512]{1,0:T(8,128)(2,1)S(1)}, bf16[256,512]{1,0:T(8,128)(2,1)S(1)}, u32[]{:S(2)}, u32[]{:S(2)}) collective-permute-start(bf16[256,512]{1,0:T(8,128)(2,1)S(1)} %fusion.c0), channel_id=1, source_target_pairs={{0,1},{1,0},{2,3},{3,2},{4,5},{5,4},{6,7},{7,6},{8,9},{9,8},{10,11... | collective-permute-start | bytes 786440 | tf_op jit(solution)/shard_map/ppermute | solution.py:422
  65.3 24.0 %collective-permute-start.14 = (bf16[256,512]{1,0:T(8,128)(2,1)S(1)}, bf16[256,512]{1,0:T(8,128)(2,1)S(1)}, u32[]{:S(2)}, u32[]{:S(2)}) collective-permute-start(bf16[256,512]{1,0:T(8,128)(2,1)S(1)} %fusion.c0), channel_id=1, source_target_pairs={{0,2},{1,3},{2,0},{3,1},{4,6},{5,7},{6,4},{7,5},{8,10},{9,11},{10,... | collective-permute-start | bytes 786440 | tf_op jit(solution)/shard_map/ppermute | solution.py:422
  66.4 28.4 %collective-permute-start.6 = (bf16[256,512]{1,0:T(8,128)(2,1)S(1)}, bf16[256,512]{1,0:T(8,128)(2,1)S(1)}, u32[]{:S(2)}, u32[]{:S(2)}) collective-permute-start(bf16[256,512]{1,0:T(8,128)(2,1)S(1)} %fusion.1.c0), channel_id=1, source_target_pairs={{0,2},{1,3},{2,0},{3,1},{4,6},{5,7},{6,4},{7,5},{8,10},{9,11},{10,... | collective-permute-start | bytes 786440 | tf_op jit(solution)/shard_map/ppermute | solution.py:422
  67.8 31.4 %collective-permute-start.10 = (bf16[256,512]{1,0:T(8,128)(2,1)S(1)}, bf16[256,512]{1,0:T(8,128)(2,1)S(1)}, u32[]{:S(2)}, u32[]{:S(2)}) collective-permute-start(bf16[256,512]{1,0:T(8,128)(2,1)S(1)} %fusion.1.c0), channel_id=1, source_target_pairs={{0,1},{1,0},{2,3},{3,2},{4,5},{5,4},{6,7},{7,6},{8,9},{9,8},{10,11... | collective-permute-start | bytes 786440 | tf_op jit(solution)/shard_map/ppermute | solution.py:422
  89.2 13.4 %collective-permute-start.15 = (bf16[256,512]{1,0:T(8,128)(2,1)S(1)}, bf16[256,512]{1,0:T(8,128)(2,1)S(1)}, u32[]{:S(2)}, u32[]{:S(2)}) collective-permute-start(bf16[256,512]{1,0:T(8,128)(2,1)S(1)} %collective-permute-done.14.c0), channel_id=1, source_target_pairs={{0,1},{1,0},{2,3},{3,2},{4,5},{5,4},{6,7},{7,6},{8,9},{9,8},{10,11... | collective-permute-start | bytes 786440 | tf_op jit(solution)/shard_map/ppermute | solution.py:422
  94.9 12.1 %collective-permute-start.7 = (bf16[256,512]{1,0:T(8,128)(2,1)S(1)}, bf16[256,512]{1,0:T(8,128)(2,1)S(1)}, u32[]{:S(2)}, u32[]{:S(2)}) collective-permute-start(bf16[256,512]{1,0:T(8,128)(2,1)S(1)} %collective-permute-done.6.c0), channel_id=1, source_target_pairs={{0,1},{1,0},{2,3},{3,2},{4,5},{5,4},{6,7},{7,6},{8,9},{9,8},{10,11... | collective-permute-start | bytes 786440 | tf_op jit(solution)/shard_map/ppermute | solution.py:422
  102.6 1.0 copy-start

commit v6 on v5

--- a/solution.py
+++ b/solution.py
@@ -431,6 +431,30 @@
     return lax.ppermute(block, axes, route)
 
 
+def end_plane(s):
+    return s % Z_CHIPS in (0, Z_CHIPS - 1)
+
+
+def within_planes(block, flip):
+    axes = ("seq", *HEAD)
+    seqs = [s for s in range(lax.axis_size("seq")) if not end_plane(s)]
+    return lax.ppermute(
+        block, axes, [(s * 4 + h, s * 4 + (h ^ flip)) for s in seqs for h in range(4)]
+    )
+
+
+def to_end_planes(block, flip):
+    axes = ("seq", *HEAD)
+    route = []
+    for s in range(lax.axis_size("seq")):
+        if end_plane(s):
+            inward = 1 if s % Z_CHIPS == 0 else -1
+            for h in range(4):
+                source = s + inward * (1 + h % 2)
+                route.append((source * 4 + (h ^ flip), s * 4 + h))
+    return lax.ppermute(block, axes, route)
+
+
 def body(
     encoder_queries,
     encoder_keys,
@@ -458,7 +482,8 @@
     q_beside = exchanged(decoder_queries, 0)
     q_beyond = exchanged(decoder_queries, 1)
     across2, across3, across1 = cut_call(part, out_weight, columns)
-    w2 = swapped(across2, 2)
+    w2_end = to_end_planes(across2, 2)
+    w2 = within_planes(across2, 2)
     w3 = other_side(across3, 3)
     w1 = swapped(across1, 1)
     encoder_args = (position, block_counts, lists, encoder_queries, k3, v3)
@@ -473,12 +498,20 @@
         returned.append((from_beside, from_beyond))
     own = serve_call(*tables, [decoder_queries])
     tokens = decoder_input.shape[0]
+    contexts = [own[i] + returned[i][0] + returned[i][1] for i in range(PARTS)]
     decoder_out = None
-    for i in range(PARTS):
-        context = own[i] + returned[i][0] + returned[i][1]
+    exchanges = []
+    for context in contexts:
         across = swapped(context, 2)
         aside = swapped(context, 1)
         corner = swapped(across, 1)
+        exchanges.append((aside, across, corner))
+    aside, across, corner = exchanges[-1]
+    w2, w2_end, aside = lax.optimization_barrier((w2, w2_end, aside))
+    exchanges[-1] = (aside, across, corner)
+    w2 = w2 + w2_end
+    for i, context in enumerate(contexts):
+        aside, across, corner = exchanges[i]
         total = project_call(
             part, [context, aside], [out_weight, w1], decoder_input, jnp.float32, i, tokens // PARTS
         )

time: 111 us -> 123 us (1.11)
  the two profiles are of different devices: /device:TPU:23 before, /device:TPU:24 now
where the time goes in v6:
time: 123 us; the launch traced here: 121 us
  Pallas kernels  43.7 us (36%)
  waiting for transfers between devices  38.5 us (31%)
  starting transfers between devices  32.1 us (26%)
  other arithmetic  4.91 us (4%)
    ppermute x8, waiting for transfers between devices, exchanged(): return lax.ppermute(block, 'seq', route)  26.7 us
    ppermute x8, starting transfers between devices, exchanged(): return lax.ppermute(block, 'seq', route)  25.9 us
    pallas_call x4, Pallas kernels, project_call(): pl.pallas_call(project_kernel, grid_spec=pltpu.PrefetchScalarGridSpec(num...  13.4 us
    ppermute x7, waiting for transfers between devices, swapped(): return lax.ppermute(block, HEAD, [(i, i ^ flip) for i in range(4)])  11.8 us
    pallas_call x2, Pallas kernels, serve_call(): pl.pallas_call(serve_kernel, in_specs=[smem] * 3 + [hbm] * 2 + [vmem if s...  9.76 us
    pallas_call x1, Pallas kernels, encoder_call(): pl.pallas_call(inner_kernel, in_specs=[smem] * 3 + [hbm] * 3, out_specs=h...  9.54 us
    pallas_call x1, Pallas kernels, encoder_call(): pl.pallas_call(edge_kernel, in_specs=[smem] * 3 + [hbm] * 3 + [pl.BlockSp...  5.77 us
    ppermute x7, starting transfers between devices, swapped(): return lax.ppermute(block, HEAD, [(i, i ^ flip) for i in range(4)])  3.21 us
  transfers between devices with their start and end apart: 18, of which 6 were waited for; matrix products, arithmetic and copies ran while one was open for 4% of the time, Pallas kernels for 31%

profile of v6, /device:TPU:24, one launch (start us, length us, event | category | flops | bytes accessed | tf_op | source)
XLA Modules:
  0.0 121.0 jit_solution(14593441405400168928)
XLA Ops:
  0.6 2.2 %pack_edges.1 = (bf16[512,512]{1,0:T(8,128)(2,1)}, bf16[512,512]{1,0:T(8,128)(2,1)}) custom-call(s32[1]{0:T(128)} %bitcast.pos, bf16[1536,512]{1,0:T(8,128)(2,1)} %k.1, bf16[1536,512]{1,0:T(8,128)(2,1)} %v.1), custom_call_target="tpu_custom_call" | custom-call | tf_op jit(solution)/shard_map/pack_edges/pallas_call | solution.py:87
  2.9 2.0 %collective-permute-start = (bf16[512,512]{1,0:T(8,128)(2,1)}, bf16[512,512]{1,0:T(8,128)(2,1)S(1)}, u32[]{:S(2)}, u32[]{:S(2)}) collective-permute-start(bf16[512,512]{1,0:T(8,128)(2,1)} %get-tuple-element.16), channel_id=1, source_target_pairs={{0,4},{4,0},{8,12},{12,8},{16,20},{20,16},{24,28},{28,24},{32,36},... | collective-permute-start | bytes 1572872 | tf_op jit(solution)/shard_map/ppermute | solution.py:418
  4.9 9.5 %collective-permute-start.1 = (bf16[512,512]{1,0:T(8,128)(2,1)}, bf16[512,512]{1,0:T(8,128)(2,1)S(1)}, u32[]{:S(2)}, u32[]{:S(2)}) collective-permute-start(bf16[512,512]{1,0:T(8,128)(2,1)} %get-tuple-element.17), channel_id=1, source_target_pairs={{4,8},{8,4},{12,16},{16,12},{20,24},{24,20},{28,32},{32,28},{36,40... | collective-permute-start | bytes 1572872 | tf_op jit(solution)/shard_map/ppermute | solution.py:418
  14.5 3.9 %collective-permute-start.3 = (bf16[512,512]{1,0:T(8,128)(2,1)S(1)}, bf16[512,512]{1,0:T(8,128)(2,1)S(1)}, u32[]{:S(2)}, u32[]{:S(2)}) collective-permute-start(bf16[512,512]{1,0:T(8,128)(2,1)S(1)} %copy-done.1), channel_id=1, source_target_pairs={{4,8},{8,4},{12,16},{16,12},{20,24},{24,20},{28,32},{32,28},{36,40... | collective-permute-start | bytes 1572872 | tf_op jit(solution)/shard_map/ppermute | solution.py:418
  18.4 2.9 %cut_weight.1 = (bf16[512,1024]{1,0:T(8,128)(2,1)}, bf16[512,1024]{1,0:T(8,128)(2,1)}, bf16[512,1024]{1,0:T(8,128)(2,1)}) custom-call(s32[1]{0:T(128)} %bitcast.8.part, bf16[512,4096]{1,0:T(8,128)(2,1)} %w0.3), custom_call_target="tpu_custom_call" | custom-call | tf_op jit(solution)/shard_map/cut_weight/pallas_call | solution.py:367
  21.3 1.6 %collective-permute-start.8 = (bf16[512,1024]{1,0:T(8,128)(2,1)}, bf16[512,1024]{1,0:T(8,128)(2,1)}, u32[]{:S(2)}, u32[]{:S(2)}) collective-permute-start(bf16[512,1024]{1,0:T(8,128)(2,1)} %get-tuple-element.21), channel_id=1, source_target_pairs={{4,6},{5,7},{6,4},{7,5},{8,10},{9,11},{10,8},{11,9},{12,14},{13,15... | collective-permute-start | bytes 3145736 | tf_op jit(solution)/shard_map/ppermute | solution.py:441
  23.0 9.5 %encoder_inner.1._ = bf16[12,128,512]{2,1,0:T(8,128)(2,1)} custom-call(s32[1]{0:T(128)} %bitcast.pos, s32[12]{0:T(128)} %counts.3, s32[4,12]{1,0:T(4,128)} %bitcast.41, bf16[12,128,512]{2,1,0:T(8,128)(2,1)} %bitcast.36, bf16[12,128,512]{2,1,0:T(8,128)(2,1)} %bitcast.29, bf16[12,128,512]{2,1,0:T(8,128)(2,1)} %bitcast.34), custom_call_target="tpu_custom_call" | custom-call | tf_op jit(solution)/shard_map/encoder_inner/pallas_call | solution.py:210
  32.5 5.8 %encoder_edge.1.e = bf16[12,128,512]{2,1,0:T(8,128)(2,1)} custom-call(s32[1]{0:T(128)} %bitcast.pos, s32[12]{0:T(128)} %counts.3, s32[4,12]{1,0:T(4,128)} %bitcast.42, bf16[12,128,512]{2,1,0:T(8,128)(2,1)} %bitcast.37, bf16[12,128,512]{2,1,0:T(8,128)(2,1)} %bitcast.30, bf16[12,128,512]{2,1,0:T(8,128)(2,1)} %bitcast.35, ...), custom_call_target="tpu_custom_call", output_to_operand_aliasing={{}: (8, {})} | custom-call | tf_op jit(solution)/shard_map/encoder_edge/pallas_call | solution.py:219
  38.3 6.4 %shard_map.114 = (bf16[2,128,512]{2,1,0:T(8,128)(2,1)}, bf16[2,128,512]{2,1,0:T(8,128)(2,1)}, bf16[2,128,512]{2,1,0:T(8,128)(2,1)}, bf16[2,128,512]{2,1,0:T(8,128)(2,1)}) custom-call(s32[1]{0:T(128)} %bitcast.pos, s32[256]{0:T(256)} %owners.3, s32[2,256]{1,0:T(2,128)} %bitcast.39, bf16[12,128,512]{2,1,0:T(8,128)(2,1)} %bitcast.31, ...), custom_call_target="tpu_custom_call" | custom-call | tf_op jit(solution)/shard_map/pallas_call | solution.py:317
  44.8 4.9 %collective-permute-start.5 = (bf16[256,512]{1,0:T(8,128)(2,1)}, bf16[256,512]{1,0:T(8,128)(2,1)S(1)}, u32[]{:S(2)}, u32[]{:S(2)}) collective-permute-start(bf16[256,512]{1,0:T(8,128)(2,1)} %bitcast.46), channel_id=1, source_target_pairs={{4,8},{8,4},{12,16},{16,12},{20,24},{24,20},{28,32},{32,28},{36,40... | collective-permute-start | bytes 786440 | tf_op jit(solution)/shard_map/ppermute | solution.py:418
  49.8 1.3 %collective-permute-start.9 = (bf16[512,1024]{1,0:T(8,128)(2,1)}, bf16[512,1024]{1,0:T(8,128)(2,1)}, u32[]{:S(2)}, u32[]{:S(2)}) collective-permute-start(bf16[512,1024]{1,0:T(8,128)(2,1)} %get-tuple-element.21), channel_id=1, source_target_pairs={{6,0},{11,1},{4,2},{9,3},{26,28},{23,29},{24,30},{21,31},{38,32},{... | collective-permute-start | bytes 3145736 | tf_op jit(solution)/shard_map/ppermute | solution.py:455
  51.1 5.4 %collective-permute-start.14 = (bf16[256,512]{1,0:T(8,128)(2,1)}, bf16[256,512]{1,0:T(8,128)(2,1)S(1)}, u32[]{:S(2)}, u32[]{:S(2)}) collective-permute-start(bf16[256,512]{1,0:T(8,128)(2,1)} %bitcast.44), channel_id=1, source_target_pairs={{4,8},{8,4},{12,16},{16,12},{20,24},{24,20},{28,32},{32,28},{36,40... | collective-permute-start | bytes 786440 | tf_op jit(solution)/shard_map/ppermute | solution.py:418
  56.5 3.5 %collective-permute-done.5 = bf16[256,512]{1,0:T(8,128)(2,1)S(1)} collective-permute-done((bf16[256,512]{1,0:T(8,128)(2,1)}, bf16[256,512]{1,0:T(8,128)(2,1)S(1)}, u32[]{:S(2)}, u32[]{:S(2)}) %collective-permute-start.5) | collective-permute-done | bytes 262176 | tf_op jit(solution)/shard_map/ppermute | solution.py:418
  60.9 9.5 %collective-permute-done.14 = bf16[256,512]{1,0:T(8,128)(2,1)S(1)} collective-permute-done((bf16[256,512]{1,0:T(8,128)(2,1)}, bf16[256,512]{1,0:T(8,128)(2,1)S(1)}, u32[]{:S(2)}, u32[]{:S(2)}) %collective-permute-start.14) | collective-permute-done | bytes 262176 | tf_op jit(solution)/shard_map/ppermute | solution.py:418
  70.4 3.3 %shard_map.113 = (bf16[2,128,512]{2,1,0:T(8,128)(2,1)}, bf16[2,128,512]{2,1,0:T(8,128)(2,1)}) custom-call(s32[1]{0:T(128)} %bitcast.pos, s32[256]{0:T(256)} %owners.3, s32[2,256]{1,0:T(2,128)} %bitcast.40, bf16[12,128,512]{2,1,0:T(8,128)(2,1)} %bitcast.32, bf16[12,128,512]{2,1,0:T(8,128)(2,1)} %encoder_edge.1.e, bf16[4,128,512]{2,1,0:T(8,128)(2,1)} %bitcast.38), custom_call_target="tpu_custom_call" | custom-call | tf_op jit(solution)/shard_map/pallas_call | solution.py:317
  74.7 12.9 %collective-permute-done.13 = bf16[256,512]{1,0:T(8,128)(2,1)S(1)} collective-permute-done((bf16[256,512]{1,0:T(8,128)(2,1)}, bf16[256,512]{1,0:T(8,128)(2,1)S(1)}, u32[]{:S(2)}, u32[]{:S(2)}) %collective-permute-start.13) | collective-permute-done | bytes 262176 | tf_op jit(solution)/shard_map/ppermute | solution.py:418
  87.6 1.4 %collective-permute-start.6 = (bf16[256,512]{1,0:T(8,128)(2,1)S(1)}, bf16[256,512]{1,0:T(8,128)(2,1)S(1)}, u32[]{:S(2)}, u32[]{:S(2)}) collective-permute-start(bf16[256,512]{1,0:T(8,128)(2,1)S(1)} %fusion.1.c0), channel_id=1, source_target_pairs={{0,2},{1,3},{2,0},{3,1},{4,6},{5,7},{6,4},{7,5},{8,10},{9,11},{10,... | collective-permute-start | bytes 786440 | tf_op jit(solution)/shard_map/ppermute | solution.py:422
  90.1 6.7 %collective-permute-done.6.c0 = bf16[256,512]{1,0:T(8,128)(2,1)S(1)} collective-permute-done((bf16[256,512]{1,0:T(8,128)(2,1)S(1)}, bf16[256,512]{1,0:T(8,128)(2,1)S(1)}, u32[]{:S(2)}, u32[]{:S(2)}) %collective-permute-start.6) | collective-permute-done | bytes 262176 | tf_op jit(solution)/shard_map/ppermute | solution.py:422
  98.0 5.1 %collective-permute-done.15.c0 = bf16[256,512]{1,0:T(8,128)(2,1)S(1)} collective-permute-done((bf16[256,512]{1,0:T(8,128)(2,1)S(1)}, bf16[256,512]{1,0:T(8,128)(2,1)S(1)}, u32[]{:S(2)}, u32[]{:S(2)}) %collective-permute-start.15) | collective-permute-done | bytes 262176 | tf_op jit(solution)/shard_map/ppermute | solution.py:422
  103.6 2.9 %add.21.w0 = bf16[512,1024]{1,0:T(8,128)(2,1)} add(bf16[512,1024]{1,0:T(8,128)(2,1)} %collective-permute-done.8, bf16[512,1024]{1,0:T(8,128)(2,1)} %collective-permute-done.9) | non-fusion elementwise | flops 524288 | bytes 3145728 | tf_op jit(solution)/shard_map/add | solution.py:512
  107.5 3.4 %shard_map.115.r_ref = f32[256,1024]{1,0:T(8,128)} custom-call(s32[1]{0:T(128)} %bitcast.8.part, bf16[256,512]{1,0:T(8,128)(2,1)S(1)} %fusion.1.c0, bf16[256,512]{1,0:T(8,128)(2,1)S(1)} %collective-permute-done.10.c1, bf16[512,4096]{1,0:T(8,128)(2,1)} %w0.3, bf16[512,1024]{1,0:T(8,128)(2,1)} %copy-done, bf16[512,1024]{1,0:T(8,128)(2,1)} %r_ref.3), custom_call_target="tpu_custom_call" | custom-call | tf_op jit(solution)/shard_map/pallas_call | solution.py:398
  110.9 3.4 %shard_map.116.r_ref = f32[256,1024]{1,0:T(8,128)} custom-call(s32[1]{0:T(128)} %bitcast.8.part, bf16[256,512]{1,0:T(8,128)(2,1)S(1)} %fusion.c0, bf16[256,512]{1,0:T(8,128)(2,1)S(1)} %collective-permute-done.17.c1, bf16[512,4096]{1,0:T(8,128)(2,1)} %w0.3, bf16[512,1024]{1,0:T(8,128)(2,1)} %copy-done, bf16[512,1024]{1,0:T(8,128)(2,1)} %r_ref.3), custom_call_target="tpu_custom_call" | custom-call | tf_op jit(solution)/shard_map/pallas_call | solution.py:398
  114.2 3.4 %shard_map.117.refs_0_ = bf16[512,1024]{1,0:T(8,128)(2,1)} custom-call(s32[1]{0:T(128)} %bitcast.8.part, bf16[256,512]{1,0:T(8,128)(2,1)S(1)} %collective-permute-done.15.c0, bf16[256,512]{1,0:T(8,128)(2,1)S(1)} %collective-permute-done.16.c1, bf16[512,1024]{1,0:T(8,128)(2,1)} %add.21.w0, bf16[512,1024]{1,0:T(8,128)(2,1)} %collective-permute-done.11.w1, ...), custom_call_target="tpu_custom_call" | custom-call | tf_op jit(solution)/shard_map/pallas_call | solution.py:398
  117.6 3.4 %shard_map.118 = bf16[512,1024]{1,0:T(8,128)(2,1)} custom-call(s32[1]{0:T(128)} %bitcast.8.part, bf16[256,512]{1,0:T(8,128)(2,1)S(1)} %collective-permute-done.6.c0, bf16[256,512]{1,0:T(8,128)(2,1)S(1)} %collective-permute-done.7.c1, bf16[512,1024]{1,0:T(8,128)(2,1)} %add.21.w0, ...), custom_call_target="tpu_custom_call", output_to_operand_aliasing={{}: (6, {})} | custom-call | tf_op jit(solution)/shard_map/pallas_call | solution.py:398
  (29 shorter events, 5.8 us)
Async XLA Ops:
  0.6 13.7 %copy-start.1 = (bf16[512,512]{1,0:T(8,128)(2,1)S(1)}, bf16[512,512]{1,0:T(8,128)(2,1)}, u32[]{:S(2)}) copy-start(bf16[512,512]{1,0:T(8,128)(2,1)} %param.15) | copy-start | bytes 1572868
  2.9 29.6 %collective-permute-start = (bf16[512,512]{1,0:T(8,128)(2,1)}, bf16[512,512]{1,0:T(8,128)(2,1)S(1)}, u32[]{:S(2)}, u32[]{:S(2)}) collective-permute-start(bf16[512,512]{1,0:T(8,128)(2,1)} %get-tuple-element.16), channel_id=1, source_target_pairs={{0,4},{4,0},{8,12},{12,8},{16,20},{20,16},{24,28},{28,24},{32,36},... | collective-permute-start | bytes 1572872 | tf_op jit(solution)/shard_map/ppermute | solution.py:418
  4.9 27.6 %collective-permute-start.1 = (bf16[512,512]{1,0:T(8,128)(2,1)}, bf16[512,512]{1,0:T(8,128)(2,1)S(1)}, u32[]{:S(2)}, u32[]{:S(2)}) collective-permute-start(bf16[512,512]{1,0:T(8,128)(2,1)} %get-tuple-element.17), channel_id=1, source_target_pairs={{4,8},{8,4},{12,16},{16,12},{20,24},{24,20},{28,32},{32,28},{36,40... | collective-permute-start | bytes 1572872 | tf_op jit(solution)/shard_map/ppermute | solution.py:418
  14.4 23.9 %collective-permute-start.2 = (bf16[512,512]{1,0:T(8,128)(2,1)S(1)}, bf16[512,512]{1,0:T(8,128)(2,1)S(1)}, u32[]{:S(2)}, u32[]{:S(2)}) collective-permute-start(bf16[512,512]{1,0:T(8,128)(2,1)S(1)} %copy-done.1), channel_id=1, source_target_pairs={{0,4},{4,0},{8,12},{12,8},{16,20},{20,16},{24,28},{28,24},{32,36},... | collective-permute-start | bytes 1572872 | tf_op jit(solution)/shard_map/ppermute | solution.py:418
  14.5 23.8 %collective-permute-start.3 = (bf16[512,512]{1,0:T(8,128)(2,1)S(1)}, bf16[512,512]{1,0:T(8,128)(2,1)S(1)}, u32[]{:S(2)}, u32[]{:S(2)}) collective-permute-start(bf16[512,512]{1,0:T(8,128)(2,1)S(1)} %copy-done.1), channel_id=1, source_target_pairs={{4,8},{8,4},{12,16},{16,12},{20,24},{24,20},{28,32},{32,28},{36,40... | collective-permute-start | bytes 1572872 | tf_op jit(solution)/shard_map/ppermute | solution.py:418
  21.3 76.2 %collective-permute-start.8 = (bf16[512,1024]{1,0:T(8,128)(2,1)}, bf16[512,1024]{1,0:T(8,128)(2,1)}, u32[]{:S(2)}, u32[]{:S(2)}) collective-permute-start(bf16[512,1024]{1,0:T(8,128)(2,1)} %get-tuple-element.21), channel_id=1, source_target_pairs={{4,6},{5,7},{6,4},{7,5},{8,10},{9,11},{10,8},{11,9},{12,14},{13,15... | collective-permute-start | bytes 3145736 | tf_op jit(solution)/shard_map/ppermute | solution.py:441
  44.8 15.3 %collective-permute-start.5 = (bf16[256,512]{1,0:T(8,128)(2,1)}, bf16[256,512]{1,0:T(8,128)(2,1)S(1)}, u32[]{:S(2)}, u32[]{:S(2)}) collective-permute-start(bf16[256,512]{1,0:T(8,128)(2,1)} %bitcast.46), channel_id=1, source_target_pairs={{4,8},{8,4},{12,16},{16,12},{20,24},{24,20},{28,32},{32,28},{36,40... | collective-permute-start | bytes 786440 | tf_op jit(solution)/shard_map/ppermute | solution.py:418
  49.7 11.2 %collective-permute-start.4 = (bf16[256,512]{1,0:T(8,128)(2,1)}, bf16[256,512]{1,0:T(8,128)(2,1)S(1)}, u32[]{:S(2)}, u32[]{:S(2)}) collective-permute-start(bf16[256,512]{1,0:T(8,128)(2,1)} %bitcast.45), channel_id=1, source_target_pairs={{0,4},{4,0},{8,12},{12,8},{16,20},{20,16},{24,28},{28,24},{32,36},... | collective-permute-start | bytes 786440 | tf_op jit(solution)/shard_map/ppermute | solution.py:418
  49.8 47.7 %collective-permute-start.9 = (bf16[512,1024]{1,0:T(8,128)(2,1)}, bf16[512,1024]{1,0:T(8,128)(2,1)}, u32[]{:S(2)}, u32[]{:S(2)}) collective-permute-start(bf16[512,1024]{1,0:T(8,128)(2,1)} %get-tuple-element.21), channel_id=1, source_target_pairs={{6,0},{11,1},{4,2},{9,3},{26,28},{23,29},{24,30},{21,31},{38,32},{... | collective-permute-start | bytes 3145736 | tf_op jit(solution)/shard_map/ppermute | solution.py:455
  51.1 19.3 %collective-permute-start.14 = (bf16[256,512]{1,0:T(8,128)(2,1)}, bf16[256,512]{1,0:T(8,128)(2,1)S(1)}, u32[]{:S(2)}, u32[]{:S(2)}) collective-permute-start(bf16[256,512]{1,0:T(8,128)(2,1)} %bitcast.44), channel_id=1, source_target_pairs={{4,8},{8,4},{12,16},{16,12},{20,24},{24,20},{28,32},{32,28},{36,40... | collective-permute-start | bytes 786440 | tf_op jit(solution)/shard_map/ppermute | solution.py:418
  60.0 46.5 %collective-permute-start.12 = (bf16[512,1024]{1,0:T(8,128)(2,1)}, bf16[512,1024]{1,0:T(8,128)(2,1)S(1)}, u32[]{:S(2)}, u32[]{:S(2)}) collective-permute-start(bf16[512,1024]{1,0:T(8,128)(2,1)} %get-tuple-element.26), channel_id=1, source_target_pairs={{0,1},{1,0},{2,3},{3,2},{4,5},{5,4},{6,7},{7,6},{8,9},{9,8},{10,11... | collective-permute-start | bytes 3145736 | tf_op jit(solution)/shard_map/ppermute | solution.py:422
  60.9 26.7 %collective-permute-start.13 = (bf16[256,512]{1,0:T(8,128)(2,1)}, bf16[256,512]{1,0:T(8,128)(2,1)S(1)}, u32[]{:S(2)}, u32[]{:S(2)}) collective-permute-start(bf16[256,512]{1,0:T(8,128)(2,1)} %bitcast.43), channel_id=1, source_target_pairs={{0,4},{4,0},{8,12},{12,8},{16,20},{20,16},{24,28},{28,24},{32,36},... | collective-permute-start | bytes 786440 | tf_op jit(solution)/shard_map/ppermute | solution.py:418
  70.4 43.8 %collective-permute-start.11 = (bf16[512,1024]{1,0:T(8,128)(2,1)}, bf16[512,1024]{1,0:T(8,128)(2,1)}, u32[]{:S(2)}, u32[]{:S(2)}) collective-permute-start(bf16[512,1024]{1,0:T(8,128)(2,1)} %get-tuple-element.24), channel_id=1, source_target_pairs={{0,35},{1,34},{2,33},{3,32},{4,39},{5,38},{6,37},{7,36},{8,43},{9,... | collective-permute-start | bytes 3145736 | tf_op jit(solution)/shard_map/ppermute | solution.py:431
  87.6 9.1 %collective-permute-start.6 = (bf16[256,512]{1,0:T(8,128)(2,1)S(1)}, bf16[256,512]{1,0:T(8,128)(2,1)S(1)}, u32[]{:S(2)}, u32[]{:S(2)}) collective-permute-start(bf16[256,512]{1,0:T(8,128)(2,1)S(1)} %fusion.1.c0), channel_id=1, source_target_pairs={{0,2},{1,3},{2,0},{3,1},{4,6},{5,7},{6,4},{7,5},{8,10},{9,11},{10,... | collective-permute-start | bytes 786440 | tf_op jit(solution)/shard_map/ppermute | solution.py:422
  96.7 6.4 %collective-permute-start.15 = (bf16[256,512]{1,0:T(8,128)(2,1)S(1)}, bf16[256,512]{1,0:T(8,128)(2,1)S(1)}, u32[]{:S(2)}, u32[]{:S(2)}) collective-permute-start(bf16[256,512]{1,0:T(8,128)(2,1)S(1)} %fusion.c0), channel_id=1, source_target_pairs={{0,2},{1,3},{2,0},{3,1},{4,6},{5,7},{6,4},{7,5},{8,10},{9,11},{10,... | collective-permute-start | bytes 786440 | tf_op jit(solution)/shard_map/ppermute | solution.py:422
  97.5 5.6 %collective-permute-start.10 = (bf16[256,512]{1,0:T(8,128)(2,1)S(1)}, bf16[256,512]{1,0:T(8,128)(2,1)S(1)}, u32[]{:S(2)}, u32[]{:S(2)}) collective-permute-start(bf16[256,512]{1,0:T(8,128)(2,1)S(1)} %fusion.1.c0), channel_id=1, source_target_pairs={{0,1},{1,0},{2,3},{3,2},{4,5},{5,4},{6,7},{7,6},{8,9},{9,8},{10,11... | collective-permute-start | bytes 786440 | tf_op jit(solution)/shard_map/ppermute | solution.py:422
  97.5 13.4 %collective-permute-start.17 = (bf16[256,512]{1,0:T(8,128)(2,1)S(1)}, bf16[256,512]{1,0:T(8,128)(2,1)S(1)}, u32[]{:S(2)}, u32[]{:S(2)}) collective-permute-start(bf16[256,512]{1,0:T(8,128)(2,1)S(1)} %fusion.c0), channel_id=1, source_target_pairs={{0,1},{1,0},{2,3},{3,2},{4,5},{5,4},{6,7},{7,6},{8,9},{9,8},{10,11... | collective-permute-start | bytes 786440 | tf_op jit(solution)/shard_map/ppermute | solution.py:422
  103.1 11.1 %collective-permute-start.16 = (bf16[256,512]{1,0:T(8,128)(2,1)S(1)}, bf16[256,512]{1,0:T(8,128)(2,1)S(1)}, u32[]{:S(2)}, u32[]{:S(2)}) collective-permute-start(bf16[256,512]{1,0:T(8,128)(2,1)S(1)} %collective-permute-done.15.c0), channel_id=1, source_target_pairs={{0,1},{1,0},{2,3},{3,2},{4,5},{5,4},{6,7},{7,6},{8,9},{9,8},{10,11... | collective-permute-start | bytes 786440 | tf_op jit(solution)/shard_map/ppermute | solution.py:422
  103.1 14.5 %collective-permute-start.7 = (bf16[256,512]{1,0:T(8,128)(2,1)S(1)}, bf16[256,512]{1,0:T(8,128)(2,1)S(1)}, u32[]{:S(2)}, u32[]{:S(2)}) collective-permute-start(bf16[256,512]{1,0:T(8,128)(2,1)S(1)} %collective-permute-done.6.c0), channel_id=1, source_target_pairs={{0,1},{1,0},{2,3},{3,2},{4,5},{5,4},{6,7},{7,6},{8,9},{9,8},{10,11... | collective-permute-start | bytes 786440 | tf_op jit(solution)/shard_map/ppermute | solution.py:422
  106.5 1.0 copy-start

commit v7 on v5

--- a/solution.py
+++ b/solution.py
@@ -1,3 +1,5 @@
+import functools
+
 import jax
 import jax.numpy as jnp
 from jax import lax
@@ -14,6 +16,7 @@
 CROSS = 2
 QUAD = 4
 PARTS = 2
+ANSWERS = 1
 Z_CHIPS = 8
 QW = HD * QUAD
 HEAD = ("head_0", "head_1")
@@ -228,10 +231,10 @@
 
 
 def serve_kernel(pos, owners, slots, k, e, *refs):
-    sources = (len(refs) - 6) // (1 + PARTS)
+    sources = (len(refs) - 6) // (1 + ANSWERS)
     queries = refs[:sources]
-    answers = refs[sources : (1 + PARTS) * sources]
-    kb, eb, qb, ob, load_sems, answer_sem = refs[(1 + PARTS) * sources :]
+    answers = refs[sources : (1 + ANSWERS) * sources]
+    kb, eb, qb, ob, load_sems, answer_sem = refs[(1 + ANSWERS) * sources :]
     mine = pos[0]
     per = queries[0].shape[0]
     total = owners.shape[0] // per
@@ -267,13 +270,13 @@
                 for copy in loads(i, t, s0, s1):
                     copy.start()
 
-    share = per // PARTS
+    share = per // ANSWERS
 
     def answer(part, i):
         rows = ob.at[pl.ds(i * per + part * share, share)]
         return pltpu.make_async_copy(rows, answers[part * sources + i], answer_sem)
 
-    for part in range(PARTS):
+    for part in range(ANSWERS):
         for i in range(sources):
 
             @pl.loop(part * share, (part + 1) * share)
@@ -298,7 +301,7 @@
 
             answer(part, i).start()
 
-    for part in range(PARTS):
+    for part in range(ANSWERS):
         for i in range(sources):
             answer(part, i).wait()
 
@@ -317,9 +320,9 @@
     out = pl.pallas_call(
         serve_kernel,
         in_specs=[smem] * 3 + [hbm] * 2 + [vmem if sources > 1 else hbm] * sources,
-        out_specs=[hbm] * (sources * PARTS),
-        out_shape=[jax.ShapeDtypeStruct((per // PARTS, BLK, width), jnp.bfloat16)]
-        * (sources * PARTS),
+        out_specs=[hbm] * (sources * ANSWERS),
+        out_shape=[jax.ShapeDtypeStruct((per // ANSWERS, BLK, width), jnp.bfloat16)]
+        * (sources * ANSWERS),
         scratch_shapes=[
             pltpu.VMEM((served, CROSS, BLK, width), jnp.bfloat16),
             pltpu.VMEM((served, CROSS, BLK, width), jnp.bfloat16),
@@ -352,33 +355,45 @@
         store.wait()
 
 
-def cut_kernel(part, w, a, b, c, sa, sb, sc, load_sem, store_sem):
+def cut_kernel(part, w, a, b, c, d, sa, sb, sc, sd, load_sem, store_sem):
     columns = a.shape[1]
+    split = a.shape[0]
     plan = []
-    for flip, dst in ((2, a), (3, b), (1, c)):
+    for flip, rows, dst in (
+        (2, pl.ds(0, split), a),
+        (2, pl.ds(split, w.shape[0] - split), b),
+        (3, pl.ds(0, w.shape[0]), c),
+        (1, pl.ds(0, w.shape[0]), d),
+    ):
         start = pl.multiple_of((part[0] ^ flip) * columns, columns)
-        plan.append((w.at[:, pl.ds(start, columns)], dst))
-    move(plan, (sa, sb, sc), load_sem, store_sem)
+        plan.append((w.at[rows, pl.ds(start, columns)], dst))
+    move(plan, (sa, sb, sc, sd), load_sem, store_sem)
 
 
 def cut_call(part, w, columns):
-    shape = jax.ShapeDtypeStruct((w.shape[0], columns), w.dtype)
+    rows = w.shape[0]
+    split = rows * 3 // 4
+    shapes = [(n, columns) for n in (split, rows - split, rows, rows)]
     hbm = pl.BlockSpec(memory_space=pl.ANY)
     return pl.pallas_call(
         cut_kernel,
         in_specs=[pl.BlockSpec(memory_space=pltpu.SMEM), hbm],
-        out_specs=[hbm] * 3,
-        out_shape=[shape] * 3,
-        scratch_shapes=[pltpu.VMEM(shape.shape, w.dtype)] * 3
-        + [pltpu.SemaphoreType.DMA((3,)), pltpu.SemaphoreType.DMA],
+        out_specs=[hbm] * 4,
+        out_shape=[jax.ShapeDtypeStruct(x, w.dtype) for x in shapes],
+        scratch_shapes=[pltpu.VMEM(x, w.dtype) for x in shapes]
+        + [pltpu.SemaphoreType.DMA((4,)), pltpu.SemaphoreType.DMA],
         name="cut_weight",
     )(part, w)
 
 
-def project_kernel(part, c0, c1, w0, w1, r_ref, *refs):
+def project_kernel(counts, part, c0, c1, *refs):
+    first, second = counts
+    weights = refs[: first + second]
+    r_ref = refs[first + second]
     total = r_ref[...].astype(jnp.float32)
-    for c, w in ((c0, w0), (c1, w1)):
-        total = total + jnp.dot(c[...], w[...], preferred_element_type=jnp.float32)
+    for c, ws in ((c0, weights[:first]), (c1, weights[first:])):
+        w = jnp.concatenate([x[...] for x in ws], axis=0) if len(ws) > 1 else ws[0][...]
+        total = total + jnp.dot(c[...], w, preferred_element_type=jnp.float32)
     refs[-1][...] = total.astype(refs[-1].dtype)
 
 
@@ -388,15 +403,16 @@
     here = index if added.shape[0] > tokens else 0
     there = index if out_tokens > tokens else 0
     c_spec = pl.BlockSpec((tokens, width), lambda i, p: (0, 0))
+    flat = [w for ws in weights for w in ws]
     w_specs = [
-        pl.BlockSpec((width, columns), lambda i, p: (0, p[0]))
+        pl.BlockSpec((w.shape[0], columns), lambda i, p: (0, p[0]))
         if w.shape[1] > columns
-        else pl.BlockSpec((width, columns), lambda i, p: (0, 0))
-        for w in weights
+        else pl.BlockSpec((w.shape[0], columns), lambda i, p: (0, 0))
+        for w in flat
     ]
     more = [] if earlier is None else [earlier]
     return pl.pallas_call(
-        project_kernel,
+        functools.partial(project_kernel, tuple(len(ws) for ws in weights)),
         grid_spec=pltpu.PrefetchScalarGridSpec(
             num_scalar_prefetch=1,
             grid=(1,),
@@ -407,8 +423,8 @@
             out_specs=pl.BlockSpec((tokens, columns), lambda i, p: (there, 0)),
         ),
         out_shape=jax.ShapeDtypeStruct((out_tokens, columns), dtype),
-        input_output_aliases={6: 0} if more else {},
-    )(part, *[in_vmem(c) for c in contexts], *weights, added, *more)
+        input_output_aliases={4 + len(flat): 0} if more else {},
+    )(part, *[in_vmem(c) for c in contexts], *flat, added, *more)
 
 
 def exchanged(block, first):
@@ -457,8 +473,9 @@
     beyond = exchanged(beyond, 1)
     q_beside = exchanged(decoder_queries, 0)
     q_beyond = exchanged(decoder_queries, 1)
-    across2, across3, across1 = cut_call(part, out_weight, columns)
-    w2 = swapped(across2, 2)
+    across2, around2, across3, across1 = cut_call(part, out_weight, columns)
+    w2_most = swapped(across2, 2)
+    w2_rest = other_side(around2, 2)
     w3 = other_side(across3, 3)
     w1 = swapped(across1, 1)
     encoder_args = (position, block_counts, lists, encoder_queries, k3, v3)
@@ -466,24 +483,30 @@
     e3 = encoder_call(*encoder_args, edges=(beside, beyond, partial))
     tables = (position, span_owner, slots, k3, e3)
     answers = serve_call(*tables, [q_beside, q_beyond])
-    returned = []
-    for i in range(PARTS):
-        from_beside = exchanged(answers[2 * i], 0)
-        from_beyond = exchanged(answers[2 * i + 1], 1)
-        returned.append((from_beside, from_beyond))
-    own = serve_call(*tables, [decoder_queries])
+    from_beside = exchanged(answers[0], 0)
+    from_beyond = exchanged(answers[1], 1)
+    (own,) = serve_call(*tables, [decoder_queries])
     tokens = decoder_input.shape[0]
+    share = tokens // PARTS
     decoder_out = None
     for i in range(PARTS):
-        context = own[i] + returned[i][0] + returned[i][1]
+        rows = slice(i * share, (i + 1) * share)
+        context = own[rows] + from_beside[rows] + from_beyond[rows]
         across = swapped(context, 2)
         aside = swapped(context, 1)
         corner = swapped(across, 1)
         total = project_call(
-            part, [context, aside], [out_weight, w1], decoder_input, jnp.float32, i, tokens // PARTS
+            part, [context, aside], [[out_weight], [w1]], decoder_input, jnp.float32, i, share
         )
         decoder_out = project_call(
-            part, [across, corner], [w2, w3], total, jnp.bfloat16, i, tokens, decoder_out
+            part,
+            [across, corner],
+            [[in_vmem(w2_most), in_vmem(w2_rest)], [w3]],
+            total,
+            jnp.bfloat16,
+            i,
+            tokens,
+            decoder_out,
         )
     return (e3.reshape(blocks * BLK, width), decoder_out)
 

time: 111 us -> 104 us (0.937)
  the two profiles are of different devices: /device:TPU:23 before, /device:TPU:21 now
where the time goes in v7:
time: 104 us; the launch traced here: 103 us
  Pallas kernels  39.6 us (38%)
  waiting for transfers between devices  31.1 us (30%)
  starting transfers between devices  30.4 us (29%)
  local copies, waits for them, and re-layouts  1.12 us (1%)
    ppermute x8, waiting for transfers between devices, swapped(): return lax.ppermute(block, HEAD, [(i, i ^ flip) for i in range(4)])  26.2 us
    ppermute x6, starting transfers between devices, exchanged(): return lax.ppermute(block, 'seq', route)  18.9 us
    pallas_call x4, Pallas kernels, project_call(): pl.pallas_call(functools.partial(project_kernel, tuple((len(ws) for ws in...  12.8 us
    ppermute x8, starting transfers between devices, swapped(): return lax.ppermute(block, HEAD, [(i, i ^ flip) for i in range(4)])  10.5 us
    pallas_call x1, Pallas kernels, encoder_call(): pl.pallas_call(inner_kernel, in_specs=[smem] * 3 + [hbm] * 3, out_specs=h...  8.63 us
    pallas_call x2, Pallas kernels, serve_call(): pl.pallas_call(serve_kernel, in_specs=[smem] * 3 + [hbm] * 2 + [vmem if s...  7.06 us
    pallas_call x1, Pallas kernels, encoder_call(): pl.pallas_call(edge_kernel, in_specs=[smem] * 3 + [hbm] * 3 + [pl.BlockSp...  5.98 us
    ppermute x6, waiting for transfers between devices, exchanged(): return lax.ppermute(block, 'seq', route)  4.86 us
  transfers between devices with their start and end apart: 16, of which 3 were waited for; matrix products, arithmetic and copies ran while one was open for 1% of the time, Pallas kernels for 28%

profile of v7, /device:TPU:21, one launch (start us, length us, event | category | flops | bytes accessed | tf_op | source)
XLA Modules:
  0.0 103.1 jit_solution(13028808751613939084)
XLA Ops:
  0.6 2.2 %pack_edges.1 = (bf16[512,512]{1,0:T(8,128)(2,1)}, bf16[512,512]{1,0:T(8,128)(2,1)}) custom-call(s32[1]{0:T(128)} %bitcast.pos, bf16[1536,512]{1,0:T(8,128)(2,1)} %k.1, bf16[1536,512]{1,0:T(8,128)(2,1)} %v.1), custom_call_target="tpu_custom_call" | custom-call | tf_op jit(solution)/shard_map/pack_edges/pallas_call | solution.py:90
  2.9 1.7 %collective-permute-start = (bf16[512,512]{1,0:T(8,128)(2,1)}, bf16[512,512]{1,0:T(8,128)(2,1)S(1)}, u32[]{:S(2)}, u32[]{:S(2)}) collective-permute-start(bf16[512,512]{1,0:T(8,128)(2,1)} %get-tuple-element.10), channel_id=1, source_target_pairs={{0,4},{4,0},{8,12},{12,8},{16,20},{20,16},{24,28},{28,24},{32,36},... | collective-permute-start | bytes 1572872 | tf_op jit(solution)/shard_map/ppermute | solution.py:434
  4.6 6.5 %collective-permute-start.1 = (bf16[512,512]{1,0:T(8,128)(2,1)}, bf16[512,512]{1,0:T(8,128)(2,1)S(1)}, u32[]{:S(2)}, u32[]{:S(2)}) collective-permute-start(bf16[512,512]{1,0:T(8,128)(2,1)} %get-tuple-element.11), channel_id=1, source_target_pairs={{4,8},{8,4},{12,16},{16,12},{20,24},{24,20},{28,32},{32,28},{36,40... | collective-permute-start | bytes 1572872 | tf_op jit(solution)/shard_map/ppermute | solution.py:434
  11.2 3.3 %collective-permute-start.3 = (bf16[512,512]{1,0:T(8,128)(2,1)S(1)}, bf16[512,512]{1,0:T(8,128)(2,1)S(1)}, u32[]{:S(2)}, u32[]{:S(2)}) collective-permute-start(bf16[512,512]{1,0:T(8,128)(2,1)S(1)} %copy-done), channel_id=1, source_target_pairs={{4,8},{8,4},{12,16},{16,12},{20,24},{24,20},{28,32},{32,28},{36,40... | collective-permute-start | bytes 1572872 | tf_op jit(solution)/shard_map/ppermute | solution.py:434
  14.6 8.6 %encoder_inner.1._ = bf16[12,128,512]{2,1,0:T(8,128)(2,1)} custom-call(s32[1]{0:T(128)} %bitcast.pos, s32[12]{0:T(128)} %counts.3, s32[4,12]{1,0:T(4,128)} %bitcast.35, bf16[12,128,512]{2,1,0:T(8,128)(2,1)} %bitcast.30, bf16[12,128,512]{2,1,0:T(8,128)(2,1)} %bitcast.23, bf16[12,128,512]{2,1,0:T(8,128)(2,1)} %bitcast.28), custom_call_target="tpu_custom_call" | custom-call | tf_op jit(solution)/shard_map/encoder_inner/pallas_call | solution.py:213
  23.2 6.0 %encoder_edge.1.e = bf16[12,128,512]{2,1,0:T(8,128)(2,1)} custom-call(s32[1]{0:T(128)} %bitcast.pos, s32[12]{0:T(128)} %counts.3, s32[4,12]{1,0:T(4,128)} %bitcast.36, bf16[12,128,512]{2,1,0:T(8,128)(2,1)} %bitcast.31, bf16[12,128,512]{2,1,0:T(8,128)(2,1)} %bitcast.24, bf16[12,128,512]{2,1,0:T(8,128)(2,1)} %bitcast.29, ...), custom_call_target="tpu_custom_call", output_to_operand_aliasing={{}: (8, {})} | custom-call | tf_op jit(solution)/shard_map/encoder_edge/pallas_call | solution.py:222
  29.2 4.8 %collective-permute-done.3 = bf16[512,512]{1,0:T(8,128)(2,1)S(1)} collective-permute-done((bf16[512,512]{1,0:T(8,128)(2,1)S(1)}, bf16[512,512]{1,0:T(8,128)(2,1)S(1)}, u32[]{:S(2)}, u32[]{:S(2)}) %collective-permute-start.3) | collective-permute-done | bytes 524320 | tf_op jit(solution)/shard_map/ppermute | solution.py:434
  34.1 5.4 %shard_map.114 = (bf16[4,128,512]{2,1,0:T(8,128)(2,1)}, bf16[4,128,512]{2,1,0:T(8,128)(2,1)}) custom-call(s32[1]{0:T(128)} %bitcast.pos, s32[256]{0:T(256)} %owners.3, s32[2,256]{1,0:T(2,128)} %bitcast.33, bf16[12,128,512]{2,1,0:T(8,128)(2,1)} %bitcast.25, bf16[12,128,512]{2,1,0:T(8,128)(2,1)} %encoder_edge.1.e, bf16[4,128,512]{2,1,0:T(8,128)(2,1)S(1)} %bitcast.19, ...), custom_call_target="tpu_custom_call" | custom-call | tf_op jit(solution)/shard_map/pallas_call | solution.py:320
  39.6 7.1 %collective-permute-start.5 = (bf16[512,512]{1,0:T(8,128)(2,1)}, bf16[512,512]{1,0:T(8,128)(2,1)S(1)}, u32[]{:S(2)}, u32[]{:S(2)}) collective-permute-start(bf16[512,512]{1,0:T(8,128)(2,1)} %bitcast.37), channel_id=1, source_target_pairs={{4,8},{8,4},{12,16},{16,12},{20,24},{24,20},{28,32},{32,28},{36,40... | collective-permute-start | bytes 1572872 | tf_op jit(solution)/shard_map/ppermute | solution.py:434
  46.7 2.9 %cut_weight.1 = (bf16[384,1024]{1,0:T(8,128)(2,1)}, bf16[128,1024]{1,0:T(8,128)(2,1)}, bf16[512,1024]{1,0:T(8,128)(2,1)}, bf16[512,1024]{1,0:T(8,128)(2,1)}) custom-call(s32[1]{0:T(128)} %bitcast.8.part, bf16[512,4096]{1,0:T(8,128)(2,1)} %refs_0_.3), custom_call_target="tpu_custom_call" | custom-call | tf_op jit(solution)/shard_map/cut_weight/pallas_call | solution.py:378
  49.6 2.2 %collective-permute-start.12 = (bf16[512,1024]{1,0:T(8,128)(2,1)}, bf16[512,1024]{1,0:T(8,128)(2,1)}, u32[]{:S(2)}, u32[]{:S(2)}) collective-permute-start(bf16[512,1024]{1,0:T(8,128)(2,1)} %get-tuple-element.17), channel_id=1, source_target_pairs={{0,1},{1,0},{2,3},{3,2},{4,5},{5,4},{6,7},{7,6},{8,9},{9,8},{10,11... | collective-permute-start | bytes 3145736 | tf_op jit(solution)/shard_map/ppermute | solution.py:438
  51.8 0.9 collective-permute-start.10
  52.7 1.8 %collective-permute-start.8 = (bf16[384,1024]{1,0:T(8,128)(2,1)}, bf16[384,1024]{1,0:T(8,128)(2,1)S(1)}, u32[]{:S(2)}, u32[]{:S(2)}) collective-permute-start(bf16[384,1024]{1,0:T(8,128)(2,1)} %get-tuple-element.14), channel_id=1, source_target_pairs={{0,2},{1,3},{2,0},{3,1},{4,6},{5,7},{6,4},{7,5},{8,10},{9,11},{10,... | collective-permute-start | bytes 2359304 | tf_op jit(solution)/shard_map/ppermute | solution.py:438
  54.5 1.7 %shard_map.113 = bf16[4,128,512]{2,1,0:T(8,128)(2,1)} custom-call(s32[1]{0:T(128)} %bitcast.pos, s32[256]{0:T(256)} %owners.3, s32[2,256]{1,0:T(2,128)} %bitcast.34, bf16[12,128,512]{2,1,0:T(8,128)(2,1)} %bitcast.26, bf16[12,128,512]{2,1,0:T(8,128)(2,1)} %encoder_edge.1.e, bf16[4,128,512]{2,1,0:T(8,128)(2,1)} %bitcast.32), custom_call_target="tpu_custom_call" | custom-call | tf_op jit(solution)/shard_map/pallas_call | solution.py:320
  56.2 1.1 %fusion = (bf16[2,128,512]{2,1,0:T(8,128)(2,1)S(1)}, bf16[2,128,512]{2,1,0:T(8,128)(2,1)S(1)}) fusion(bf16[4,128,512]{2,1,0:T(8,128)(2,1)} %shard_map.113), kind=kLoop, calls=%fused_computation.4 | loop fusion | bytes 1048576 | tf_op jit(solution)/shard_map/slice | solution.py:494
  57.4 2.6 %collective-permute-start.15 = (bf16[256,512]{1,0:T(8,128)(2,1)S(1)}, bf16[256,512]{1,0:T(8,128)(2,1)S(1)}, u32[]{:S(2)}, u32[]{:S(2)}) collective-permute-start(bf16[256,512]{1,0:T(8,128)(2,1)S(1)} %get-tuple-element.18.c0), channel_id=1, source_target_pairs={{0,1},{1,0},{2,3},{3,2},{4,5},{5,4},{6,7},{7,6},{8,9},{9,8},{10,11... | collective-permute-start | bytes 786440 | tf_op jit(solution)/shard_map/ppermute | solution.py:438
  60.1 1.8 %collective-permute-start.13 = (bf16[256,512]{1,0:T(8,128)(2,1)S(1)}, bf16[256,512]{1,0:T(8,128)(2,1)S(1)}, u32[]{:S(2)}, u32[]{:S(2)}) collective-permute-start(bf16[256,512]{1,0:T(8,128)(2,1)S(1)} %get-tuple-element.18.c0), channel_id=1, source_target_pairs={{0,2},{1,3},{2,0},{3,1},{4,6},{5,7},{6,4},{7,5},{8,10},{9,11},{10,... | collective-permute-start | bytes 786440 | tf_op jit(solution)/shard_map/ppermute | solution.py:438
  63.0 21.2 %collective-permute-done.13.c0 = bf16[256,512]{1,0:T(8,128)(2,1)S(1)} collective-permute-done((bf16[256,512]{1,0:T(8,128)(2,1)S(1)}, bf16[256,512]{1,0:T(8,128)(2,1)S(1)}, u32[]{:S(2)}, u32[]{:S(2)}) %collective-permute-start.13) | collective-permute-done | bytes 262176 | tf_op jit(solution)/shard_map/ppermute | solution.py:438
  84.2 0.6 collective-permute-start.14
  84.8 5.0 %collective-permute-done.6.c0 = bf16[256,512]{1,0:T(8,128)(2,1)S(1)} collective-permute-done((bf16[256,512]{1,0:T(8,128)(2,1)S(1)}, bf16[256,512]{1,0:T(8,128)(2,1)S(1)}, u32[]{:S(2)}, u32[]{:S(2)}) %collective-permute-start.6) | collective-permute-done | bytes 262176 | tf_op jit(solution)/shard_map/ppermute | solution.py:438
  90.3 3.4 %shard_map.116.refs_3_ = f32[256,1024]{1,0:T(8,128)} custom-call(s32[1]{0:T(128)} %bitcast.8.part, bf16[256,512]{1,0:T(8,128)(2,1)S(1)} %get-tuple-element.18.c0, bf16[256,512]{1,0:T(8,128)(2,1)S(1)} %collective-permute-done.15.c1, bf16[512,4096]{1,0:T(8,128)(2,1)} %refs_0_.3, bf16[512,1024]{1,0:T(8,128)(2,1)} %collective-permute-done.12.refs_1_, ...), custom_call_target="tpu_custom_call" | custom-call | tf_op jit(solution)/shard_map/pallas_call | solution.py:414
  93.6 3.4 %shard_map.115.refs_3_ = f32[256,1024]{1,0:T(8,128)} custom-call(s32[1]{0:T(128)} %bitcast.8.part, bf16[256,512]{1,0:T(8,128)(2,1)S(1)} %get-tuple-element.19.c0, bf16[256,512]{1,0:T(8,128)(2,1)S(1)} %collective-permute-done.11.c1, bf16[512,4096]{1,0:T(8,128)(2,1)} %refs_0_.3, bf16[512,1024]{1,0:T(8,128)(2,1)} %collective-permute-done.12.refs_1_, ...), custom_call_target="tpu_custom_call" | custom-call | tf_op jit(solution)/shard_map/pallas_call | solution.py:414
  97.0 3.0 %shard_map.117.refs_4_ = bf16[512,1024]{1,0:T(8,128)(2,1)} custom-call(s32[1]{0:T(128)} %bitcast.8.part, bf16[256,512]{1,0:T(8,128)(2,1)S(1)} %collective-permute-done.13.c0, bf16[256,512]{1,0:T(8,128)(2,1)S(1)} %collective-permute-done.14.c1, bf16[384,1024]{1,0:T(8,128)(2,1)S(1)} %collective-permute-done.8.refs_0_, ...), custom_call_target="tpu_custom_call" | custom-call | tf_op jit(solution)/shard_map/pallas_call | solution.py:414
  100.1 3.0 %shard_map.118 = bf16[512,1024]{1,0:T(8,128)(2,1)} custom-call(s32[1]{0:T(128)} %bitcast.8.part, bf16[256,512]{1,0:T(8,128)(2,1)S(1)} %collective-permute-done.6.c0, bf16[256,512]{1,0:T(8,128)(2,1)S(1)} %collective-permute-done.7.c1, bf16[384,1024]{1,0:T(8,128)(2,1)S(1)} %collective-permute-done.8.refs_0_, ...), custom_call_target="tpu_custom_call", output_to_operand_aliasing={{}: (7, {})} | custom-call | tf_op jit(solution)/shard_map/pallas_call | solution.py:414
  (24 shorter events, 2.0 us)
Async XLA Ops:
  0.6 10.5 %copy-start = (bf16[512,512]{1,0:T(8,128)(2,1)S(1)}, bf16[512,512]{1,0:T(8,128)(2,1)}, u32[]{:S(2)}) copy-start(bf16[512,512]{1,0:T(8,128)(2,1)} %param.15) | copy-start | bytes 1572868
  2.9 20.3 %collective-permute-start = (bf16[512,512]{1,0:T(8,128)(2,1)}, bf16[512,512]{1,0:T(8,128)(2,1)S(1)}, u32[]{:S(2)}, u32[]{:S(2)}) collective-permute-start(bf16[512,512]{1,0:T(8,128)(2,1)} %get-tuple-element.10), channel_id=1, source_target_pairs={{0,4},{4,0},{8,12},{12,8},{16,20},{20,16},{24,28},{28,24},{32,36},... | collective-permute-start | bytes 1572872 | tf_op jit(solution)/shard_map/ppermute | solution.py:434
  4.6 18.6 %collective-permute-start.1 = (bf16[512,512]{1,0:T(8,128)(2,1)}, bf16[512,512]{1,0:T(8,128)(2,1)S(1)}, u32[]{:S(2)}, u32[]{:S(2)}) collective-permute-start(bf16[512,512]{1,0:T(8,128)(2,1)} %get-tuple-element.11), channel_id=1, source_target_pairs={{4,8},{8,4},{12,16},{16,12},{20,24},{24,20},{28,32},{32,28},{36,40... | collective-permute-start | bytes 1572872 | tf_op jit(solution)/shard_map/ppermute | solution.py:434
  11.1 18.1 %collective-permute-start.2 = (bf16[512,512]{1,0:T(8,128)(2,1)S(1)}, bf16[512,512]{1,0:T(8,128)(2,1)S(1)}, u32[]{:S(2)}, u32[]{:S(2)}) collective-permute-start(bf16[512,512]{1,0:T(8,128)(2,1)S(1)} %copy-done), channel_id=1, source_target_pairs={{0,4},{4,0},{8,12},{12,8},{16,20},{20,16},{24,28},{28,24},{32,36},... | collective-permute-start | bytes 1572872 | tf_op jit(solution)/shard_map/ppermute | solution.py:434
  11.2 22.8 %collective-permute-start.3 = (bf16[512,512]{1,0:T(8,128)(2,1)S(1)}, bf16[512,512]{1,0:T(8,128)(2,1)S(1)}, u32[]{:S(2)}, u32[]{:S(2)}) collective-permute-start(bf16[512,512]{1,0:T(8,128)(2,1)S(1)} %copy-done), channel_id=1, source_target_pairs={{4,8},{8,4},{12,16},{16,12},{20,24},{24,20},{28,32},{32,28},{36,40... | collective-permute-start | bytes 1572872 | tf_op jit(solution)/shard_map/ppermute | solution.py:434
  39.5 17.9 %collective-permute-start.4 = (bf16[512,512]{1,0:T(8,128)(2,1)}, bf16[512,512]{1,0:T(8,128)(2,1)S(1)}, u32[]{:S(2)}, u32[]{:S(2)}) collective-permute-start(bf16[512,512]{1,0:T(8,128)(2,1)} %bitcast.38), channel_id=1, source_target_pairs={{0,4},{4,0},{8,12},{12,8},{16,20},{20,16},{24,28},{28,24},{32,36},... | collective-permute-start | bytes 1572872 | tf_op jit(solution)/shard_map/ppermute | solution.py:434
  39.6 17.8 %collective-permute-start.5 = (bf16[512,512]{1,0:T(8,128)(2,1)}, bf16[512,512]{1,0:T(8,128)(2,1)S(1)}, u32[]{:S(2)}, u32[]{:S(2)}) collective-permute-start(bf16[512,512]{1,0:T(8,128)(2,1)} %bitcast.37), channel_id=1, source_target_pairs={{4,8},{8,4},{12,16},{16,12},{20,24},{24,20},{28,32},{32,28},{36,40... | collective-permute-start | bytes 1572872 | tf_op jit(solution)/shard_map/ppermute | solution.py:434
  49.6 12.3 %collective-permute-start.12 = (bf16[512,1024]{1,0:T(8,128)(2,1)}, bf16[512,1024]{1,0:T(8,128)(2,1)}, u32[]{:S(2)}, u32[]{:S(2)}) collective-permute-start(bf16[512,1024]{1,0:T(8,128)(2,1)} %get-tuple-element.17), channel_id=1, source_target_pairs={{0,1},{1,0},{2,3},{3,2},{4,5},{5,4},{6,7},{7,6},{8,9},{9,8},{10,11... | collective-permute-start | bytes 3145736 | tf_op jit(solution)/shard_map/ppermute | solution.py:438
  51.8 45.2 %collective-permute-start.10 = (bf16[512,1024]{1,0:T(8,128)(2,1)}, bf16[512,1024]{1,0:T(8,128)(2,1)}, u32[]{:S(2)}, u32[]{:S(2)}) collective-permute-start(bf16[512,1024]{1,0:T(8,128)(2,1)} %get-tuple-element.16), channel_id=1, source_target_pairs={{0,35},{1,34},{2,33},{3,32},{4,39},{5,38},{6,37},{7,36},{8,43},{9,... | collective-permute-start | bytes 3145736 | tf_op jit(solution)/shard_map/ppermute | solution.py:447
  52.7 44.3 %collective-permute-start.8 = (bf16[384,1024]{1,0:T(8,128)(2,1)}, bf16[384,1024]{1,0:T(8,128)(2,1)S(1)}, u32[]{:S(2)}, u32[]{:S(2)}) collective-permute-start(bf16[384,1024]{1,0:T(8,128)(2,1)} %get-tuple-element.14), channel_id=1, source_target_pairs={{0,2},{1,3},{2,0},{3,1},{4,6},{5,7},{6,4},{7,5},{8,10},{9,11},{10,... | collective-permute-start | bytes 2359304 | tf_op jit(solution)/shard_map/ppermute | solution.py:438
  56.2 28.0 %copy-start.1 = (bf16[128,1024]{1,0:T(8,128)(2,1)S(1)}, bf16[128,1024]{1,0:T(8,128)(2,1)}, u32[]{:S(2)}) copy-start(bf16[128,1024]{1,0:T(8,128)(2,1)} %get-tuple-element.15) | copy-start | bytes 786436
  57.4 5.0 %collective-permute-start.15 = (bf16[256,512]{1,0:T(8,128)(2,1)S(1)}, bf16[256,512]{1,0:T(8,128)(2,1)S(1)}, u32[]{:S(2)}, u32[]{:S(2)}) collective-permute-start(bf16[256,512]{1,0:T(8,128)(2,1)S(1)} %get-tuple-element.18.c0), channel_id=1, source_target_pairs={{0,1},{1,0},{2,3},{3,2},{4,5},{5,4},{6,7},{7,6},{8,9},{9,8},{10,11... | collective-permute-start | bytes 786440 | tf_op jit(solution)/shard_map/ppermute | solution.py:438
  60.1 24.1 %collective-permute-start.13 = (bf16[256,512]{1,0:T(8,128)(2,1)S(1)}, bf16[256,512]{1,0:T(8,128)(2,1)S(1)}, u32[]{:S(2)}, u32[]{:S(2)}) collective-permute-start(bf16[256,512]{1,0:T(8,128)(2,1)S(1)} %get-tuple-element.18.c0), channel_id=1, source_target_pairs={{0,2},{1,3},{2,0},{3,1},{4,6},{5,7},{6,4},{7,5},{8,10},{9,11},{10,... | collective-permute-start | bytes 786440 | tf_op jit(solution)/shard_map/ppermute | solution.py:438
  61.9 22.3 %collective-permute-start.11 = (bf16[256,512]{1,0:T(8,128)(2,1)S(1)}, bf16[256,512]{1,0:T(8,128)(2,1)S(1)}, u32[]{:S(2)}, u32[]{:S(2)}) collective-permute-start(bf16[256,512]{1,0:T(8,128)(2,1)S(1)} %get-tuple-element.19.c0), channel_id=1, source_target_pairs={{0,1},{1,0},{2,3},{3,2},{4,5},{5,4},{6,7},{7,6},{8,9},{9,8},{10,11... | collective-permute-start | bytes 786440 | tf_op jit(solution)/shard_map/ppermute | solution.py:438
  62.4 27.4 %collective-permute-start.6 = (bf16[256,512]{1,0:T(8,128)(2,1)S(1)}, bf16[256,512]{1,0:T(8,128)(2,1)S(1)}, u32[]{:S(2)}, u32[]{:S(2)}) collective-permute-start(bf16[256,512]{1,0:T(8,128)(2,1)S(1)} %get-tuple-element.19.c0), channel_id=1, source_target_pairs={{0,2},{1,3},{2,0},{3,1},{4,6},{5,7},{6,4},{7,5},{8,10},{9,11},{10,... | collective-permute-start | bytes 786440 | tf_op jit(solution)/shard_map/ppermute | solution.py:438
  84.2 12.8 %collective-permute-start.9 = (bf16[128,1024]{1,0:T(8,128)(2,1)S(1)}, bf16[128,1024]{1,0:T(8,128)(2,1)S(1)}, u32[]{:S(2)}, u32[]{:S(2)}) collective-permute-start(bf16[128,1024]{1,0:T(8,128)(2,1)S(1)} %copy-done.1), channel_id=1, source_target_pairs={{0,34},{1,35},{2,32},{3,33},{4,38},{5,39},{6,36},{7,37},{8,42},{9,... | collective-permute-start | bytes 786440 | tf_op jit(solution)/shard_map/ppermute | solution.py:447
  84.2 12.8 %collective-permute-start.14 = (bf16[256,512]{1,0:T(8,128)(2,1)S(1)}, bf16[256,512]{1,0:T(8,128)(2,1)S(1)}, u32[]{:S(2)}, u32[]{:S(2)}) collective-permute-start(bf16[256,512]{1,0:T(8,128)(2,1)S(1)} %collective-permute-done.13.c0), channel_id=1, source_target_pairs={{0,1},{1,0},{2,3},{3,2},{4,5},{5,4},{6,7},{7,6},{8,9},{9,8},{10,11... | collective-permute-start | bytes 786440 | tf_op jit(solution)/shard_map/ppermute | solution.py:438
  89.8 10.3 %collective-permute-start.7 = (bf16[256,512]{1,0:T(8,128)(2,1)S(1)}, bf16[256,512]{1,0:T(8,128)(2,1)S(1)}, u32[]{:S(2)}, u32[]{:S(2)}) collective-permute-start(bf16[256,512]{1,0:T(8,128)(2,1)S(1)} %collective-permute-done.6.c0), channel_id=1, source_target_pairs={{0,1},{1,0},{2,3},{3,2},{4,5},{5,4},{6,7},{7,6},{8,9},{9,8},{10,11... | collective-permute-start | bytes 786440 | tf_op jit(solution)/shard_map/ppermute | solution.py:438

commit v8 on v7

--- a/solution.py
+++ b/solution.py
@@ -108,7 +108,27 @@
             attend(q_ref, [kb.at[i] for i in ids[:n]], [vb.at[i] for i in ids[:n]], o_ref)
 
 
-def inner_kernel(pos, counts, lists, q, k, v, e, kb, vb, qb, eb, k_sem, v_sem, q_sem, e_sem):
+def inner_kernel(pos, counts, lists, part, q, k, v, w, e, *refs):
+    pieces, (kb, vb, qb, eb) = refs[:4], refs[4:8]
+    stages = refs[8:12]
+    k_sem, v_sem, q_sem, e_sem, load_sem, store_sem = refs[12:]
+    columns = pieces[0].shape[1]
+    split = pieces[0].shape[0]
+    cuts = (
+        (2, pl.ds(0, split)),
+        (2, pl.ds(split, w.shape[0] - split)),
+        (3, pl.ds(0, w.shape[0])),
+        (1, pl.ds(0, w.shape[0])),
+    )
+
+    def load(i):
+        flip, rows = cuts[i]
+        start = pl.multiple_of((part[0] ^ flip) * columns, columns)
+        return pltpu.make_async_copy(w.at[rows, pl.ds(start, columns)], stages[i], load_sem.at[i])
+
+    def store(i):
+        return pltpu.make_async_copy(stages[i], pieces[i], store_sem.at[i])
+
     blocks = k.shape[0]
     base = pos[0] * blocks
 
@@ -129,6 +149,8 @@
         values(i).start()
         if REACH <= i < blocks - REACH:
             queries(i).start()
+    for i in range(len(cuts)):
+        load(i).start()
     for i in range(2 * REACH):
         keys(i).wait()
         values(i).wait()
@@ -140,9 +162,17 @@
         queries(b).wait()
         encode_block(b, base, counts, lists, qb.at[b], kb, vb, eb.at[b])
         result(b).start()
+        for i in range(len(cuts)):
+
+            @pl.when(b == REACH + 1 + i)
+            def _(i=i):
+                load(i).wait()
+                store(i).start()
 
     for i in range(REACH, blocks - REACH):
         result(i).wait()
+    for i in range(len(cuts)):
+        store(i).wait()
 
 
 def edge_kernel(
@@ -198,7 +228,7 @@
         pltpu.make_async_copy(eb.at[t], e.at[t], e_sem).wait()
 
 
-def encoder_call(position, counts, lists, q, k3, v3, edges=None):
+def encoder_call(position, counts, lists, q, k3, v3, weight=None, edges=None):
     blocks, _, width = k3.shape
     smem = pl.BlockSpec(memory_space=pltpu.SMEM)
     hbm = pl.BlockSpec(memory_space=pl.ANY)
@@ -210,14 +240,21 @@
     shape = jax.ShapeDtypeStruct(k3.shape, jnp.bfloat16)
     args = (position, counts, lists, cut(q), k3, v3)
     if edges is None:
+        part, w, columns = weight
+        rows = w.shape[0]
+        split = rows * 3 // 4
+        pieces = [(n, columns) for n in (split, rows - split, rows, rows)]
         return pl.pallas_call(
             inner_kernel,
-            in_specs=[smem] * 3 + [hbm] * 3,
-            out_specs=hbm,
-            out_shape=shape,
-            scratch_shapes=[room(blocks)] * 4 + [dma((blocks,))] * 3 + [dma],
+            in_specs=[smem] * 4 + [hbm] * 4,
+            out_specs=[hbm] * 5,
+            out_shape=[shape] + [jax.ShapeDtypeStruct(x, w.dtype) for x in pieces],
+            scratch_shapes=[room(blocks)] * 4
+            + [pltpu.VMEM(x, w.dtype) for x in pieces]
+            + [dma((blocks,))] * 3
+            + [dma, dma((4,)), dma((4,))],
             name="encoder_inner",
-        )(*args)
+        )(*args[:3], part, *args[3:], w)
     beside, beyond, partial = edges
     return pl.pallas_call(
         edge_kernel,
@@ -343,49 +380,6 @@
     return pltpu.with_memory_space_constraint(x, pltpu.VMEM)
 
 
-def move(plan, stages, load_sem, store_sem):
-    loads = [pltpu.make_async_copy(src, stages[i], load_sem.at[i]) for i, (src, _) in enumerate(plan)]
-    stores = [pltpu.make_async_copy(stages[i], dst, store_sem) for i, (_, dst) in enumerate(plan)]
-    for load in loads:
-        load.start()
-    for load, store in zip(loads, stores):
-        load.wait()
-        store.start()
-    for store in stores:
-        store.wait()
-
-
-def cut_kernel(part, w, a, b, c, d, sa, sb, sc, sd, load_sem, store_sem):
-    columns = a.shape[1]
-    split = a.shape[0]
-    plan = []
-    for flip, rows, dst in (
-        (2, pl.ds(0, split), a),
-        (2, pl.ds(split, w.shape[0] - split), b),
-        (3, pl.ds(0, w.shape[0]), c),
-        (1, pl.ds(0, w.shape[0]), d),
-    ):
-        start = pl.multiple_of((part[0] ^ flip) * columns, columns)
-        plan.append((w.at[rows, pl.ds(start, columns)], dst))
-    move(plan, (sa, sb, sc, sd), load_sem, store_sem)
-
-
-def cut_call(part, w, columns):
-    rows = w.shape[0]
-    split = rows * 3 // 4
-    shapes = [(n, columns) for n in (split, rows - split, rows, rows)]
-    hbm = pl.BlockSpec(memory_space=pl.ANY)
-    return pl.pallas_call(
-        cut_kernel,
-        in_specs=[pl.BlockSpec(memory_space=pltpu.SMEM), hbm],
-        out_specs=[hbm] * 4,
-        out_shape=[jax.ShapeDtypeStruct(x, w.dtype) for x in shapes],
-        scratch_shapes=[pltpu.VMEM(x, w.dtype) for x in shapes]
-        + [pltpu.SemaphoreType.DMA((4,)), pltpu.SemaphoreType.DMA],
-        name="cut_weight",
-    )(part, w)
-
-
 def project_kernel(counts, part, c0, c1, *refs):
     first, second = counts
     weights = refs[: first + second]
@@ -400,9 +394,10 @@
 def project_call(part, contexts, weights, added, dtype, index, out_tokens, earlier=None):
     tokens, width = contexts[0].shape
     columns = added.shape[1]
+    tile = min(tokens, out_tokens // PARTS)
     here = index if added.shape[0] > tokens else 0
     there = index if out_tokens > tokens else 0
-    c_spec = pl.BlockSpec((tokens, width), lambda i, p: (0, 0))
+    c_spec = pl.BlockSpec((tile, width), lambda i, p: (i, 0))
     flat = [w for ws in weights for w in ws]
     w_specs = [
         pl.BlockSpec((w.shape[0], columns), lambda i, p: (0, p[0]))
@@ -415,12 +410,12 @@
         functools.partial(project_kernel, tuple(len(ws) for ws in weights)),
         grid_spec=pltpu.PrefetchScalarGridSpec(
             num_scalar_prefetch=1,
-            grid=(1,),
+            grid=(tokens // tile,),
             in_specs=[c_spec] * 2
             + w_specs
-            + [pl.BlockSpec((tokens, columns), lambda i, p: (here, 0))]
+            + [pl.BlockSpec((tile, columns), lambda i, p: (here + i, 0))]
             + [pl.BlockSpec(memory_space=pl.ANY)] * len(more),
-            out_specs=pl.BlockSpec((tokens, columns), lambda i, p: (there, 0)),
+            out_specs=pl.BlockSpec((tile, columns), lambda i, p: (there + i, 0)),
         ),
         out_shape=jax.ShapeDtypeStruct((out_tokens, columns), dtype),
         input_output_aliases={4 + len(flat): 0} if more else {},
@@ -473,13 +468,14 @@
     beyond = exchanged(beyond, 1)
     q_beside = exchanged(decoder_queries, 0)
     q_beyond = exchanged(decoder_queries, 1)
-    across2, around2, across3, across1 = cut_call(part, out_weight, columns)
+    encoder_args = (position, block_counts, lists, encoder_queries, k3, v3)
+    partial, across2, around2, across3, across1 = encoder_call(
+        *encoder_args, weight=(part, out_weight, columns)
+    )
     w2_most = swapped(across2, 2)
     w2_rest = other_side(around2, 2)
     w3 = other_side(across3, 3)
     w1 = swapped(across1, 1)
-    encoder_args = (position, block_counts, lists, encoder_queries, k3, v3)
-    partial = encoder_call(*encoder_args)
     e3 = encoder_call(*encoder_args, edges=(beside, beyond, partial))
     tables = (position, span_owner, slots, k3, e3)
     answers = serve_call(*tables, [q_beside, q_beyond])
@@ -488,19 +484,21 @@
     (own,) = serve_call(*tables, [decoder_queries])
     tokens = decoder_input.shape[0]
     share = tokens // PARTS
+    context = own + from_beside + from_beyond
+    halves = []
+    for i in range(PARTS):
+        across = swapped(context[i * share : (i + 1) * share], 2)
+        corner = swapped(across, 1)
+        halves.append([across, corner])
+    aside = swapped(context, 1)
+    total = project_call(
+        part, [context, aside], [[out_weight], [w1]], decoder_input, jnp.float32, 0, tokens
+    )
     decoder_out = None
     for i in range(PARTS):
-        rows = slice(i * share, (i + 1) * share)
-        context = own[rows] + from_beside[rows] + from_beyond[rows]
-        across = swapped(context, 2)
-        aside = swapped(context, 1)
-        corner = swapped(across, 1)
-        total = project_call(
-            part, [context, aside], [[out_weight], [w1]], decoder_input, jnp.float32, i, share
-        )
         decoder_out = project_call(
             part,
-            [across, corner],
+            halves[i],
             [[in_vmem(w2_most), in_vmem(w2_rest)], [w3]],
             total,
             jnp.bfloat16,

time: 104 us -> 101 us (0.971)
  Pallas kernels: 39.6 us -> 34.3 us
  waiting for transfers between devices: 31.1 us -> 35.3 us
  starting transfers between devices: 30.4 us -> 29.1 us
  local copies, waits for them, and re-layouts: 1.12 us -> 0.04 us
    ppermute x6, waiting for transfers between devices: 4.86 us -> 8.75 us  [exchanged(): return lax.ppermute(block, 'seq', route)]
    pallas_call x2 -> x1, Pallas kernels: 11.5 us -> 8.77 us  [encoder_call(): pl.pallas_call(inner_kernel, in_specs=[smem] * 4 + [hbm] * 4, out_specs=[...]
    pallas_call x4 -> x3, Pallas kernels: 12.8 us -> 10.2 us  [project_call(): pl.pallas_call(functools.partial(project_kernel, tuple((len(ws) for ws in...]
    ppermute x8 -> x7, starting transfers between devices: 10.5 us -> 9.34 us  [swapped(): return lax.ppermute(block, HEAD, [(i, i ^ flip) for i in range(4)])]
    slice x1, local copies, waits for them, and re-layouts: 1.11 us -> 0.03 us  [body(): across = swapped(context[i * share:(i + 1) * share], 2)]
    ppermute x8 -> x7, waiting for transfers between devices: 26.2 us -> 26.5 us  [swapped(): return lax.ppermute(block, HEAD, [(i, i ^ flip) for i in range(4)])]
  transfers between devices with their start and end apart: 16 -> 15, of which waited for: 3 -> 4; matrix products, arithmetic and copies ran while one was open for 1% -> 1% of each run, Pallas kernels for 28% -> 23%
where the time goes in v8:
time: 101 us
  waiting for transfers between devices  35.3 us (35%)
  Pallas kernels  34.3 us (34%)
  starting transfers between devices  29.1 us (29%)
  other arithmetic  1.12 us (1%)
    ppermute x7, waiting for transfers between devices, swapped(): return lax.ppermute(block, HEAD, [(i, i ^ flip) for i in range(4)])  26.5 us
    ppermute x6, starting transfers between devices, exchanged(): return lax.ppermute(block, 'seq', route)  18.8 us
    pallas_call x3, Pallas kernels, project_call(): pl.pallas_call(functools.partial(project_kernel, tuple((len(ws) for ws in...  10.2 us
    ppermute x7, starting transfers between devices, swapped(): return lax.ppermute(block, HEAD, [(i, i ^ flip) for i in range(4)])  9.34 us
    pallas_call x1, Pallas kernels, encoder_call(): pl.pallas_call(inner_kernel, in_specs=[smem] * 4 + [hbm] * 4, out_specs=[...  8.77 us
    ppermute x6, waiting for transfers between devices, exchanged(): return lax.ppermute(block, 'seq', route)  8.75 us
    pallas_call x2, Pallas kernels, serve_call(): pl.pallas_call(serve_kernel, in_specs=[smem] * 3 + [hbm] * 2 + [vmem if s...  7.08 us
    pallas_call x1, Pallas kernels, encoder_call(): pl.pallas_call(edge_kernel, in_specs=[smem] * 3 + [hbm] * 3 + [pl.BlockSp...  5.98 us
  transfers between devices with their start and end apart: 15, of which 4 were waited for; matrix products, arithmetic and copies ran while one was open for 1% of the time, Pallas kernels for 23%

profile of v8, /device:TPU:21, one launch (start us, length us, event | category | flops | bytes accessed | tf_op | source)
XLA Modules:
  0.0 100.6 jit_solution(5468155120803343675)
XLA Ops:
  0.6 2.2 %pack_edges.1 = (bf16[512,512]{1,0:T(8,128)(2,1)}, bf16[512,512]{1,0:T(8,128)(2,1)}) custom-call(s32[1]{0:T(128)} %bitcast.pos, bf16[1536,512]{1,0:T(8,128)(2,1)} %k.1, bf16[1536,512]{1,0:T(8,128)(2,1)} %v.1), custom_call_target="tpu_custom_call" | custom-call | tf_op jit(solution)/shard_map/pack_edges/pallas_call | solution.py:90
  2.9 1.8 %collective-permute-start = (bf16[512,512]{1,0:T(8,128)(2,1)}, bf16[512,512]{1,0:T(8,128)(2,1)S(1)}, u32[]{:S(2)}, u32[]{:S(2)}) collective-permute-start(bf16[512,512]{1,0:T(8,128)(2,1)} %get-tuple-element.11), channel_id=1, source_target_pairs={{0,4},{4,0},{8,12},{12,8},{16,20},{20,16},{24,28},{28,24},{32,36},... | collective-permute-start | bytes 1572872 | tf_op jit(solution)/shard_map/ppermute | solution.py:429
  4.7 6.5 %collective-permute-start.1 = (bf16[512,512]{1,0:T(8,128)(2,1)}, bf16[512,512]{1,0:T(8,128)(2,1)S(1)}, u32[]{:S(2)}, u32[]{:S(2)}) collective-permute-start(bf16[512,512]{1,0:T(8,128)(2,1)} %get-tuple-element.12), channel_id=1, source_target_pairs={{4,8},{8,4},{12,16},{16,12},{20,24},{24,20},{28,32},{32,28},{36,40... | collective-permute-start | bytes 1572872 | tf_op jit(solution)/shard_map/ppermute | solution.py:429
  11.2 3.3 %collective-permute-start.3 = (bf16[512,512]{1,0:T(8,128)(2,1)S(1)}, bf16[512,512]{1,0:T(8,128)(2,1)S(1)}, u32[]{:S(2)}, u32[]{:S(2)}) collective-permute-start(bf16[512,512]{1,0:T(8,128)(2,1)S(1)} %copy-done.1), channel_id=1, source_target_pairs={{4,8},{8,4},{12,16},{16,12},{20,24},{24,20},{28,32},{32,28},{36,40... | collective-permute-start | bytes 1572872 | tf_op jit(solution)/shard_map/ppermute | solution.py:429
  14.6 8.8 %encoder_inner.1 = (bf16[12,128,512]{2,1,0:T(8,128)(2,1)}, bf16[384,1024]{1,0:T(8,128)(2,1)}, bf16[128,1024]{1,0:T(8,128)(2,1)}, bf16[512,1024]{1,0:T(8,128)(2,1)}, bf16[512,1024]{1,0:T(8,128)(2,1)}) custom-call(s32[1]{0:T(128)} %bitcast.pos, s32[12]{0:T(128)} %counts.3, s32[4,12]{1,0:T(4,128)} %bitcast.35, s32[1]{0:T(128)} %bitcast.7.part, ...), custom_call_target="tpu_custom_call" | custom-call | tf_op jit(solution)/shard_map/encoder_inner/pallas_call | solution.py:247
  23.4 6.0 %encoder_edge.1.e = bf16[12,128,512]{2,1,0:T(8,128)(2,1)} custom-call(s32[1]{0:T(128)} %bitcast.pos, s32[12]{0:T(128)} %counts.3, s32[4,12]{1,0:T(4,128)} %bitcast.36, bf16[12,128,512]{2,1,0:T(8,128)(2,1)} %bitcast.31, bf16[12,128,512]{2,1,0:T(8,128)(2,1)} %bitcast.24, bf16[12,128,512]{2,1,0:T(8,128)(2,1)} %bitcast.29, ...), custom_call_target="tpu_custom_call", output_to_operand_aliasing={{}: (8, {})} | custom-call | tf_op jit(solution)/shard_map/encoder_edge/pallas_call | solution.py:259
  29.4 4.7 %collective-permute-done.3 = bf16[512,512]{1,0:T(8,128)(2,1)S(1)} collective-permute-done((bf16[512,512]{1,0:T(8,128)(2,1)S(1)}, bf16[512,512]{1,0:T(8,128)(2,1)S(1)}, u32[]{:S(2)}, u32[]{:S(2)}) %collective-permute-start.3) | collective-permute-done | bytes 524320 | tf_op jit(solution)/shard_map/ppermute | solution.py:429
  34.1 5.4 %shard_map.114 = (bf16[4,128,512]{2,1,0:T(8,128)(2,1)}, bf16[4,128,512]{2,1,0:T(8,128)(2,1)}) custom-call(s32[1]{0:T(128)} %bitcast.pos, s32[256]{0:T(256)} %owners.3, s32[2,256]{1,0:T(2,128)} %bitcast.33, bf16[12,128,512]{2,1,0:T(8,128)(2,1)} %bitcast.25, bf16[12,128,512]{2,1,0:T(8,128)(2,1)} %encoder_edge.1.e, bf16[4,128,512]{2,1,0:T(8,128)(2,1)S(1)} %bitcast.19, ...), custom_call_target="tpu_custom_call" | custom-call | tf_op jit(solution)/shard_map/pallas_call | solution.py:357
  39.6 7.1 %collective-permute-start.5 = (bf16[512,512]{1,0:T(8,128)(2,1)}, bf16[512,512]{1,0:T(8,128)(2,1)S(1)}, u32[]{:S(2)}, u32[]{:S(2)}) collective-permute-start(bf16[512,512]{1,0:T(8,128)(2,1)} %bitcast.37), channel_id=1, source_target_pairs={{4,8},{8,4},{12,16},{16,12},{20,24},{24,20},{28,32},{32,28},{36,40... | collective-permute-start | bytes 1572872 | tf_op jit(solution)/shard_map/ppermute | solution.py:429
  46.7 2.2 %collective-permute-start.12 = (bf16[512,1024]{1,0:T(8,128)(2,1)}, bf16[512,1024]{1,0:T(8,128)(2,1)S(1)}, u32[]{:S(2)}, u32[]{:S(2)}) collective-permute-start(bf16[512,1024]{1,0:T(8,128)(2,1)} %get-tuple-element.19), channel_id=1, source_target_pairs={{0,1},{1,0},{2,3},{3,2},{4,5},{5,4},{6,7},{7,6},{8,9},{9,8},{10,11... | collective-permute-start | bytes 3145736 | tf_op jit(solution)/shard_map/ppermute | solution.py:433
  48.9 0.9 collective-permute-start.10
  49.8 1.8 %collective-permute-start.8 = (bf16[384,1024]{1,0:T(8,128)(2,1)}, bf16[384,1024]{1,0:T(8,128)(2,1)S(1)}, u32[]{:S(2)}, u32[]{:S(2)}) collective-permute-start(bf16[384,1024]{1,0:T(8,128)(2,1)} %get-tuple-element.16), channel_id=1, source_target_pairs={{0,2},{1,3},{2,0},{3,1},{4,6},{5,7},{6,4},{7,5},{8,10},{9,11},{10,... | collective-permute-start | bytes 2359304 | tf_op jit(solution)/shard_map/ppermute | solution.py:433
  51.6 1.7 %shard_map.113 = bf16[4,128,512]{2,1,0:T(8,128)(2,1)} custom-call(s32[1]{0:T(128)} %bitcast.pos, s32[256]{0:T(256)} %owners.3, s32[2,256]{1,0:T(2,128)} %bitcast.34, bf16[12,128,512]{2,1,0:T(8,128)(2,1)} %bitcast.26, bf16[12,128,512]{2,1,0:T(8,128)(2,1)} %encoder_edge.1.e, bf16[4,128,512]{2,1,0:T(8,128)(2,1)} %bitcast.32), custom_call_target="tpu_custom_call" | custom-call | tf_op jit(solution)/shard_map/pallas_call | solution.py:357
  53.3 4.0 %collective-permute-done.5 = bf16[512,512]{1,0:T(8,128)(2,1)S(1)} collective-permute-done((bf16[512,512]{1,0:T(8,128)(2,1)}, bf16[512,512]{1,0:T(8,128)(2,1)S(1)}, u32[]{:S(2)}, u32[]{:S(2)}) %collective-permute-start.5) | collective-permute-done | bytes 524320 | tf_op jit(solution)/shard_map/ppermute | solution.py:429
  57.3 1.1 %fusion.c0 = bf16[512,512]{1,0:T(8,128)(2,1)S(1)} fusion(bf16[512,512]{1,0:T(8,128)(2,1)S(1)} %collective-permute-done.5, bf16[512,512]{1,0:T(8,128)(2,1)S(1)} %collective-permute-done.4, bf16[4,128,512]{2,1,0:T(8,128)(2,1)} %shard_map.113), kind=kLoop, calls=%fused_computation.1 | loop fusion | flops 524288 | bytes 2097152 | tf_op jit(solution)/shard_map/add | solution.py:487
  58.4 2.7 %collective-permute-start.11 = (bf16[512,512]{1,0:T(8,128)(2,1)S(1)}, bf16[512,512]{1,0:T(8,128)(2,1)S(1)}, u32[]{:S(2)}, u32[]{:S(2)}) collective-permute-start(bf16[512,512]{1,0:T(8,128)(2,1)S(1)} %fusion.c0), channel_id=1, source_target_pairs={{0,1},{1,0},{2,3},{3,2},{4,5},{5,4},{6,7},{7,6},{8,9},{9,8},{10,11... | collective-permute-start | bytes 1572872 | tf_op jit(solution)/shard_map/ppermute | solution.py:433
  61.2 2.0 %collective-permute-start.13 = (bf16[256,512]{1,0:T(8,128)(2,1)S(1)}, bf16[256,512]{1,0:T(8,128)(2,1)S(1)}, u32[]{:S(2)}, u32[]{:S(2)}) collective-permute-start(bf16[256,512]{1,0:T(8,128)(2,1)S(1)} %get-tuple-element.20), channel_id=1, source_target_pairs={{0,2},{1,3},{2,0},{3,1},{4,6},{5,7},{6,4},{7,5},{8,10},{9,11},{10,... | collective-permute-start | bytes 786440 | tf_op jit(solution)/shard_map/ppermute | solution.py:433
  63.2 0.1 collective-permute-start.6
  63.3 20.9 %collective-permute-done.13.c0 = bf16[256,512]{1,0:T(8,128)(2,1)S(1)} collective-permute-done((bf16[256,512]{1,0:T(8,128)(2,1)S(1)}, bf16[256,512]{1,0:T(8,128)(2,1)S(1)}, u32[]{:S(2)}, u32[]{:S(2)}) %collective-permute-start.13) | collective-permute-done | bytes 262176 | tf_op jit(solution)/shard_map/ppermute | solution.py:433
  84.2 5.6 %collective-permute-done.6.c0 = bf16[256,512]{1,0:T(8,128)(2,1)S(1)} collective-permute-done((bf16[256,512]{1,0:T(8,128)(2,1)S(1)}, bf16[256,512]{1,0:T(8,128)(2,1)S(1)}, u32[]{:S(2)}, u32[]{:S(2)}) %collective-permute-start.6) | collective-permute-done | bytes 262176 | tf_op jit(solution)/shard_map/ppermute | solution.py:433
  89.8 0.5 collective-permute-start.14
  90.4 4.1 %shard_map.115.refs_3_ = f32[512,1024]{1,0:T(8,128)} custom-call(s32[1]{0:T(128)} %bitcast.7.part, bf16[512,512]{1,0:T(8,128)(2,1)S(1)} %fusion.c0, bf16[512,512]{1,0:T(8,128)(2,1)S(1)} %collective-permute-done.11.c1, bf16[512,4096]{1,0:T(8,128)(2,1)} %refs_0_.1, bf16[512,1024]{1,0:T(8,128)(2,1)} %copy-done, bf16[512,1024]{1,0:T(8,128)(2,1)} %refs_2_.1), custom_call_target="tpu_custom_call" | custom-call | tf_op jit(solution)/shard_map/pallas_call | solution.py:409
  94.5 3.0 %shard_map.116.refs_4_ = bf16[512,1024]{1,0:T(8,128)(2,1)} custom-call(s32[1]{0:T(128)} %bitcast.7.part, bf16[256,512]{1,0:T(8,128)(2,1)S(1)} %collective-permute-done.13.c0, bf16[256,512]{1,0:T(8,128)(2,1)S(1)} %collective-permute-done.14.c1, bf16[384,1024]{1,0:T(8,128)(2,1)S(1)} %collective-permute-done.8.refs_0_, ...), custom_call_target="tpu_custom_call" | custom-call | tf_op jit(solution)/shard_map/pallas_call | solution.py:409
  97.6 3.0 %shard_map.117 = bf16[512,1024]{1,0:T(8,128)(2,1)} custom-call(s32[1]{0:T(128)} %bitcast.7.part, bf16[256,512]{1,0:T(8,128)(2,1)S(1)} %collective-permute-done.6.c0, bf16[256,512]{1,0:T(8,128)(2,1)S(1)} %collective-permute-done.7.c1, bf16[384,1024]{1,0:T(8,128)(2,1)S(1)} %collective-permute-done.8.refs_0_, ...), custom_call_target="tpu_custom_call", output_to_operand_aliasing={{}: (7, {})} | custom-call | tf_op jit(solution)/shard_map/pallas_call | solution.py:409
  (20 shorter events, 0.3 us)
Async XLA Ops:
  0.6 10.5 %copy-start.1 = (bf16[512,512]{1,0:T(8,128)(2,1)S(1)}, bf16[512,512]{1,0:T(8,128)(2,1)}, u32[]{:S(2)}) copy-start(bf16[512,512]{1,0:T(8,128)(2,1)} %param.15) | copy-start | bytes 1572868
  2.9 20.5 %collective-permute-start = (bf16[512,512]{1,0:T(8,128)(2,1)}, bf16[512,512]{1,0:T(8,128)(2,1)S(1)}, u32[]{:S(2)}, u32[]{:S(2)}) collective-permute-start(bf16[512,512]{1,0:T(8,128)(2,1)} %get-tuple-element.11), channel_id=1, source_target_pairs={{0,4},{4,0},{8,12},{12,8},{16,20},{20,16},{24,28},{28,24},{32,36},... | collective-permute-start | bytes 1572872 | tf_op jit(solution)/shard_map/ppermute | solution.py:429
  4.7 18.7 %collective-permute-start.1 = (bf16[512,512]{1,0:T(8,128)(2,1)}, bf16[512,512]{1,0:T(8,128)(2,1)S(1)}, u32[]{:S(2)}, u32[]{:S(2)}) collective-permute-start(bf16[512,512]{1,0:T(8,128)(2,1)} %get-tuple-element.12), channel_id=1, source_target_pairs={{4,8},{8,4},{12,16},{16,12},{20,24},{24,20},{28,32},{32,28},{36,40... | collective-permute-start | bytes 1572872 | tf_op jit(solution)/shard_map/ppermute | solution.py:429
  11.1 18.2 %collective-permute-start.2 = (bf16[512,512]{1,0:T(8,128)(2,1)S(1)}, bf16[512,512]{1,0:T(8,128)(2,1)S(1)}, u32[]{:S(2)}, u32[]{:S(2)}) collective-permute-start(bf16[512,512]{1,0:T(8,128)(2,1)S(1)} %copy-done.1), channel_id=1, source_target_pairs={{0,4},{4,0},{8,12},{12,8},{16,20},{20,16},{24,28},{28,24},{32,36},... | collective-permute-start | bytes 1572872 | tf_op jit(solution)/shard_map/ppermute | solution.py:429
  11.2 22.9 %collective-permute-start.3 = (bf16[512,512]{1,0:T(8,128)(2,1)S(1)}, bf16[512,512]{1,0:T(8,128)(2,1)S(1)}, u32[]{:S(2)}, u32[]{:S(2)}) collective-permute-start(bf16[512,512]{1,0:T(8,128)(2,1)S(1)} %copy-done.1), channel_id=1, source_target_pairs={{4,8},{8,4},{12,16},{16,12},{20,24},{24,20},{28,32},{32,28},{36,40... | collective-permute-start | bytes 1572872 | tf_op jit(solution)/shard_map/ppermute | solution.py:429
  39.5 13.7 %collective-permute-start.4 = (bf16[512,512]{1,0:T(8,128)(2,1)}, bf16[512,512]{1,0:T(8,128)(2,1)S(1)}, u32[]{:S(2)}, u32[]{:S(2)}) collective-permute-start(bf16[512,512]{1,0:T(8,128)(2,1)} %bitcast.38), channel_id=1, source_target_pairs={{0,4},{4,0},{8,12},{12,8},{16,20},{20,16},{24,28},{28,24},{32,36},... | collective-permute-start | bytes 1572872 | tf_op jit(solution)/shard_map/ppermute | solution.py:429
  39.6 17.6 %collective-permute-start.5 = (bf16[512,512]{1,0:T(8,128)(2,1)}, bf16[512,512]{1,0:T(8,128)(2,1)S(1)}, u32[]{:S(2)}, u32[]{:S(2)}) collective-permute-start(bf16[512,512]{1,0:T(8,128)(2,1)} %bitcast.37), channel_id=1, source_target_pairs={{4,8},{8,4},{12,16},{16,12},{20,24},{24,20},{28,32},{32,28},{36,40... | collective-permute-start | bytes 1572872 | tf_op jit(solution)/shard_map/ppermute | solution.py:429
  46.7 16.5 %collective-permute-start.12 = (bf16[512,1024]{1,0:T(8,128)(2,1)}, bf16[512,1024]{1,0:T(8,128)(2,1)S(1)}, u32[]{:S(2)}, u32[]{:S(2)}) collective-permute-start(bf16[512,1024]{1,0:T(8,128)(2,1)} %get-tuple-element.19), channel_id=1, source_target_pairs={{0,1},{1,0},{2,3},{3,2},{4,5},{5,4},{6,7},{7,6},{8,9},{9,8},{10,11... | collective-permute-start | bytes 3145736 | tf_op jit(solution)/shard_map/ppermute | solution.py:433
  48.9 45.6 %collective-permute-start.10 = (bf16[512,1024]{1,0:T(8,128)(2,1)}, bf16[512,1024]{1,0:T(8,128)(2,1)}, u32[]{:S(2)}, u32[]{:S(2)}) collective-permute-start(bf16[512,1024]{1,0:T(8,128)(2,1)} %get-tuple-element.18), channel_id=1, source_target_pairs={{0,35},{1,34},{2,33},{3,32},{4,39},{5,38},{6,37},{7,36},{8,43},{9,... | collective-permute-start | bytes 3145736 | tf_op jit(solution)/shard_map/ppermute | solution.py:442
  49.8 44.7 %collective-permute-start.8 = (bf16[384,1024]{1,0:T(8,128)(2,1)}, bf16[384,1024]{1,0:T(8,128)(2,1)S(1)}, u32[]{:S(2)}, u32[]{:S(2)}) collective-permute-start(bf16[384,1024]{1,0:T(8,128)(2,1)} %get-tuple-element.16), channel_id=1, source_target_pairs={{0,2},{1,3},{2,0},{3,1},{4,6},{5,7},{6,4},{7,5},{8,10},{9,11},{10,... | collective-permute-start | bytes 2359304 | tf_op jit(solution)/shard_map/ppermute | solution.py:433
  58.4 31.9 %collective-permute-start.11 = (bf16[512,512]{1,0:T(8,128)(2,1)S(1)}, bf16[512,512]{1,0:T(8,128)(2,1)S(1)}, u32[]{:S(2)}, u32[]{:S(2)}) collective-permute-start(bf16[512,512]{1,0:T(8,128)(2,1)S(1)} %fusion.c0), channel_id=1, source_target_pairs={{0,1},{1,0},{2,3},{3,2},{4,5},{5,4},{6,7},{7,6},{8,9},{9,8},{10,11... | collective-permute-start | bytes 1572872 | tf_op jit(solution)/shard_map/ppermute | solution.py:433
  61.2 23.1 %collective-permute-start.13 = (bf16[256,512]{1,0:T(8,128)(2,1)S(1)}, bf16[256,512]{1,0:T(8,128)(2,1)S(1)}, u32[]{:S(2)}, u32[]{:S(2)}) collective-permute-start(bf16[256,512]{1,0:T(8,128)(2,1)S(1)} %get-tuple-element.20), channel_id=1, source_target_pairs={{0,2},{1,3},{2,0},{3,1},{4,6},{5,7},{6,4},{7,5},{8,10},{9,11},{10,... | collective-permute-start | bytes 786440 | tf_op jit(solution)/shard_map/ppermute | solution.py:433
  63.2 21.0 %copy-start = (bf16[512,1024]{1,0:T(8,128)(2,1)}, bf16[512,1024]{1,0:T(8,128)(2,1)S(1)}, u32[]{:S(2)}) copy-start(bf16[512,1024]{1,0:T(8,128)(2,1)S(1)} %collective-permute-done.12.refs_1_) | copy-start | bytes 3145732
  63.2 26.6 %collective-permute-start.6 = (bf16[256,512]{1,0:T(8,128)(2,1)S(1)}, bf16[256,512]{1,0:T(8,128)(2,1)S(1)}, u32[]{:S(2)}, u32[]{:S(2)}) collective-permute-start(bf16[256,512]{1,0:T(8,128)(2,1)S(1)} %get-tuple-element.21), channel_id=1, source_target_pairs={{0,2},{1,3},{2,0},{3,1},{4,6},{5,7},{6,4},{7,5},{8,10},{9,11},{10,... | collective-permute-start | bytes 786440 | tf_op jit(solution)/shard_map/ppermute | solution.py:433
  84.2 10.3 %collective-permute-start.9 = (bf16[128,1024]{1,0:T(8,128)(2,1)}, bf16[128,1024]{1,0:T(8,128)(2,1)S(1)}, u32[]{:S(2)}, u32[]{:S(2)}) collective-permute-start(bf16[128,1024]{1,0:T(8,128)(2,1)} %get-tuple-element.17), channel_id=1, source_target_pairs={{0,34},{1,35},{2,32},{3,33},{4,38},{5,39},{6,36},{7,37},{8,42},{9,... | collective-permute-start | bytes 786440 | tf_op jit(solution)/shard_map/ppermute | solution.py:442
  89.8 4.7 %collective-permute-start.14 = (bf16[256,512]{1,0:T(8,128)(2,1)S(1)}, bf16[256,512]{1,0:T(8,128)(2,1)S(1)}, u32[]{:S(2)}, u32[]{:S(2)}) collective-permute-start(bf16[256,512]{1,0:T(8,128)(2,1)S(1)} %collective-permute-done.13.c0), channel_id=1, source_target_pairs={{0,1},{1,0},{2,3},{3,2},{4,5},{5,4},{6,7},{7,6},{8,9},{9,8},{10,11... | collective-permute-start | bytes 786440 | tf_op jit(solution)/shard_map/ppermute | solution.py:433
  90.3 7.3 %collective-permute-start.7 = (bf16[256,512]{1,0:T(8,128)(2,1)S(1)}, bf16[256,512]{1,0:T(8,128)(2,1)S(1)}, u32[]{:S(2)}, u32[]{:S(2)}) collective-permute-start(bf16[256,512]{1,0:T(8,128)(2,1)S(1)} %collective-permute-done.6.c0), channel_id=1, source_target_pairs={{0,1},{1,0},{2,3},{3,2},{4,5},{5,4},{6,7},{7,6},{8,9},{9,8},{10,11... | collective-permute-start | bytes 786440 | tf_op jit(solution)/shard_map/ppermute | solution.py:433

commit v9 on v8

--- a/solution.py
+++ b/solution.py
@@ -176,9 +176,46 @@
 
 
 def edge_kernel(
-    pos, counts, lists, q, k, v, beside, beyond, _, e, kb, vb, qb, eb, far_sem, in_sem, e_sem
+    per,
+    awaited,
+    pos,
+    counts,
+    lists,
+    owners,
+    slots,
+    q,
+    k,
+    v,
+    beside,
+    beyond,
+    _,
+    e,
+    kb,
+    vb,
+    qb,
+    eb,
+    far_sem,
+    in_sem,
+    e_sem,
 ):
     blocks = k.shape[0]
+    total = owners.shape[0] // per
+    named = jnp.int32(0)
+    for shift in (-1, 1):
+        source = pos[0] + shift
+        for t in range(per):
+            d = jnp.clip(source, 0, total - 1) * per + t
+            live = (source >= 0) & (source < total) & (owners[d] == pos[0])
+            bits = jnp.left_shift(jnp.int32(1), slots[0, d])
+            bits = bits | jnp.left_shift(jnp.int32(1), slots[1, d])
+            named = named | jnp.where(live, bits, 0)
+
+    def block_of(t):
+        return jnp.where(t < REACH, t, blocks - 2 * REACH + t)
+
+    def due(t):
+        return (jnp.right_shift(named, block_of(t)) & 1) == awaited
+
     near = 2 * REACH
     even = pos[0] % 2 == 0
     base = pos[0] * blocks - REACH
@@ -218,14 +255,21 @@
     for copy in local + edges(beyond, beside):
         copy.wait()
 
+    def result(t):
+        return pltpu.make_async_copy(eb.at[t], e.at[block_of(t)], e_sem)
+
     @pl.loop(0, near)
     def _(t):
-        b = jnp.where(t < REACH, t, blocks - near + t)
-        encode_block(b, base, counts, lists, qb.at[t], kb, vb, eb.at[t])
-        pltpu.make_async_copy(eb.at[t], e.at[b], e_sem).start()
-
-    for t in range(near):
-        pltpu.make_async_copy(eb.at[t], e.at[t], e_sem).wait()
+        @pl.when(due(t))
+        def _():
+            encode_block(block_of(t), base, counts, lists, qb.at[t], kb, vb, eb.at[t])
+            result(t).start()
+
+    @pl.loop(0, near)
+    def _(t):
+        @pl.when(due(t))
+        def _():
+            result(t).wait()
 
 
 def encoder_call(position, counts, lists, q, k3, v3, weight=None, edges=None):
@@ -255,16 +299,16 @@
             + [dma, dma((4,)), dma((4,))],
             name="encoder_inner",
         )(*args[:3], part, *args[3:], w)
-    beside, beyond, partial = edges
+    per, awaited, owners, slots, beside, beyond, partial = edges
     return pl.pallas_call(
-        edge_kernel,
-        in_specs=[smem] * 3 + [hbm] * 3 + [pl.BlockSpec(memory_space=pltpu.VMEM)] * 2 + [hbm],
+        functools.partial(edge_kernel, per, awaited),
+        in_specs=[smem] * 5 + [hbm] * 3 + [pl.BlockSpec(memory_space=pltpu.VMEM)] * 2 + [hbm],
         out_specs=hbm,
         out_shape=shape,
         scratch_shapes=[room(blocks + 2 * REACH)] * 2 + [room(2 * REACH)] * 2 + [dma] * 3,
-        input_output_aliases={8: 0},
+        input_output_aliases={10: 0},
         name="encoder_edge",
-    )(*args, in_vmem(cut(beside)), in_vmem(cut(beyond)), partial)
+    )(*args[:3], owners, slots, *args[3:], in_vmem(cut(beside)), in_vmem(cut(beyond)), partial)
 
 
 def serve_kernel(pos, owners, slots, k, e, *refs):
@@ -476,12 +520,16 @@
     w2_rest = other_side(around2, 2)
     w3 = other_side(across3, 3)
     w1 = swapped(across1, 1)
-    e3 = encoder_call(*encoder_args, edges=(beside, beyond, partial))
-    tables = (position, span_owner, slots, k3, e3)
-    answers = serve_call(*tables, [q_beside, q_beyond])
+    edges = (span_owner, slots, beside, beyond)
+    per = decoder_queries.shape[0] // BLK
+    e3 = encoder_call(*encoder_args, edges=(per, 1, *edges, partial))
+    tables = (position, span_owner, slots, k3)
+    answers = serve_call(*tables, e3, [q_beside, q_beyond])
+    e3, *answers = lax.optimization_barrier((e3, *answers))
     from_beside = exchanged(answers[0], 0)
     from_beyond = exchanged(answers[1], 1)
-    (own,) = serve_call(*tables, [decoder_queries])
+    e3 = encoder_call(*encoder_args, edges=(per, 0, *edges, e3))
+    (own,) = serve_call(*tables, e3, [decoder_queries])
     tokens = decoder_input.shape[0]
     share = tokens // PARTS
     context = own + from_beside + from_beyond

time: 101 us -> 101 us (level)
  Pallas kernels: 34.3 us -> 37.6 us
  waiting for transfers between devices: 35.3 us -> 33.5 us
  starting transfers between devices: 29.1 us -> 27.5 us
    pallas_call x1 -> x2, Pallas kernels: 5.98 us -> 9.24 us  [encoder_call(): pl.pallas_call(functools.partial(edge_kernel, per, awaited), in_specs=[sm...]
    ppermute x6, waiting for transfers between devices: 8.75 us -> 6.79 us  [exchanged(): return lax.ppermute(block, 'seq', route)]
  transfers between devices with their start and end apart: 15 -> 15, of which waited for: 4 -> 4; matrix products, arithmetic and copies ran while one was open for 1% -> 1% of each run, Pallas kernels for 23% -> 27%
where the time goes in v9:
time: 101 us
  Pallas kernels  37.6 us (37%)
  waiting for transfers between devices  33.5 us (33%)
  starting transfers between devices  27.5 us (27%)
  other arithmetic  1.16 us (1%)
    ppermute x7, waiting for transfers between devices, swapped(): return lax.ppermute(block, HEAD, [(i, i ^ flip) for i in range(4)])  26.7 us
    ppermute x6, starting transfers between devices, exchanged(): return lax.ppermute(block, 'seq', route)  17.9 us
    pallas_call x3, Pallas kernels, project_call(): pl.pallas_call(functools.partial(project_kernel, tuple((len(ws) for ws in...  10.2 us
    pallas_call x2, Pallas kernels, encoder_call(): pl.pallas_call(functools.partial(edge_kernel, per, awaited), in_specs=[sm...  9.24 us
    pallas_call x1, Pallas kernels, encoder_call(): pl.pallas_call(inner_kernel, in_specs=[smem] * 4 + [hbm] * 4, out_specs=[...  8.77 us
    ppermute x7, starting transfers between devices, swapped(): return lax.ppermute(block, HEAD, [(i, i ^ flip) for i in range(4)])  8.7 us
    pallas_call x2, Pallas kernels, serve_call(): pl.pallas_call(serve_kernel, in_specs=[smem] * 3 + [hbm] * 2 + [vmem if s...  7.1 us
    ppermute x6, waiting for transfers between devices, exchanged(): return lax.ppermute(block, 'seq', route)  6.79 us
  transfers between devices with their start and end apart: 15, of which 4 were waited for; matrix products, arithmetic and copies ran while one was open for 1% of the time, Pallas kernels for 27%

profile of v9, /device:TPU:21, one launch (start us, length us, event | category | flops | bytes accessed | tf_op | source)
XLA Modules:
  0.0 100.6 jit_solution(11329656687446986723)
XLA Ops:
  0.6 2.2 %pack_edges.1 = (bf16[512,512]{1,0:T(8,128)(2,1)}, bf16[512,512]{1,0:T(8,128)(2,1)}) custom-call(s32[1]{0:T(128)} %bitcast.pos, bf16[1536,512]{1,0:T(8,128)(2,1)} %k.1, bf16[1536,512]{1,0:T(8,128)(2,1)} %v.1), custom_call_target="tpu_custom_call" | custom-call | tf_op jit(solution)/shard_map/pack_edges/pallas_call | solution.py:90
  2.9 1.8 %collective-permute-start = (bf16[512,512]{1,0:T(8,128)(2,1)}, bf16[512,512]{1,0:T(8,128)(2,1)S(1)}, u32[]{:S(2)}, u32[]{:S(2)}) collective-permute-start(bf16[512,512]{1,0:T(8,128)(2,1)} %get-tuple-element.14), channel_id=1, source_target_pairs={{0,4},{4,0},{8,12},{12,8},{16,20},{20,16},{24,28},{28,24},{32,36},... | collective-permute-start | bytes 1572872 | tf_op jit(solution)/shard_map/ppermute | solution.py:473
  4.7 6.5 %collective-permute-start.1 = (bf16[512,512]{1,0:T(8,128)(2,1)}, bf16[512,512]{1,0:T(8,128)(2,1)S(1)}, u32[]{:S(2)}, u32[]{:S(2)}) collective-permute-start(bf16[512,512]{1,0:T(8,128)(2,1)} %get-tuple-element.15), channel_id=1, source_target_pairs={{4,8},{8,4},{12,16},{16,12},{20,24},{24,20},{28,32},{32,28},{36,40... | collective-permute-start | bytes 1572872 | tf_op jit(solution)/shard_map/ppermute | solution.py:473
  11.1 2.4 %collective-permute-start.3 = (bf16[512,512]{1,0:T(8,128)(2,1)S(1)}, bf16[512,512]{1,0:T(8,128)(2,1)S(1)}, u32[]{:S(2)}, u32[]{:S(2)}) collective-permute-start(bf16[512,512]{1,0:T(8,128)(2,1)S(1)} %copy-done), channel_id=1, source_target_pairs={{4,8},{8,4},{12,16},{16,12},{20,24},{24,20},{28,32},{32,28},{36,40... | collective-permute-start | bytes 1572872 | tf_op jit(solution)/shard_map/ppermute | solution.py:473
  13.7 8.8 %encoder_inner.1 = (bf16[12,128,512]{2,1,0:T(8,128)(2,1)}, bf16[384,1024]{1,0:T(8,128)(2,1)}, bf16[128,1024]{1,0:T(8,128)(2,1)}, bf16[512,1024]{1,0:T(8,128)(2,1)}, bf16[512,1024]{1,0:T(8,128)(2,1)}) custom-call(s32[1]{0:T(128)} %bitcast.pos, s32[12]{0:T(128)} %counts.5, s32[4,12]{1,0:T(4,128)} %bitcast.42, s32[1]{0:T(128)} %bitcast.8.part, ...), custom_call_target="tpu_custom_call" | custom-call | tf_op jit(solution)/shard_map/encoder_inner/pallas_call | solution.py:291
  22.5 0.4 collective-permute-done.1
  22.9 4.9 %encoder_edge.2.e._ = bf16[12,128,512]{2,1,0:T(8,128)(2,1)} custom-call(s32[1]{0:T(128)} %bitcast.pos, s32[12]{0:T(128)} %counts.5, s32[4,12]{1,0:T(4,128)} %bitcast.43, s32[256]{0:T(256)} %owners.7, s32[2,256]{1,0:T(2,128)} %bitcast.38, bf16[12,128,512]{2,1,0:T(8,128)(2,1)} %bitcast.35, ...), custom_call_target="tpu_custom_call", output_to_operand_aliasing={{}: (10, {})} | custom-call | tf_op jit(solution)/shard_map/encoder_edge/pallas_call | solution.py:303
  27.8 6.4 %collective-permute-done.3 = bf16[512,512]{1,0:T(8,128)(2,1)S(1)} collective-permute-done((bf16[512,512]{1,0:T(8,128)(2,1)S(1)}, bf16[512,512]{1,0:T(8,128)(2,1)S(1)}, u32[]{:S(2)}, u32[]{:S(2)}) %collective-permute-start.3) | collective-permute-done | bytes 524320 | tf_op jit(solution)/shard_map/ppermute | solution.py:473
  34.1 5.4 %shard_map.113 = (bf16[4,128,512]{2,1,0:T(8,128)(2,1)}, bf16[4,128,512]{2,1,0:T(8,128)(2,1)}) custom-call(s32[1]{0:T(128)} %bitcast.pos, s32[256]{0:T(256)} %owners.7, s32[2,256]{1,0:T(2,128)} %bitcast.39, bf16[12,128,512]{2,1,0:T(8,128)(2,1)} %bitcast.27, bf16[12,128,512]{2,1,0:T(8,128)(2,1)} %encoder_edge.2.e._, bf16[4,128,512]{2,1,0:T(8,128)(2,1)S(1)} %bitcast.24, ...), custom_call_target="tpu_custom_call" | custom-call | tf_op jit(solution)/shard_map/pallas_call | solution.py:401
  39.6 7.1 %collective-permute-start.5 = (bf16[512,512]{1,0:T(8,128)(2,1)}, bf16[512,512]{1,0:T(8,128)(2,1)S(1)}, u32[]{:S(2)}, u32[]{:S(2)}) collective-permute-start(bf16[512,512]{1,0:T(8,128)(2,1)} %bitcast.45), channel_id=1, source_target_pairs={{4,8},{8,4},{12,16},{16,12},{20,24},{24,20},{28,32},{32,28},{36,40... | collective-permute-start | bytes 1572872 | tf_op jit(solution)/shard_map/ppermute | solution.py:473
  46.7 2.2 %collective-permute-start.12 = (bf16[512,1024]{1,0:T(8,128)(2,1)}, bf16[512,1024]{1,0:T(8,128)(2,1)}, u32[]{:S(2)}, u32[]{:S(2)}) collective-permute-start(bf16[512,1024]{1,0:T(8,128)(2,1)} %get-tuple-element.25), channel_id=1, source_target_pairs={{0,1},{1,0},{2,3},{3,2},{4,5},{5,4},{6,7},{7,6},{8,9},{9,8},{10,11... | collective-permute-start | bytes 3145736 | tf_op jit(solution)/shard_map/ppermute | solution.py:477
  48.9 0.9 collective-permute-start.10
  49.8 1.8 %collective-permute-start.8 = (bf16[384,1024]{1,0:T(8,128)(2,1)}, bf16[384,1024]{1,0:T(8,128)(2,1)S(1)}, u32[]{:S(2)}, u32[]{:S(2)}) collective-permute-start(bf16[384,1024]{1,0:T(8,128)(2,1)} %get-tuple-element.22), channel_id=1, source_target_pairs={{0,2},{1,3},{2,0},{3,1},{4,6},{5,7},{6,4},{7,5},{8,10},{9,11},{10,... | collective-permute-start | bytes 2359304 | tf_op jit(solution)/shard_map/ppermute | solution.py:477
  51.6 4.4 %encoder_edge.3.e = bf16[12,128,512]{2,1,0:T(8,128)(2,1)} custom-call(s32[1]{0:T(128)} %bitcast.pos, s32[12]{0:T(128)} %counts.5, s32[4,12]{1,0:T(4,128)} %bitcast.44, s32[256]{0:T(256)} %owners.7, s32[2,256]{1,0:T(2,128)} %bitcast.40, bf16[12,128,512]{2,1,0:T(8,128)(2,1)} %bitcast.36, ...), custom_call_target="tpu_custom_call", output_to_operand_aliasing={{}: (10, {})} | custom-call | tf_op jit(solution)/shard_map/encoder_edge/pallas_call | solution.py:303
  56.0 1.7 %shard_map.114 = bf16[4,128,512]{2,1,0:T(8,128)(2,1)} custom-call(s32[1]{0:T(128)} %bitcast.pos, s32[256]{0:T(256)} %owners.7, s32[2,256]{1,0:T(2,128)} %bitcast.41, bf16[12,128,512]{2,1,0:T(8,128)(2,1)} %bitcast.29, bf16[12,128,512]{2,1,0:T(8,128)(2,1)} %encoder_edge.3.e, bf16[4,128,512]{2,1,0:T(8,128)(2,1)} %bitcast.37), custom_call_target="tpu_custom_call" | custom-call | tf_op jit(solution)/shard_map/pallas_call | solution.py:401
  57.7 1.2 %fusion.c0 = bf16[512,512]{1,0:T(8,128)(2,1)S(1)} fusion(bf16[512,512]{1,0:T(8,128)(2,1)S(1)} %collective-permute-done.5, bf16[512,512]{1,0:T(8,128)(2,1)S(1)} %collective-permute-done.4, bf16[4,128,512]{2,1,0:T(8,128)(2,1)} %shard_map.114), kind=kLoop, calls=%fused_computation.1 | loop fusion | flops 524288 | bytes 2097152 | tf_op jit(solution)/shard_map/add | solution.py:535
  58.9 2.3 %collective-permute-start.11 = (bf16[512,512]{1,0:T(8,128)(2,1)S(1)}, bf16[512,512]{1,0:T(8,128)(2,1)S(1)}, u32[]{:S(2)}, u32[]{:S(2)}) collective-permute-start(bf16[512,512]{1,0:T(8,128)(2,1)S(1)} %fusion.c0), channel_id=1, source_target_pairs={{0,1},{1,0},{2,3},{3,2},{4,5},{5,4},{6,7},{7,6},{8,9},{9,8},{10,11... | collective-permute-start | bytes 1572872 | tf_op jit(solution)/shard_map/ppermute | solution.py:477
  61.2 1.9 %collective-permute-start.13 = (bf16[256,512]{1,0:T(8,128)(2,1)S(1)}, bf16[256,512]{1,0:T(8,128)(2,1)S(1)}, u32[]{:S(2)}, u32[]{:S(2)}) collective-permute-start(bf16[256,512]{1,0:T(8,128)(2,1)S(1)} %get-tuple-element.26), channel_id=1, source_target_pairs={{0,2},{1,3},{2,0},{3,1},{4,6},{5,7},{6,4},{7,5},{8,10},{9,11},{10,... | collective-permute-start | bytes 786440 | tf_op jit(solution)/shard_map/ppermute | solution.py:477
  63.2 21.1 %collective-permute-done.13.c0 = bf16[256,512]{1,0:T(8,128)(2,1)S(1)} collective-permute-done((bf16[256,512]{1,0:T(8,128)(2,1)S(1)}, bf16[256,512]{1,0:T(8,128)(2,1)S(1)}, u32[]{:S(2)}, u32[]{:S(2)}) %collective-permute-start.13) | collective-permute-done | bytes 262176 | tf_op jit(solution)/shard_map/ppermute | solution.py:477
  84.2 5.6 %collective-permute-done.6.c0 = bf16[256,512]{1,0:T(8,128)(2,1)S(1)} collective-permute-done((bf16[256,512]{1,0:T(8,128)(2,1)S(1)}, bf16[256,512]{1,0:T(8,128)(2,1)S(1)}, u32[]{:S(2)}, u32[]{:S(2)}) %collective-permute-start.6) | collective-permute-done | bytes 262176 | tf_op jit(solution)/shard_map/ppermute | solution.py:477
  89.8 0.5 collective-permute-start.14
  90.4 4.1 %shard_map.115.refs_3_ = f32[512,1024]{1,0:T(8,128)} custom-call(s32[1]{0:T(128)} %bitcast.8.part, bf16[512,512]{1,0:T(8,128)(2,1)S(1)} %fusion.c0, bf16[512,512]{1,0:T(8,128)(2,1)S(1)} %collective-permute-done.11.c1, bf16[512,4096]{1,0:T(8,128)(2,1)} %refs_0_.1, bf16[512,1024]{1,0:T(8,128)(2,1)} %collective-permute-done.12.refs_1_, bf16[512,1024]{1,0:T(8,128)(2,1)} %refs_2_.1), custom_call_target="tpu_custom_call" | custom-call | tf_op jit(solution)/shard_map/pallas_call | solution.py:453
  94.5 3.0 %shard_map.116.refs_4_ = bf16[512,1024]{1,0:T(8,128)(2,1)} custom-call(s32[1]{0:T(128)} %bitcast.8.part, bf16[256,512]{1,0:T(8,128)(2,1)S(1)} %collective-permute-done.13.c0, bf16[256,512]{1,0:T(8,128)(2,1)S(1)} %collective-permute-done.14.c1, bf16[384,1024]{1,0:T(8,128)(2,1)S(1)} %collective-permute-done.8.refs_0_, ...), custom_call_target="tpu_custom_call" | custom-call | tf_op jit(solution)/shard_map/pallas_call | solution.py:453
  97.6 3.0 %shard_map.117 = bf16[512,1024]{1,0:T(8,128)(2,1)} custom-call(s32[1]{0:T(128)} %bitcast.8.part, bf16[256,512]{1,0:T(8,128)(2,1)S(1)} %collective-permute-done.6.c0, bf16[256,512]{1,0:T(8,128)(2,1)S(1)} %collective-permute-done.7.c1, bf16[384,1024]{1,0:T(8,128)(2,1)S(1)} %collective-permute-done.8.refs_0_, ...), custom_call_target="tpu_custom_call", output_to_operand_aliasing={{}: (7, {})} | custom-call | tf_op jit(solution)/shard_map/pallas_call | solution.py:453
  (21 shorter events, 0.4 us)
Async XLA Ops:
  0.6 10.5 %copy-start = (bf16[512,512]{1,0:T(8,128)(2,1)S(1)}, bf16[512,512]{1,0:T(8,128)(2,1)}, u32[]{:S(2)}) copy-start(bf16[512,512]{1,0:T(8,128)(2,1)} %param.15) | copy-start | bytes 1572868
  2.9 19.6 %collective-permute-start = (bf16[512,512]{1,0:T(8,128)(2,1)}, bf16[512,512]{1,0:T(8,128)(2,1)S(1)}, u32[]{:S(2)}, u32[]{:S(2)}) collective-permute-start(bf16[512,512]{1,0:T(8,128)(2,1)} %get-tuple-element.14), channel_id=1, source_target_pairs={{0,4},{4,0},{8,12},{12,8},{16,20},{20,16},{24,28},{28,24},{32,36},... | collective-permute-start | bytes 1572872 | tf_op jit(solution)/shard_map/ppermute | solution.py:473
  4.7 18.2 %collective-permute-start.1 = (bf16[512,512]{1,0:T(8,128)(2,1)}, bf16[512,512]{1,0:T(8,128)(2,1)S(1)}, u32[]{:S(2)}, u32[]{:S(2)}) collective-permute-start(bf16[512,512]{1,0:T(8,128)(2,1)} %get-tuple-element.15), channel_id=1, source_target_pairs={{4,8},{8,4},{12,16},{16,12},{20,24},{24,20},{28,32},{32,28},{36,40... | collective-permute-start | bytes 1572872 | tf_op jit(solution)/shard_map/ppermute | solution.py:473
  11.1 23.0 %collective-permute-start.3 = (bf16[512,512]{1,0:T(8,128)(2,1)S(1)}, bf16[512,512]{1,0:T(8,128)(2,1)S(1)}, u32[]{:S(2)}, u32[]{:S(2)}) collective-permute-start(bf16[512,512]{1,0:T(8,128)(2,1)S(1)} %copy-done), channel_id=1, source_target_pairs={{4,8},{8,4},{12,16},{16,12},{20,24},{24,20},{28,32},{32,28},{36,40... | collective-permute-start | bytes 1572872 | tf_op jit(solution)/shard_map/ppermute | solution.py:473
  13.6 20.6 %collective-permute-start.2 = (bf16[512,512]{1,0:T(8,128)(2,1)S(1)}, bf16[512,512]{1,0:T(8,128)(2,1)S(1)}, u32[]{:S(2)}, u32[]{:S(2)}) collective-permute-start(bf16[512,512]{1,0:T(8,128)(2,1)S(1)} %copy-done), channel_id=1, source_target_pairs={{0,4},{4,0},{8,12},{12,8},{16,20},{20,16},{24,28},{28,24},{32,36},... | collective-permute-start | bytes 1572872 | tf_op jit(solution)/shard_map/ppermute | solution.py:473
  39.5 18.1 %collective-permute-start.4 = (bf16[512,512]{1,0:T(8,128)(2,1)}, bf16[512,512]{1,0:T(8,128)(2,1)S(1)}, u32[]{:S(2)}, u32[]{:S(2)}) collective-permute-start(bf16[512,512]{1,0:T(8,128)(2,1)} %bitcast.46), channel_id=1, source_target_pairs={{0,4},{4,0},{8,12},{12,8},{16,20},{20,16},{24,28},{28,24},{32,36},... | collective-permute-start | bytes 1572872 | tf_op jit(solution)/shard_map/ppermute | solution.py:473
  39.6 18.1 %collective-permute-start.5 = (bf16[512,512]{1,0:T(8,128)(2,1)}, bf16[512,512]{1,0:T(8,128)(2,1)S(1)}, u32[]{:S(2)}, u32[]{:S(2)}) collective-permute-start(bf16[512,512]{1,0:T(8,128)(2,1)} %bitcast.45), channel_id=1, source_target_pairs={{4,8},{8,4},{12,16},{16,12},{20,24},{24,20},{28,32},{32,28},{36,40... | collective-permute-start | bytes 1572872 | tf_op jit(solution)/shard_map/ppermute | solution.py:473
  46.7 16.3 %collective-permute-start.12 = (bf16[512,1024]{1,0:T(8,128)(2,1)}, bf16[512,1024]{1,0:T(8,128)(2,1)}, u32[]{:S(2)}, u32[]{:S(2)}) collective-permute-start(bf16[512,1024]{1,0:T(8,128)(2,1)} %get-tuple-element.25), channel_id=1, source_target_pairs={{0,1},{1,0},{2,3},{3,2},{4,5},{5,4},{6,7},{7,6},{8,9},{9,8},{10,11... | collective-permute-start | bytes 3145736 | tf_op jit(solution)/shard_map/ppermute | solution.py:477
  48.9 45.6 %collective-permute-start.10 = (bf16[512,1024]{1,0:T(8,128)(2,1)}, bf16[512,1024]{1,0:T(8,128)(2,1)}, u32[]{:S(2)}, u32[]{:S(2)}) collective-permute-start(bf16[512,1024]{1,0:T(8,128)(2,1)} %get-tuple-element.24), channel_id=1, source_target_pairs={{0,35},{1,34},{2,33},{3,32},{4,39},{5,38},{6,37},{7,36},{8,43},{9,... | collective-permute-start | bytes 3145736 | tf_op jit(solution)/shard_map/ppermute | solution.py:486
  49.8 44.7 %collective-permute-start.8 = (bf16[384,1024]{1,0:T(8,128)(2,1)}, bf16[384,1024]{1,0:T(8,128)(2,1)S(1)}, u32[]{:S(2)}, u32[]{:S(2)}) collective-permute-start(bf16[384,1024]{1,0:T(8,128)(2,1)} %get-tuple-element.22), channel_id=1, source_target_pairs={{0,2},{1,3},{2,0},{3,1},{4,6},{5,7},{6,4},{7,5},{8,10},{9,11},{10,... | collective-permute-start | bytes 2359304 | tf_op jit(solution)/shard_map/ppermute | solution.py:477
  57.7 26.6 %copy-start.1 = (bf16[128,1024]{1,0:T(8,128)(2,1)S(1)}, bf16[128,1024]{1,0:T(8,128)(2,1)}, u32[]{:S(2)}) copy-start(bf16[128,1024]{1,0:T(8,128)(2,1)} %get-tuple-element.23) | copy-start | bytes 786436
  58.9 31.4 %collective-permute-start.11 = (bf16[512,512]{1,0:T(8,128)(2,1)S(1)}, bf16[512,512]{1,0:T(8,128)(2,1)S(1)}, u32[]{:S(2)}, u32[]{:S(2)}) collective-permute-start(bf16[512,512]{1,0:T(8,128)(2,1)S(1)} %fusion.c0), channel_id=1, source_target_pairs={{0,1},{1,0},{2,3},{3,2},{4,5},{5,4},{6,7},{7,6},{8,9},{9,8},{10,11... | collective-permute-start | bytes 1572872 | tf_op jit(solution)/shard_map/ppermute | solution.py:477
  61.2 23.0 %collective-permute-start.13 = (bf16[256,512]{1,0:T(8,128)(2,1)S(1)}, bf16[256,512]{1,0:T(8,128)(2,1)S(1)}, u32[]{:S(2)}, u32[]{:S(2)}) collective-permute-start(bf16[256,512]{1,0:T(8,128)(2,1)S(1)} %get-tuple-element.26), channel_id=1, source_target_pairs={{0,2},{1,3},{2,0},{3,1},{4,6},{5,7},{6,4},{7,5},{8,10},{9,11},{10,... | collective-permute-start | bytes 786440 | tf_op jit(solution)/shard_map/ppermute | solution.py:477
  63.0 26.8 %collective-permute-start.6 = (bf16[256,512]{1,0:T(8,128)(2,1)S(1)}, bf16[256,512]{1,0:T(8,128)(2,1)S(1)}, u32[]{:S(2)}, u32[]{:S(2)}) collective-permute-start(bf16[256,512]{1,0:T(8,128)(2,1)S(1)} %get-tuple-element.27), channel_id=1, source_target_pairs={{0,2},{1,3},{2,0},{3,1},{4,6},{5,7},{6,4},{7,5},{8,10},{9,11},{10,... | collective-permute-start | bytes 786440 | tf_op jit(solution)/shard_map/ppermute | solution.py:477
  84.2 10.3 %collective-permute-start.9 = (bf16[128,1024]{1,0:T(8,128)(2,1)S(1)}, bf16[128,1024]{1,0:T(8,128)(2,1)S(1)}, u32[]{:S(2)}, u32[]{:S(2)}) collective-permute-start(bf16[128,1024]{1,0:T(8,128)(2,1)S(1)} %copy-done.1), channel_id=1, source_target_pairs={{0,34},{1,35},{2,32},{3,33},{4,38},{5,39},{6,36},{7,37},{8,42},{9,... | collective-permute-start | bytes 786440 | tf_op jit(solution)/shard_map/ppermute | solution.py:486
  89.8 4.7 %collective-permute-start.14 = (bf16[256,512]{1,0:T(8,128)(2,1)S(1)}, bf16[256,512]{1,0:T(8,128)(2,1)S(1)}, u32[]{:S(2)}, u32[]{:S(2)}) collective-permute-start(bf16[256,512]{1,0:T(8,128)(2,1)S(1)} %collective-permute-done.13.c0), channel_id=1, source_target_pairs={{0,1},{1,0},{2,3},{3,2},{4,5},{5,4},{6,7},{7,6},{8,9},{9,8},{10,11... | collective-permute-start | bytes 786440 | tf_op jit(solution)/shard_map/ppermute | solution.py:477
  90.3 7.3 %collective-permute-start.7 = (bf16[256,512]{1,0:T(8,128)(2,1)S(1)}, bf16[256,512]{1,0:T(8,128)(2,1)S(1)}, u32[]{:S(2)}, u32[]{:S(2)}) collective-permute-start(bf16[256,512]{1,0:T(8,128)(2,1)S(1)} %collective-permute-done.6.c0), channel_id=1, source_target_pairs={{0,1},{1,0},{2,3},{3,2},{4,5},{5,4},{6,7},{7,6},{8,9},{9,8},{10,11... | collective-permute-start | bytes 786440 | tf_op jit(solution)/shard_map/ppermute | solution.py:477
